TPU v7x, 32 devices: a whole 2x2x4 slice. The times are simulated.
32 devices in a mesh: groups: 2 (over x), ctx: 16 (over z, y, core).
Axes of the slice: x: 2, y: 2, z: 4, core: 2. Of those that a mesh axis runs over, the one named last changes fastest.
Arguments:
- query_rows: bfloat16 [16384, 1024], P(('groups', 'ctx')), parts along dimension 0, may hold values from -6 to 6
- key_rows: bfloat16 [16384, 1024], P(('groups', 'ctx')), parts along dimension 0, may hold values from -0.375 to 0.375
- value_rows: bfloat16 [16384, 2048], P(('groups', 'ctx')), parts along dimension 0, may hold values from -6 to 6
- out_grad: bfloat16 [16384, 2048], P(('groups', 'ctx')), parts along dimension 0, may hold values from -0.25 to 0.25
- log_forget: float32 [16384, 4], P(('groups', 'ctx')), parts along dimension 0, may hold values from -0.75 to 0
- input_pre: float32 [16384, 4], P(('groups', 'ctx')), parts along dimension 0, may hold values from -3 to 0.5
- doc_starts: int32 [16384], P(('groups', 'ctx')), parts along dimension 0, may hold values from 0 to 1, as said below
Outputs:
- grad_queries: bfloat16 [16384, 1024], P(('groups', 'ctx')), parts along dimension 0
- grad_keys: bfloat16 [16384, 1024], P(('groups', 'ctx')), parts along dimension 0
- grad_values: bfloat16 [16384, 2048], P(('groups', 'ctx')), parts along dimension 0
There are 2 independent parts, one for each index of `groups`. A program takes and returns all parts, laid end to end along the dimension named above; each array names one. Nothing has to cross between parts.
Inputs may be any that keep to these rules, and one draw needn't show every extreme that they name: doc_starts is 1 at the sequence's first position; every document has at most 2048 positions, and some document has exactly that many.
All inputs are finite; a program needn't handle non-finite values.
Results may differ from a plain program's by a relative error of at most 0.0056.
Values may be sent and summed in bfloat16 or wider, within the bound.
No kernel may reach another device: no remote copies, remote signals or barrier semaphores. Data moves between devices by JAX's collectives and lax.ppermute only.
A program may use at most 192 MiB of HBM per device.

v0:
```python
import jax
import jax.numpy as jnp
from jax import lax
from jax.sharding import PartitionSpec as P

TEXT_SPAN_COUNT = 4


def passed_along(block, axis, distance):
    devices = range(lax.axis_size(axis))
    route = [(i - distance, i) for i in devices if i - distance in devices]
    return lax.ppermute(block, axis, route)


def gate_terms(log_gate, input_gate, start_flags):
    decay_sum = jnp.cumsum(log_gate, axis=0)
    segment = jnp.cumsum(start_flags, axis=0)
    final_seg = segment[-1]
    gate_logits = jnp.exp(input_gate)
    leading_weight = jnp.where((segment == 0)[:, None], jnp.exp(decay_sum), 0.0)
    trailing_weight = jnp.where(
        (segment == final_seg)[:, None], jnp.exp(decay_sum[-1][None, :] - decay_sum), 0.0
    )
    carry_gain = jnp.where(final_seg == 0, jnp.exp(decay_sum[-1]), 0.0)
    return (decay_sum, segment, gate_logits, leading_weight, trailing_weight, carry_gain)


def compose(earlier, later):
    return (earlier[0] * later[0], later[0][:, None, None] * earlier[1] + later[1])


def within_reach(carry_gain, state, direction):
    sections = min((TEXT_SPAN_COUNT - 1).bit_length(), (lax.axis_size("ctx") - 1).bit_length())
    running = (carry_gain, state)
    for stride_log in range(sections):
        shifted = passed_along((running[0], running[1]), "ctx", direction * (1 << stride_log))
        running = compose(shifted, running)
    return passed_along(running[1].astype(jnp.bfloat16), "ctx", direction)


def body(query_rows, key_rows, value_rows, out_grad, log_forget, input_pre, doc_starts):
    width, heads = log_forget.shape
    key_width = query_rows.shape[1] // heads
    value_width = value_rows.shape[1] // heads
    scale_factor = key_width ** (-0.5)
    query_block = query_rows.reshape(width, heads, key_width)
    key_block = key_rows.reshape(width, heads, key_width)
    value_block = value_rows.reshape(width, heads, value_width)
    gradient_block = out_grad.reshape(width, heads, value_width)
    decay_sum, segment, gate_logits, leading_weight, trailing_weight, carry_gain = gate_terms(
        log_forget, input_pre, doc_starts
    )
    scaled_value = ((trailing_weight * gate_logits)[:, :, None] * value_block).astype(jnp.bfloat16)
    ahead_carry_state = jnp.einsum(
        "pxj,pxe->xje", key_block, scaled_value, preferred_element_type=jnp.float32
    )
    scaled_query = ((scale_factor * leading_weight)[:, :, None] * query_block).astype(jnp.bfloat16)
    reverse_carry_state = jnp.einsum(
        "pxj,pxe->xje", scaled_query, gradient_block, preferred_element_type=jnp.float32
    )
    incoming_state_block = within_reach(carry_gain, ahead_carry_state, 1)
    arriving_state_block = within_reach(carry_gain, reverse_carry_state, -1)
    position = jnp.arange(width)
    allowed = (position[:, None] >= position[None, :]) & (segment[:, None] == segment[None, :])
    gaps = decay_sum.T[:, :, None] - decay_sum.T[:, None, :]
    decay = jnp.exp(jnp.where(allowed[None], gaps, -jnp.inf))
    product = decay * jnp.einsum(
        "thv,shv->hts", gradient_block, value_block, preferred_element_type=jnp.float32
    )
    first_factor = (scale_factor * product * gate_logits.T[:, None, :]).astype(jnp.bfloat16)
    second_factor = (scale_factor * jnp.swapaxes(product, 1, 2)).astype(jnp.bfloat16)
    intersection = jnp.einsum(
        "thk,uhk->htu", key_block, query_block, preferred_element_type=jnp.float32
    )
    third_factor = (scale_factor * jnp.swapaxes(decay, 1, 2) * intersection).astype(jnp.bfloat16)
    query_part = jnp.einsum(
        "row,wra->ora", first_factor, key_block, preferred_element_type=jnp.float32
    )
    key_part = jnp.einsum(
        "bmz,zbo->mbo", second_factor, query_block, preferred_element_type=jnp.float32
    )
    value_part = jnp.einsum(
        "nyb,bnq->ynq", third_factor, gradient_block, preferred_element_type=jnp.float32
    )
    query_gradient = query_part + scale_factor * leading_weight[:, :, None] * jnp.einsum(
        "xrl,rml->xrm", gradient_block, incoming_state_block, preferred_element_type=jnp.float32
    )
    key_gradient = gate_logits[:, :, None] * (
        key_part
        + trailing_weight[:, :, None]
        * jnp.einsum(
            "xrl,rml->xrm", value_block, arriving_state_block, preferred_element_type=jnp.float32
        )
    )
    value_gradient = gate_logits[:, :, None] * (
        value_part
        + trailing_weight[:, :, None]
        * jnp.einsum(
            "jam,ame->jae", key_block, arriving_state_block, preferred_element_type=jnp.float32
        )
    )
    return (
        query_gradient.astype(jnp.bfloat16).reshape(width, heads * key_width),
        key_gradient.astype(jnp.bfloat16).reshape(width, heads * key_width),
        value_gradient.astype(jnp.bfloat16).reshape(width, heads * value_width),
    )


def solution(mesh):
    in_specs = (
        P(("groups", "ctx"), None),
        P(("groups", "ctx"), None),
        P(("groups", "ctx"), None),
        P(("groups", "ctx"), None),
        P(("groups", "ctx"), None),
        P(("groups", "ctx"), None),
        P(("groups", "ctx")),
    )
    out_specs = (P(("groups", "ctx"), None), P(("groups", "ctx"), None), P(("groups", "ctx"), None))
    return jax.shard_map(body, mesh=mesh, in_specs=in_specs, out_specs=out_specs, check_vma=False)
```

profile of v0, /device:TPU:9, one launch (start us, length us, event | category | flops | bytes accessed | tf_op | source)
XLA Modules:
  0.0 209.3 jit_solution(18248221969516494230)
XLA Ops:
  0.6 1.0 reduce-window.15
  1.6 0.1 slice.20
  1.7 0.1 slice_reduce_fusion.2
  1.8 0.1 broadcast_compare_fusion.1
  1.9 0.6 slice.24
  2.5 0.6 broadcast_compare_fusion
  3.2 0.7 reshape.167
  3.9 1.2 reduce-window.19
  5.1 0.2 slice_reduce_fusion
  5.2 0.2 reduce-window.24
  5.4 0.1 add_bitcast_fusion
  5.5 0.2 slice_reduce_fusion.1
  5.7 1.5 copy.41
  7.2 0.0 copy-start.2
  7.2 2.9 %copy.60 = bf16[512,2048]{0,1:T(8,128)(2,1)S(1)} copy(bf16[512,2048]{1,0:T(8,128)(2,1)} %param.10) | data formatting | bytes 4194304 | tf_op jit(solution)/shard_map/reshape | solution.py:49
  10.1 0.1 fusion.47
  10.2 2.1 fusion.27
  12.3 2.6 %collective-permute-start.5 = (f32[4,256,512]{1,2,0:T(8,128)}, f32[4,256,512]{1,2,0:T(8,128)}, u32[]{:S(2)}, u32[]{:S(2)}) collective-permute-start(f32[4,256,512]{1,2,0:T(8,128)} %fusion.27), channel_id=1, source_target_pairs={{1,0},{2,1},{3,2},{4,3},{5,4},{6,5},{7,6},{8,7},{9,8},{10,9},{11,1... | collective-permute-start | bytes 6291464 | tf_op jit(solution)/shard_map/ppermute | solution.py:12
  14.8 3.9 %copy.61 = bf16[512,2048]{0,1:T(8,128)(2,1)} copy(bf16[512,2048]{1,0:T(8,128)(2,1)} %param.9) | data formatting | bytes 4194304 | tf_op jit(solution)/shard_map/reshape | solution.py:48
  18.8 3.9 %fusion.25 = f32[4,256,512]{1,2,0:T(8,128)} fusion(bf16[512,4,512]{0,2,1:T(8,128)(2,1)} %bitcast.96, f32[512,4]{0,1:T(4,128)S(1)} %get-tuple-element.15, bf16[64,4,8,256]{3,2,1,0:T(8,128)(2,1)} %bitcast.105), kind=kOutput, calls=%fused_computation.37 | convolution fusion | flops 540016640 | bytes 5251072 | tf_op jit(solution)/shard_map/pxj,pxe->xje/dot_general | solution.py:54
  22.7 3.0 %collective-permute-start.1 = (f32[4,256,512]{1,2,0:T(8,128)}, f32[4,256,512]{1,2,0:T(8,128)}, u32[]{:S(2)}, u32[]{:S(2)}) collective-permute-start(f32[4,256,512]{1,2,0:T(8,128)} %fusion.25), channel_id=1, source_target_pairs={{0,1},{1,2},{2,3},{3,4},{4,5},{5,6},{6,7},{7,8},{8,9},{9,10},{10,1... | collective-permute-start | bytes 6291464 | tf_op jit(solution)/shard_map/ppermute | solution.py:12
  26.4 0.0 copy-start
  26.4 36.0 %collective-permute-done.5 = f32[4,256,512]{1,2,0:T(8,128)} collective-permute-done((f32[4,256,512]{1,2,0:T(8,128)}, f32[4,256,512]{1,2,0:T(8,128)}, u32[]{:S(2)}, u32[]{:S(2)}) %collective-permute-start.5) | collective-permute-done | bytes 2097184 | tf_op jit(solution)/shard_map/ppermute | solution.py:12
  62.5 0.2 collective-permute-done.1
  62.6 6.0 %multiply_add_fusion = (f32[4,256,512]{1,2,0:T(8,128)}, f32[4,256,512]{1,2,0:T(8,128)}) fusion(f32[4,256,512]{1,2,0:T(8,128)} %fusion.27, f32[4,256,512]{1,2,0:T(8,128)} %collective-permute-done.5, f32[4]{0:T(128)S(1)} %broadcast_select_fusion, f32[4,256,512]{1,2,0:T(8,128)} %fusion.25, f32[4,256,512]{1,2,0:T(8,128)} %collective-permute-done.1), kind=kLoop, calls=%fused_computation.22 | loop fusion | flops 2097152 | bytes 12582928 | tf_op jit(solution)/shard_map/add | solution.py:29
  68.7 1.9 collective-permute-start.6
  70.6 3.4 %collective-permute-start.2 = (f32[4,256,512]{1,2,0:T(8,128)}, f32[4,256,512]{1,2,0:T(8,128)}, u32[]{:S(2)}, u32[]{:S(2)}) collective-permute-start(f32[4,256,512]{1,2,0:T(8,128)} %get-tuple-element.25), channel_id=1, source_target_pairs={{0,2},{1,3},{2,4},{3,5},{4,6},{5,7},{6,8},{7,9},{8,10},{9,11},{10,... | collective-permute-start | bytes 6291464 | tf_op jit(solution)/shard_map/ppermute | solution.py:12
  74.0 3.3 %collective-permute-start.4 = (f32[4]{0:T(128)S(1)}, f32[4]{0:T(128)S(1)}, u32[]{:S(2)}, u32[]{:S(2)}) collective-permute-start(f32[4]{0:T(128)S(1)} %broadcast_select_fusion), channel_id=1, source_target_pairs={{1,0},{2,1},{3,2},{4,3},{5,4},{6,5},{7,6},{8,7},{9,8},{10,9},{11,1... | collective-permute-start | bytes 56 | tf_op jit(solution)/shard_map/ppermute | solution.py:12
  77.3 4.4 %collective-permute-start = (f32[4]{0:T(128)S(1)}, f32[4]{0:T(128)S(1)}, u32[]{:S(2)}, u32[]{:S(2)}) collective-permute-start(f32[4]{0:T(128)S(1)} %broadcast_select_fusion), channel_id=1, source_target_pairs={{0,1},{1,2},{2,3},{3,4},{4,5},{5,6},{6,7},{7,8},{8,9},{9,10},{10,1... | collective-permute-start | bytes 56 | tf_op jit(solution)/shard_map/ppermute | solution.py:12
  81.8 3.2 %fusion.49 = f32[4,512,512]{2,1,0:T(8,128)} fusion(bf16[512,4,512]{0,2,1:T(8,128)(2,1)S(1)} %bitcast.93, bf16[512,4,512]{0,2,1:T(8,128)(2,1)S(1)} %bitcast.98), kind=kOutput, calls=%fused_computation.74 | convolution fusion | flops 1073741824 | bytes 8388608 | tf_op jit(solution)/shard_map/thv,shv->hts/dot_general | solution.py:67
  85.0 5.2 %copy.34 = f32[4,512,512]{1,2,0:T(8,128)} copy(f32[4,512,512]{2,1,0:T(8,128)} %fusion.49) | data formatting | bytes 8388608 | tf_op jit(solution)/shard_map/thv,shv->hts/dot_general | solution.py:67
  90.2 0.3 fusion.35
  90.6 5.6 %fusion.5 = f32[4,512,256]{1,2,0:T(8,128)} fusion(f32[4,512,512]{1,2,0:T(8,128)} %copy.34, f32[4,512]{1,0:T(4,128)S(1)} %get-tuple-element.14, f32[4,512]{1,0:T(4,128)S(1)} %bitcast.110, pred[512,512]{0,1:T(8,128)(4,1)S(1)} %get-tuple-element.21, bf16[64,4,8,256]{3,2,1,0:T(8,128)(2,1)} %bitcast.106), kind=kOutput, calls=%fused_computation.11 | convolution fusion | flops 542113792 | bytes 7618560 | tf_op jit(solution)/shard_map/row,wra->ora/dot_general | solution.py:76
  96.2 67.2 %collective-permute-done.4 = f32[4]{0:T(128)S(1)} collective-permute-done((f32[4]{0:T(128)S(1)}, f32[4]{0:T(128)S(1)}, u32[]{:S(2)}, u32[]{:S(2)}) %collective-permute-start.4) | collective-permute-done | bytes 48 | tf_op jit(solution)/shard_map/ppermute | solution.py:12
  163.4 0.0 collective-permute-done
  163.5 3.6 %add_convert_fusion = bf16[4,256,512]{1,2,0:T(8,128)(2,1)} fusion(f32[4,256,512]{1,2,0:T(8,128)} %get-tuple-element.24, f32[4,256,512]{1,2,0:T(8,128)} %collective-permute-done.6, f32[4]{0:T(128)S(1)} %get-tuple-element.22), kind=kLoop, calls=%fused_computation.21 | loop fusion | flops 1572864 | bytes 5242896 | tf_op jit(solution)/shard_map/convert_element_type | solution.py:38
  167.0 2.3 %collective-permute-start.7 = (bf16[4,256,512]{1,2,0:T(8,128)(2,1)}, bf16[4,256,512]{1,2,0:T(8,128)(2,1)}, u32[]{:S(2)}, u32[]{:S(2)}) collective-permute-start(bf16[4,256,512]{1,2,0:T(8,128)(2,1)} %add_convert_fusion), channel_id=1, source_target_pairs={{1,0},{2,1},{3,2},{4,3},{5,4},{6,5},{7,6},{8,7},{9,8},{10,9},{11,1... | collective-permute-start | bytes 3145736 | tf_op jit(solution)/shard_map/ppermute | solution.py:12
  169.3 3.7 %add_convert_fusion.1 = bf16[4,256,512]{1,2,0:T(8,128)(2,1)} fusion(f32[4,256,512]{1,2,0:T(8,128)} %get-tuple-element.25, f32[4,256,512]{1,2,0:T(8,128)} %collective-permute-done.2, f32[4]{0:T(128)S(1)} %get-tuple-element.23), kind=kLoop, calls=%fused_computation.25 | loop fusion | flops 1572864 | bytes 5242896 | tf_op jit(solution)/shard_map/convert_element_type | solution.py:38
  173.1 3.4 %collective-permute-start.3 = (bf16[4,256,512]{1,2,0:T(8,128)(2,1)}, bf16[4,256,512]{1,2,0:T(8,128)(2,1)}, u32[]{:S(2)}, u32[]{:S(2)}) collective-permute-start(bf16[4,256,512]{1,2,0:T(8,128)(2,1)} %add_convert_fusion.1), channel_id=1, source_target_pairs={{0,1},{1,2},{2,3},{3,4},{4,5},{5,6},{6,7},{7,8},{8,9},{9,10},{10,1... | collective-permute-start | bytes 3145736 | tf_op jit(solution)/shard_map/ppermute | solution.py:12
  176.5 2.9 %fusion.7 = f32[4,512,256]{1,2,0:T(8,128)} fusion(bf16[512,4,256]{0,2,1:T(8,128)(2,1)S(1)} %bitcast.101, f32[4,512,512]{2,1,0:T(8,128)S(1)} %copy-done.1, f32[4,512]{1,0:T(4,128)S(1)} %bitcast.111, pred[512,512]{0,1:T(8,128)(4,1)S(1)} %get-tuple-element.20), kind=kOutput, calls=%fused_computation.13 | convolution fusion | flops 542113792 | bytes 7610368 | tf_op jit(solution)/shard_map/bmz,zbo->mbo/dot_general | solution.py:79
  179.4 5.6 %fusion.26 = f32[4,512,512]{1,2,0:T(8,128)} fusion(bf16[512,4,512]{0,2,1:T(8,128)(2,1)S(1)} %bitcast.94, bf16[512,4,256]{0,2,1:T(8,128)(2,1)S(1)} %bitcast.102, f32[4,512]{1,0:T(4,128)S(1)} %bitcast.112, pred[512,512]{0,1:T(8,128)(4,1)S(1)} %get-tuple-element.20, bf16[64,4,8,256]{3,2,1,0:T(8,128)(2,1)} %bitcast.107), kind=kOutput, calls=%fused_computation.38 | convolution fusion | flops 1615855616 | bytes 8658944 | tf_op jit(solution)/shard_map/nyb,bnq->ynq/dot_general | solution.py:82
  185.0 9.6 %collective-permute-done.7 = bf16[4,256,512]{1,2,0:T(8,128)(2,1)} collective-permute-done((bf16[4,256,512]{1,2,0:T(8,128)(2,1)}, bf16[4,256,512]{1,2,0:T(8,128)(2,1)}, u32[]{:S(2)}, u32[]{:S(2)}) %collective-permute-start.7) | collective-permute-done | bytes 1048608 | tf_op jit(solution)/shard_map/ppermute | solution.py:12
  194.7 3.3 %fusion.11 = bf16[512,4,256]{0,2,1:T(8,128)(2,1)S(1)} fusion(f32[4,512,256]{1,2,0:T(8,128)} %fusion.7, bf16[4,256,512]{1,2,0:T(8,128)(2,1)} %collective-permute-done.7, bf16[512,4,512]{0,2,1:T(8,128)(2,1)} %bitcast.97, f32[512,4]{0,1:T(4,128)S(1)} %get-tuple-element.16, f32[512,4]{0,1:T(4,128)S(1)} %get-tuple-element.13), kind=kOutput, calls=%fused_computation.17 | convolution fusion | flops 538968064 | bytes 6307840 | tf_op jit(solution)/shard_map/xrl,rml->xrm/dot_general | solution.py:91
  198.0 1.3 copy.52
  199.3 2.7 %fusion.13 = bf16[512,4,256]{0,2,1:T(8,128)(2,1)S(1)} fusion(f32[4,512,256]{1,2,0:T(8,128)} %fusion.5, bf16[4,256,512]{1,2,0:T(8,128)(2,1)} %collective-permute-done.3, bf16[512,4,512]{0,2,1:T(8,128)(2,1)S(1)} %bitcast.95, f32[512,4]{0,1:T(4,128)S(1)} %get-tuple-element.17), kind=kOutput, calls=%fused_computation.20 | convolution fusion | flops 538443776 | bytes 6299648 | tf_op jit(solution)/shard_map/xrl,rml->xrm/dot_general | solution.py:85
  202.0 1.3 copy.51
  203.3 3.6 %fusion.2 = bf16[512,4,512]{0,2,1:T(8,128)(2,1)S(1)} fusion(f32[4,512,512]{1,2,0:T(8,128)} %fusion.26, bf16[4,256,512]{1,2,0:T(8,128)(2,1)} %collective-permute-done.7, f32[512,4]{0,1:T(4,128)S(1)} %get-tuple-element.16, f32[512,4]{0,1:T(4,128)S(1)} %get-tuple-element.13, bf16[64,4,8,256]{3,2,1,0:T(8,128)(2,1)} %bitcast.108), kind=kOutput, calls=%fused_computation.3 | convolution fusion | flops 541065216 | bytes 8404992 | tf_op jit(solution)/shard_map/jam,ame->jae/dot_general | solution.py:98
  206.9 2.4 %copy.53 = bf16[512,2048]{1,0:T(8,128)(2,1)} copy(bf16[512,2048]{0,1:T(8,128)(2,1)S(1)} %bitcast.99) | data formatting | bytes 4194304
  (11 shorter events, 0.1 us)
Async XLA Ops:
  7.2 2.9 %copy-start.2 = (f32[512,4]{0,1:T(4,128)S(1)}, f32[512,4]{0,1:T(4,128)}, u32[]{:S(2)}) copy-start(f32[512,4]{0,1:T(4,128)} %param.12) | copy-start | bytes 24580
  12.3 50.2 %collective-permute-start.5 = (f32[4,256,512]{1,2,0:T(8,128)}, f32[4,256,512]{1,2,0:T(8,128)}, u32[]{:S(2)}, u32[]{:S(2)}) collective-permute-start(f32[4,256,512]{1,2,0:T(8,128)} %fusion.27), channel_id=1, source_target_pairs={{1,0},{2,1},{3,2},{4,3},{5,4},{6,5},{7,6},{8,7},{9,8},{10,9},{11,1... | collective-permute-start | bytes 6291464 | tf_op jit(solution)/shard_map/ppermute | solution.py:12
  22.7 39.9 %collective-permute-start.1 = (f32[4,256,512]{1,2,0:T(8,128)}, f32[4,256,512]{1,2,0:T(8,128)}, u32[]{:S(2)}, u32[]{:S(2)}) collective-permute-start(f32[4,256,512]{1,2,0:T(8,128)} %fusion.25), channel_id=1, source_target_pairs={{0,1},{1,2},{2,3},{3,4},{4,5},{5,6},{6,7},{7,8},{8,9},{9,10},{10,1... | collective-permute-start | bytes 6291464 | tf_op jit(solution)/shard_map/ppermute | solution.py:12
  26.4 55.3 %copy-start = (bf16[512,2048]{0,1:T(8,128)(2,1)S(1)}, bf16[512,2048]{0,1:T(8,128)(2,1)}, u32[]{:S(2)}) copy-start(bf16[512,2048]{0,1:T(8,128)(2,1)} %copy.61) | copy-start | bytes 6291460
  68.7 94.8 %collective-permute-start.6 = (f32[4,256,512]{1,2,0:T(8,128)}, f32[4,256,512]{1,2,0:T(8,128)}, u32[]{:S(2)}, u32[]{:S(2)}) collective-permute-start(f32[4,256,512]{1,2,0:T(8,128)} %get-tuple-element.24), channel_id=1, source_target_pairs={{2,0},{3,1},{4,2},{5,3},{6,4},{7,5},{8,6},{9,7},{10,8},{11,9},{12,... | collective-permute-start | bytes 6291464 | tf_op jit(solution)/shard_map/ppermute | solution.py:12
  70.6 98.7 %collective-permute-start.2 = (f32[4,256,512]{1,2,0:T(8,128)}, f32[4,256,512]{1,2,0:T(8,128)}, u32[]{:S(2)}, u32[]{:S(2)}) collective-permute-start(f32[4,256,512]{1,2,0:T(8,128)} %get-tuple-element.25), channel_id=1, source_target_pairs={{0,2},{1,3},{2,4},{3,5},{4,6},{5,7},{6,8},{7,9},{8,10},{9,11},{10,... | collective-permute-start | bytes 6291464 | tf_op jit(solution)/shard_map/ppermute | solution.py:12
  74.0 89.5 %collective-permute-start.4 = (f32[4]{0:T(128)S(1)}, f32[4]{0:T(128)S(1)}, u32[]{:S(2)}, u32[]{:S(2)}) collective-permute-start(f32[4]{0:T(128)S(1)} %broadcast_select_fusion), channel_id=1, source_target_pairs={{1,0},{2,1},{3,2},{4,3},{5,4},{6,5},{7,6},{8,7},{9,8},{10,9},{11,1... | collective-permute-start | bytes 56 | tf_op jit(solution)/shard_map/ppermute | solution.py:12
  77.3 86.1 %collective-permute-start = (f32[4]{0:T(128)S(1)}, f32[4]{0:T(128)S(1)}, u32[]{:S(2)}, u32[]{:S(2)}) collective-permute-start(f32[4]{0:T(128)S(1)} %broadcast_select_fusion), channel_id=1, source_target_pairs={{0,1},{1,2},{2,3},{3,4},{4,5},{5,6},{6,7},{7,8},{8,9},{9,10},{10,1... | collective-permute-start | bytes 56 | tf_op jit(solution)/shard_map/ppermute | solution.py:12
  167.0 27.7 %collective-permute-start.7 = (bf16[4,256,512]{1,2,0:T(8,128)(2,1)}, bf16[4,256,512]{1,2,0:T(8,128)(2,1)}, u32[]{:S(2)}, u32[]{:S(2)}) collective-permute-start(bf16[4,256,512]{1,2,0:T(8,128)(2,1)} %add_convert_fusion), channel_id=1, source_target_pairs={{1,0},{2,1},{3,2},{4,3},{5,4},{6,5},{7,6},{8,7},{9,8},{10,9},{11,1... | collective-permute-start | bytes 3145736 | tf_op jit(solution)/shard_map/ppermute | solution.py:12
  169.3 7.2 %copy-start.1 = (f32[4,512,512]{2,1,0:T(8,128)S(1)}, f32[4,512,512]{2,1,0:T(8,128)}, u32[]{:S(2)}) copy-start(f32[4,512,512]{2,1,0:T(8,128)} %fusion.49) | copy-start | bytes 12582916
  173.1 26.3 %collective-permute-start.3 = (bf16[4,256,512]{1,2,0:T(8,128)(2,1)}, bf16[4,256,512]{1,2,0:T(8,128)(2,1)}, u32[]{:S(2)}, u32[]{:S(2)}) collective-permute-start(bf16[4,256,512]{1,2,0:T(8,128)(2,1)} %add_convert_fusion.1), channel_id=1, source_target_pairs={{0,1},{1,2},{2,3},{3,4},{4,5},{5,6},{6,7},{7,8},{8,9},{9,10},{10,1... | collective-permute-start | bytes 3145736 | tf_op jit(solution)/shard_map/ppermute | solution.py:12
where the time goes:
time: 210 us; the launch traced here: 209 us
  waiting for transfers between devices  113 us (54%)
  matrix products  33 us (16%)
  starting transfers between devices  24.4 us (12%)
  local copies, waits for them, and re-layouts  20.4 us (10%)
  other arithmetic  17 us (8%)
    ppermute x8, waiting for transfers between devices, passed_along(): return lax.ppermute(block, axis, route)  113 us
    ppermute x8, starting transfers between devices, passed_along(): return lax.ppermute(block, axis, route)  24.4 us
    convert_element_type x2, other arithmetic, within_reach(): return passed_along(running[1].astype(jnp.bfloat16), 'ctx', direction)  7.27 us
    unnamed x11, local copies, waits for them, and re-layouts  6.53 us
    add x1, other arithmetic, compose(): later[0][:, None, None] * earlier[1] + later[1]  6.05 us
    dot_general x1, matrix products, body(): jnp.einsum('row,wra->ora', first_factor, key_block, preferred_element_typ...  5.63 us
    dot_general x1, matrix products, body(): jnp.einsum('nyb,bnq->ynq', third_factor, gradient_block, preferred_elemen...  5.6 us
    dot_general x1, local copies, waits for them, and re-layouts, body(): jnp.einsum('thv,shv->hts', gradient_block, value_block, preferred_element...  5.23 us
  transfers between devices with their start and end apart: 8, of which 4 were waited for; matrix products, arithmetic and copies ran while one was open for 20% of the time, Pallas kernels for 0%

commit v1 on v0

v1 whole, which is shorter than its diff:
```python
import functools

import jax
import jax.numpy as jnp
from jax import lax
from jax.experimental import pallas as pl
from jax.experimental.pallas import tpu as pltpu
from jax.sharding import PartitionSpec as P

F32 = jnp.float32
BF16 = jnp.bfloat16
LANES = 128
EXTRA = 8
DECAY, GATE, TAIL, HEAD, SEG, TAIL_GATE, GAIN, ROWS = 0, 4, 8, 12, 16, 24, 28, 32
VM = pl.BlockSpec(memory_space=pltpu.VMEM)
HBM = pl.BlockSpec(memory_space=pltpu.HBM)


def nt(a, b):
    return lax.dot_general(a, b, (((1,), (1,)), ((), ())), preferred_element_type=F32)


def nn(a, b):
    return lax.dot_general(a, b, (((1,), (0,)), ((), ())), preferred_element_type=F32)


def tn(a, b):
    return lax.dot_general(a, b, (((0,), (0,)), ((), ())), preferred_element_type=F32)


def three_terms(x):
    hi = x.astype(BF16)
    rest = x - hi.astype(F32)
    mid = rest.astype(BF16)
    lo = (rest - mid.astype(F32)).astype(BF16)
    return hi, mid, lo


def running_sums(x):
    rows, width = x.shape
    cuts = width // LANES
    stack = jnp.concatenate([x[:, i * LANES : (i + 1) * LANES] for i in range(cuts)], axis=0)
    parts = jnp.concatenate([t.astype(F32) for t in three_terms(stack)], axis=0).astype(BF16)
    earlier = lax.broadcasted_iota(jnp.int32, (LANES, LANES), 0)
    later = lax.broadcasted_iota(jnp.int32, (LANES, LANES), 1)
    upper = jnp.where(earlier <= later, 1.0, 0.0).astype(BF16)
    sums = nn(parts, upper)
    m = rows * cuts
    sums = sums[:m] + sums[m : 2 * m] + sums[2 * m :]
    pieces, base = [], jnp.zeros((rows, 1), F32)
    for i in range(cuts):
        piece = sums[i * rows : (i + 1) * rows]
        pieces.append(piece + base)
        base = base + piece[:, LANES - 1 :]
    return jnp.concatenate(pieces, axis=1)


def gain_rows(gain):
    heads = gain.shape[0]
    wide = jnp.concatenate([jnp.broadcast_to(gain[h : h + 1], (EXTRA, LANES)) for h in range(heads)], axis=1)
    hi, mid, lo = (t.astype(F32) for t in three_terms(wide))
    row = lax.broadcasted_iota(jnp.int32, wide.shape, 0)
    out = jnp.where(row == 0, hi, jnp.where(row == 1, mid, jnp.where(row == 2, lo, 0.0)))
    return out.astype(BF16)


def gain_of(ref, at, heads):
    block = ref[at : at + EXTRA, :].astype(F32)
    total = block[0:1] + block[1:2] + block[2:3]
    return jnp.concatenate([total[:, h * LANES : (h + 1) * LANES] for h in range(heads)], axis=0)


def wide_row(gain, h, width):
    return jnp.concatenate([gain[h : h + 1]] * (width // LANES), axis=1)


def states_kernel(
    heads, scale, lf, ip, starts, q_in, k_in, v_in, g_in, send, keep, cols, rows, q, k, v, g, seg_in, sems
):
    width = q.shape[0]
    dk, dv = q.shape[1] // heads, v.shape[1] // heads
    copies = []
    for h in range(heads):
        for i, (src, dst, w) in enumerate(((k_in, k, dk), (v_in, v, dv), (q_in, q, dk), (g_in, g, dv))):
            at = pl.ds(h * w, w)
            copies.append(pltpu.make_async_copy(src.at[:, at], dst.at[:, at], sems.at[h, i]))
            copies[-1].start()
    seg_in[...] = jnp.zeros_like(seg_in)
    seg_in[0:heads, :] = lf[...]
    seg_in[heads : heads + 1, :] = starts[...].astype(F32)
    sums = running_sums(seg_in[...])
    decay_sum, segment = sums[0:heads], sums[heads : heads + 1]
    last, final_seg = decay_sum[:, width - 1 :], segment[:, width - 1 :]
    gate = jnp.exp(ip[...])
    tail = jnp.where(segment == final_seg, jnp.exp(last - decay_sum), 0.0)
    head = jnp.where(segment == 0.0, scale * jnp.exp(decay_sum), 0.0)
    gain = jnp.where(final_seg == 0.0, jnp.exp(last), 0.0)
    rows[DECAY : DECAY + heads, :] = decay_sum
    rows[GATE : GATE + heads, :] = gate
    rows[TAIL : TAIL + heads, :] = tail
    rows[HEAD : HEAD + heads, :] = head
    rows[SEG : SEG + 8, :] = jnp.broadcast_to(segment, (8, width))
    rows[TAIL_GATE : TAIL_GATE + heads, :] = tail * gate
    rows[GAIN : GAIN + heads, :] = jnp.broadcast_to(gain, (heads, width))
    cols[...] = rows[...].T
    even = lax.rem(lax.axis_index("ctx"), 2) == 0
    for h in range(heads):
        for copy in copies[4 * h : 4 * h + 4]:
            copy.wait()
        kk, vv = slice(h * dk, (h + 1) * dk), slice(h * dv, (h + 1) * dv)
        scaled_v = (cols[:, TAIL_GATE + h : TAIL_GATE + h + 1] * v[:, vv].astype(F32)).astype(BF16)
        scaled_q = (cols[:, HEAD + h : HEAD + h + 1] * q[:, kk].astype(F32)).astype(BF16)
        forward = tn(k[:, kk], scaled_v)
        backward = tn(scaled_q, g[:, vv])
        send[kk, :] = jnp.where(even, forward, backward).astype(BF16)
        keep[kk, :] = jnp.where(even, backward, forward)
    send[heads * dk :, :] = gain_rows(jnp.broadcast_to(gain, (heads, LANES)))


def chip_kernel(heads, keep, near, rows, out):
    n = keep.shape[0]
    dk, width = n // heads, keep.shape[1]
    own = rows[GAIN : GAIN + heads, 0:LANES]
    for h in range(heads):
        at = slice(h * dk, (h + 1) * dk)
        out[at, :] = (keep[at, :] + wide_row(own, h, width) * near[at, :].astype(F32)).astype(BF16)
    out[n:, :] = gain_rows(own * gain_of(near, n, heads))


def far_kernel(heads, first, second, out):
    n, width = out.shape
    dk = n // heads
    gain = gain_of(first, n, heads)
    for h in range(heads):
        at = slice(h * dk, (h + 1) * dk)
        out[at, :] = (first[at, :].astype(F32) + wide_row(gain, h, width) * second[at, :].astype(F32)).astype(BF16)


def block_kernel(heads, scale, q, k, v, g, cols, rows, gq, gk, gv):
    width = q.shape[0]
    half = width // 2
    dk, dv = q.shape[1] // heads, v.shape[1] // heads
    t = lax.broadcasted_iota(jnp.int32, (half, half), 0)
    u = lax.broadcasted_iota(jnp.int32, (half, half), 1)
    causal = t >= u
    spans = [slice(i * half, (i + 1) * half) for i in range(2)]
    seg_c = [cols[s, SEG : SEG + 1] for s in spans]
    seg_r = [rows[SEG : SEG + 1, s] for s in spans]
    pairs = ((0, 0), (1, 0), (1, 1))
    allowed = [(seg_c[a] == seg_r[b]) & causal if a == b else seg_c[a] == seg_r[b] for a, b in pairs]
    for h in range(heads):
        kk, vv = slice(h * dk, (h + 1) * dk), slice(h * dv, (h + 1) * dv)
        total_q, total_k, total_v = [None] * 2, [None] * 2, [None] * 2

        def add(total, i, x):
            total[i] = x if total[i] is None else total[i] + x

        for (a, b), ok in zip(pairs, allowed, strict=True):
            ra, rb = spans[a], spans[b]
            gap = cols[ra, DECAY + h : DECAY + h + 1] - rows[DECAY + h : DECAY + h + 1, rb]
            decay = scale * jnp.exp(jnp.where(ok, gap, -jnp.inf))
            product = decay * nt(g[ra, vv], v[rb, vv])
            first = (product * rows[GATE + h : GATE + h + 1, rb]).astype(BF16)
            third = (decay * nt(q[ra, kk], k[rb, kk])).astype(BF16)
            add(total_q, a, nn(first, k[rb, kk]))
            add(total_k, b, tn(product.astype(BF16), q[ra, kk]))
            add(total_v, b, tn(third, g[ra, vv]))
        for i in range(2):
            gate = cols[spans[i], GATE + h : GATE + h + 1]
            gq[spans[i], kk] = total_q[i]
            gk[spans[i], kk] = gate * total_k[i]
            gv[spans[i], vv] = gate * total_v[i]


def tail_kernel(
    heads, near, far, other, k, v, g, cols, gq, gk, gv, out_q, out_k, out_v, buf_q, buf_k, buf_v, sems
):
    n, width = far.shape
    dk, dv = n // heads, width
    even = lax.rem(lax.axis_index("ctx"), 2) == 0
    gain = gain_of(near, n, heads)
    copies = []
    for h in range(heads):
        kk, vv = slice(h * dk, (h + 1) * dk), slice(h * dv, (h + 1) * dv)
        x = far[kk, :].astype(F32)
        y = near[kk, :].astype(F32) + wide_row(gain, h, width) * other[kk, :].astype(F32)
        incoming = jnp.where(even, x, y).astype(BF16)
        arriving = jnp.where(even, y, x).astype(BF16)
        tail = cols[:, TAIL_GATE + h : TAIL_GATE + h + 1]
        buf_q[:, kk] = (gq[:, kk] + cols[:, HEAD + h : HEAD + h + 1] * nt(g[:, vv], incoming)).astype(BF16)
        buf_k[:, kk] = (gk[:, kk] + tail * nt(v[:, vv], arriving)).astype(BF16)
        buf_v[:, vv] = (gv[:, vv] + tail * nn(k[:, kk], arriving)).astype(BF16)
        for i, (src, dst, at) in enumerate(((buf_q, out_q, kk), (buf_k, out_k, kk), (buf_v, out_v, vv))):
            copies.append(pltpu.make_async_copy(src.at[:, at], dst.at[:, at], sems.at[h, i]))
            copies[-1].start()
    for copy in copies:
        copy.wait()


def call(kernel, outs, ins, specs_in, specs_out, scratch=(), mib=24, flops=0, moved=0):
    return pl.pallas_call(
        kernel,
        out_shape=[jax.ShapeDtypeStruct(*o) for o in outs],
        in_specs=specs_in,
        out_specs=specs_out,
        scratch_shapes=list(scratch),
        compiler_params=pltpu.CompilerParams(vmem_limit_bytes=mib << 20),
        cost_estimate=pl.CostEstimate(flops=flops, bytes_accessed=moved, transcendentals=0),
    )(*ins)


def in_hbm(x):
    return pltpu.with_memory_space_constraint(x, pltpu.HBM)


def swap(x, route):
    return lax.ppermute(x, "ctx", route)


def routes(size):
    chips = size // 2
    both = lambda pairs: [p for a, b in pairs for p in ((a, b), (b, a))]
    on_chip = both([(2 * c, 2 * c + 1) for c in range(chips)])
    adjacent = both([(2 * c + 1, 2 * c + 2) for c in range(chips - 1)])
    second = both([(2 * c + 1, 2 * c + 4) for c in range(chips - 2)])
    return on_chip, adjacent, second


def body(query_rows, key_rows, value_rows, out_grad, log_forget, input_pre, doc_starts):
    width, heads = log_forget.shape
    dk, dv = query_rows.shape[1] // heads, value_rows.shape[1] // heads
    scale = dk ** (-0.5)
    n = heads * dk
    on_chip, adjacent, second = routes(lax.axis_size("ctx"))
    unit = 2 * width * dk * dv * heads
    send, keep, cols, rows, q, k, v, g = call(
        functools.partial(states_kernel, heads, scale),
        [
            ((n + EXTRA, dv), BF16),
            ((n, dv), F32),
            ((width, ROWS), F32),
            ((ROWS, width), F32),
            (query_rows.shape, BF16),
            (key_rows.shape, BF16),
            (value_rows.shape, BF16),
            (out_grad.shape, BF16),
        ],
        (log_forget.T, input_pre.T, doc_starts.reshape(1, width))
        + tuple(in_hbm(x) for x in (query_rows, key_rows, value_rows, out_grad)),
        [VM, VM, VM, HBM, HBM, HBM, HBM],
        [VM] * 8,
        [pltpu.VMEM((8, width), F32), pltpu.SemaphoreType.DMA((heads, 4))],
        flops=2 * unit,
        moved=12 << 20,
    )
    near = swap(send, on_chip)
    (chip,) = call(
        functools.partial(chip_kernel, heads), [((n + EXTRA, dv), BF16)], (keep, near, rows), [VM] * 3, [VM], mib=16
    )
    first = swap(chip, adjacent)
    later = swap(chip, second)
    gq, gk, gv = call(
        functools.partial(block_kernel, heads, scale),
        [((width, n), F32), ((width, n), F32), ((width, heads * dv), F32)],
        (q, k, v, g, cols, rows),
        [VM] * 6,
        [VM] * 3,
        flops=8 * unit,
        moved=14 << 20,
    )
    first, later, gq = lax.optimization_barrier((first, later, gq))
    (far,) = call(functools.partial(far_kernel, heads), [((n, dv), BF16)], (first, later), [VM] * 2, [VM], mib=16)
    other = swap(far, on_chip)
    return tuple(
        call(
            functools.partial(tail_kernel, heads),
            [(query_rows.shape, BF16), (key_rows.shape, BF16), (value_rows.shape, BF16)],
            (near, far, other, k, v, g, cols, gq, gk, gv),
            [VM] * 10,
            [HBM] * 3,
            [
                pltpu.VMEM(query_rows.shape, BF16),
                pltpu.VMEM(key_rows.shape, BF16),
                pltpu.VMEM(value_rows.shape, BF16),
                pltpu.SemaphoreType.DMA((heads, 3)),
            ],
            flops=3 * unit,
            moved=17 << 20,
        )
    )


def solution(mesh):
    row = P(("groups", "ctx"), None)
    in_specs = (row,) * 6 + (P(("groups", "ctx")),)
    return jax.shard_map(body, mesh=mesh, in_specs=in_specs, out_specs=(row,) * 3, check_vma=False)
```

time: 210 us -> 48 us (0.23)
  the two profiles are of different devices: /device:TPU:9 before, /device:TPU:17 now
where the time goes in v1:
time: 48 us; the launch traced here: 47.7 us
  waiting for transfers between devices  25.9 us (54%)
  Pallas kernels  12.7 us (26%)
  starting transfers between devices  6.3 us (13%)
  local copies, waits for them, and re-layouts  2.07 us (4%)
  between operations  0.69 us (1%)
    ppermute x4, waiting for transfers between devices, swap(): return lax.ppermute(x, 'ctx', route)  25.9 us
    pallas_call x5, Pallas kernels, call(): pl.pallas_call(kernel, out_shape=[jax.ShapeDtypeStruct(*o) for o in outs]...  12.7 us
    ppermute x4, starting transfers between devices, swap(): return lax.ppermute(x, 'ctx', route)  6.3 us
    unnamed x6, local copies, waits for them, and re-layouts  2.07 us
  transfers between devices with their start and end apart: 4, of which 4 were waited for; matrix products, arithmetic and copies ran while one was open for 0% of the time, Pallas kernels for 9%

profile of v1, /device:TPU:17, one launch (start us, length us, event | category | flops | bytes accessed | tf_op | source)
XLA Modules:
  0.0 47.7 jit_solution(13092316814034098611)
XLA Ops:
  0.6 0.0 copy-start
  0.6 0.7 %copy-done = f32[512,4]{0,1:T(4,128)S(1)} copy-done((f32[512,4]{0,1:T(4,128)S(1)}, f32[512,4]{0,1:T(4,128)}, u32[]{:S(2)}) %copy-start) | copy-done | bytes 8216
  1.3 0.0 copy-start.1
  1.3 0.7 %copy-done.1 = f32[512,4]{0,1:T(4,128)S(1)} copy-done((f32[512,4]{0,1:T(4,128)S(1)}, f32[512,4]{0,1:T(4,128)}, u32[]{:S(2)}) %copy-start.1) | copy-done | bytes 8216
  2.0 0.0 copy-start.2
  2.0 0.7 %copy-done.2 = s32[512]{0:T(512)S(1)} copy-done((s32[512]{0:T(512)S(1)}, s32[512]{0:T(512)}, u32[]{:S(2)}) %copy-start.2) | copy-done | bytes 2072
  2.7 4.6 %shard_map.94 = (bf16[1032,512]{1,0:T(8,128)(2,1)S(1)}, f32[1024,512]{1,0:T(8,128)S(1)}, f32[512,32]{1,0:T(8,128)S(1)}, f32[32,512]{1,0:T(8,128)S(1)}, bf16[512,...) custom-call(f32[4,512]{1,0:T(4,128)S(1)} %bitcast.3, ...), custom_call_target="tpu_custom_call" | custom-call | flops 1073741824 | bytes 12582912 | tf_op jit(solution)/shard_map/pallas_call | solution.py:201
  7.3 0.7 %collective-permute-start = (bf16[1032,512]{1,0:T(8,128)(2,1)S(1)}, bf16[1032,512]{1,0:T(8,128)(2,1)S(1)}, u32[]{:S(2)}, u32[]{:S(2)}) collective-permute-start(bf16[1032,512]{1,0:T(8,128)(2,1)S(1)} %get-tuple-element.17), channel_id=1, source_target_pairs={{0,1},{1,0},{2,3},{3,2},{4,5},{5,4},{6,7},{7,6},{8,9},{9,8},{10,11... | collective-permute-start | bytes 3170312 | tf_op jit(solution)/shard_map/ppermute | solution.py:217
  8.0 2.3 %collective-permute-done.near = bf16[1032,512]{1,0:T(8,128)(2,1)S(1)} collective-permute-done((bf16[1032,512]{1,0:T(8,128)(2,1)S(1)}, bf16[1032,512]{1,0:T(8,128)(2,1)S(1)}, u32[]{:S(2)}, u32[]{:S(2)}) %collective-permute-start) | collective-permute-done | bytes 1056800 | tf_op jit(solution)/shard_map/ppermute | solution.py:217
  10.3 0.3 shard_map.95
  10.6 3.5 %collective-permute-start.2 = (bf16[1032,512]{1,0:T(8,128)(2,1)S(1)}, bf16[1032,512]{1,0:T(8,128)(2,1)S(1)}, u32[]{:S(2)}, u32[]{:S(2)}) collective-permute-start(bf16[1032,512]{1,0:T(8,128)(2,1)S(1)} %shard_map.95), channel_id=1, source_target_pairs={{1,4},{4,1},{3,6},{6,3},{5,8},{8,5},{7,10},{10,7},{9,12},{12,9},{1... | collective-permute-start | bytes 3170312 | tf_op jit(solution)/shard_map/ppermute | solution.py:217
  14.1 2.0 %collective-permute-start.1 = (bf16[1032,512]{1,0:T(8,128)(2,1)S(1)}, bf16[1032,512]{1,0:T(8,128)(2,1)S(1)}, u32[]{:S(2)}, u32[]{:S(2)}) collective-permute-start(bf16[1032,512]{1,0:T(8,128)(2,1)S(1)} %shard_map.95), channel_id=1, source_target_pairs={{1,2},{2,1},{3,4},{4,3},{5,6},{6,5},{7,8},{8,7},{9,10},{10,9},{11,... | collective-permute-start | bytes 3170312 | tf_op jit(solution)/shard_map/ppermute | solution.py:217
  16.1 4.5 %shard_map.96 = (f32[512,1024]{1,0:T(8,128)S(1)}, f32[512,1024]{1,0:T(8,128)S(1)}, f32[512,2048]{1,0:T(8,128)S(1)}) custom-call(bf16[512,1024]{1,0:T(8,128)(2,1)S(1)} %get-tuple-element.20.q, bf16[512,1024]{1,0:T(8,128)(2,1)S(1)} %get-tuple-element.21.k, bf16[512,2048]{1,0:T(8,128)(2,1)S(1)} %get-tuple-element.22.v, ...), custom_call_target="tpu_custom_call" | custom-call | flops 4294967296 | bytes 14680064 | tf_op jit(solution)/shard_map/pallas_call | solution.py:201
  20.6 6.2 %collective-permute-done.2.second = bf16[1032,512]{1,0:T(8,128)(2,1)S(1)} collective-permute-done((bf16[1032,512]{1,0:T(8,128)(2,1)S(1)}, bf16[1032,512]{1,0:T(8,128)(2,1)S(1)}, u32[]{:S(2)}, u32[]{:S(2)}) %collective-permute-start.2) | collective-permute-done | bytes 1056800 | tf_op jit(solution)/shard_map/ppermute | solution.py:217
  26.8 14.8 %collective-permute-done.1.first = bf16[1032,512]{1,0:T(8,128)(2,1)S(1)} collective-permute-done((bf16[1032,512]{1,0:T(8,128)(2,1)S(1)}, bf16[1032,512]{1,0:T(8,128)(2,1)S(1)}, u32[]{:S(2)}, u32[]{:S(2)}) %collective-permute-start.1) | collective-permute-done | bytes 1056800 | tf_op jit(solution)/shard_map/ppermute | solution.py:217
  41.6 0.3 shard_map.97.far
  41.9 0.1 collective-permute-start.3
  42.0 2.6 %collective-permute-done.3.other = bf16[1024,512]{1,0:T(8,128)(2,1)S(1)} collective-permute-done((bf16[1024,512]{1,0:T(8,128)(2,1)S(1)}, bf16[1024,512]{1,0:T(8,128)(2,1)S(1)}, u32[]{:S(2)}, u32[]{:S(2)}) %collective-permute-start.3) | collective-permute-done | bytes 1048608 | tf_op jit(solution)/shard_map/ppermute | solution.py:217
  44.6 3.1 %shard_map.98 = (bf16[512,1024]{1,0:T(8,128)(2,1)}, bf16[512,1024]{1,0:T(8,128)(2,1)}, bf16[512,2048]{1,0:T(8,128)(2,1)}) custom-call(bf16[1032,512]{1,0:T(8,128)(2,1)S(1)} %collective-permute-done.near, bf16[1024,512]{1,0:T(8,128)(2,1)S(1)} %shard_map.97.far, bf16[1024,512]{1,0:T(8,128)(2,1)S(1)} %collective-permute-done.3.other, ...), custom_call_target="tpu_custom_call" | custom-call | flops 1610612736 | bytes 17825792 | tf_op jit(solution)/shard_map/pallas_call | solution.py:201
Async XLA Ops:
  0.6 0.7 %copy-start = (f32[512,4]{0,1:T(4,128)S(1)}, f32[512,4]{0,1:T(4,128)}, u32[]{:S(2)}) copy-start(f32[512,4]{0,1:T(4,128)} %param.11) | copy-start | bytes 24580
  1.3 0.7 %copy-start.1 = (f32[512,4]{0,1:T(4,128)S(1)}, f32[512,4]{0,1:T(4,128)}, u32[]{:S(2)}) copy-start(f32[512,4]{0,1:T(4,128)} %param.12) | copy-start | bytes 24580
  2.0 0.7 %copy-start.2 = (s32[512]{0:T(512)S(1)}, s32[512]{0:T(512)}, u32[]{:S(2)}) copy-start(s32[512]{0:T(512)} %param.13) | copy-start | bytes 6148
  7.3 3.0 %collective-permute-start = (bf16[1032,512]{1,0:T(8,128)(2,1)S(1)}, bf16[1032,512]{1,0:T(8,128)(2,1)S(1)}, u32[]{:S(2)}, u32[]{:S(2)}) collective-permute-start(bf16[1032,512]{1,0:T(8,128)(2,1)S(1)} %get-tuple-element.17), channel_id=1, source_target_pairs={{0,1},{1,0},{2,3},{3,2},{4,5},{5,4},{6,7},{7,6},{8,9},{9,8},{10,11... | collective-permute-start | bytes 3170312 | tf_op jit(solution)/shard_map/ppermute | solution.py:217
  10.6 16.2 %collective-permute-start.2 = (bf16[1032,512]{1,0:T(8,128)(2,1)S(1)}, bf16[1032,512]{1,0:T(8,128)(2,1)S(1)}, u32[]{:S(2)}, u32[]{:S(2)}) collective-permute-start(bf16[1032,512]{1,0:T(8,128)(2,1)S(1)} %shard_map.95), channel_id=1, source_target_pairs={{1,4},{4,1},{3,6},{6,3},{5,8},{8,5},{7,10},{10,7},{9,12},{12,9},{1... | collective-permute-start | bytes 3170312 | tf_op jit(solution)/shard_map/ppermute | solution.py:217
  14.1 27.5 %collective-permute-start.1 = (bf16[1032,512]{1,0:T(8,128)(2,1)S(1)}, bf16[1032,512]{1,0:T(8,128)(2,1)S(1)}, u32[]{:S(2)}, u32[]{:S(2)}) collective-permute-start(bf16[1032,512]{1,0:T(8,128)(2,1)S(1)} %shard_map.95), channel_id=1, source_target_pairs={{1,2},{2,1},{3,4},{4,3},{5,6},{6,5},{7,8},{8,7},{9,10},{10,9},{11,... | collective-permute-start | bytes 3170312 | tf_op jit(solution)/shard_map/ppermute | solution.py:217
  41.9 2.7 %collective-permute-start.3 = (bf16[1024,512]{1,0:T(8,128)(2,1)S(1)}, bf16[1024,512]{1,0:T(8,128)(2,1)S(1)}, u32[]{:S(2)}, u32[]{:S(2)}) collective-permute-start(bf16[1024,512]{1,0:T(8,128)(2,1)S(1)} %shard_map.97.far), channel_id=1, source_target_pairs={{0,1},{1,0},{2,3},{3,2},{4,5},{5,4},{6,7},{7,6},{8,9},{9,8},{10,11... | collective-permute-start | bytes 3145736 | tf_op jit(solution)/shard_map/ppermute | solution.py:217

commit v2 on v1

v2 whole, which is shorter than its diff:
```python
import functools

import jax
import jax.numpy as jnp
from jax import lax
from jax.experimental import pallas as pl
from jax.experimental.pallas import tpu as pltpu
from jax.sharding import PartitionSpec as P

F32 = jnp.float32
BF16 = jnp.bfloat16
LANES = 128
EXTRA = 8
CHUNKS = (2, 2)
DECAY, GATE, TAIL, HEAD, SEG, TAIL_GATE, GAIN, ROWS = 0, 4, 8, 12, 16, 24, 28, 32
VM = pl.BlockSpec(memory_space=pltpu.VMEM)
HBM = pl.BlockSpec(memory_space=pltpu.HBM)


def nt(a, b):
    return lax.dot_general(a, b, (((1,), (1,)), ((), ())), preferred_element_type=F32)


def nn(a, b):
    return lax.dot_general(a, b, (((1,), (0,)), ((), ())), preferred_element_type=F32)


def tn(a, b):
    return lax.dot_general(a, b, (((0,), (0,)), ((), ())), preferred_element_type=F32)


def three_terms(x):
    hi = x.astype(BF16)
    rest = x - hi.astype(F32)
    mid = rest.astype(BF16)
    lo = (rest - mid.astype(F32)).astype(BF16)
    return hi, mid, lo


def running_sums(x):
    rows, width = x.shape
    cuts = width // LANES
    stack = jnp.concatenate([x[:, i * LANES : (i + 1) * LANES] for i in range(cuts)], axis=0)
    parts = jnp.concatenate([t.astype(F32) for t in three_terms(stack)], axis=0).astype(BF16)
    earlier = lax.broadcasted_iota(jnp.int32, (LANES, LANES), 0)
    later = lax.broadcasted_iota(jnp.int32, (LANES, LANES), 1)
    upper = jnp.where(earlier <= later, 1.0, 0.0).astype(BF16)
    sums = nn(parts, upper)
    m = rows * cuts
    sums = sums[:m] + sums[m : 2 * m] + sums[2 * m :]
    pieces, base = [], jnp.zeros((rows, 1), F32)
    for i in range(cuts):
        piece = sums[i * rows : (i + 1) * rows]
        pieces.append(piece + base)
        base = base + piece[:, LANES - 1 :]
    return jnp.concatenate(pieces, axis=1)


def gain_rows(gain, width):
    wide = [jnp.broadcast_to(gain[i : i + 1], (EXTRA, LANES)) for i in range(gain.shape[0])]
    wide = jnp.concatenate(wide + [jnp.zeros((EXTRA, width - LANES * len(wide)), F32)], axis=1)
    hi, mid, lo = (t.astype(F32) for t in three_terms(wide))
    row = lax.broadcasted_iota(jnp.int32, wide.shape, 0)
    out = jnp.where(row == 0, hi, jnp.where(row == 1, mid, jnp.where(row == 2, lo, 0.0)))
    return out.astype(BF16)


def gain_of(ref, at, heads):
    block = ref[at : at + EXTRA, :].astype(F32)
    total = block[0:1] + block[1:2] + block[2:3]
    return jnp.concatenate([total[:, h * LANES : (h + 1) * LANES] for h in range(heads)], axis=0)


def wide_row(gain, h, width):
    return jnp.concatenate([gain[h : h + 1]] * (width // LANES), axis=1)


def states_of(span, heads, q, k, v, g, cols, rows, send, keep):
    dk, dv = q.shape[1] // heads, v.shape[1] // heads
    even = lax.rem(lax.axis_index("ctx"), 2) == 0
    for i, h in enumerate(span):
        kk, vv, at = slice(h * dk, (h + 1) * dk), slice(h * dv, (h + 1) * dv), slice(i * dk, (i + 1) * dk)
        scaled_v = (cols[:, TAIL_GATE + h : TAIL_GATE + h + 1] * v[:, vv].astype(F32)).astype(BF16)
        scaled_q = (cols[:, HEAD + h : HEAD + h + 1] * q[:, kk].astype(F32)).astype(BF16)
        forward = tn(k[:, kk], scaled_v)
        backward = tn(scaled_q, g[:, vv])
        send[at, :] = jnp.where(even, forward, backward).astype(BF16)
        keep[at, :] = jnp.where(even, backward, forward)
    send[len(span) * dk :, :] = gain_rows(rows[GAIN + span[0] : GAIN + span[-1] + 1, 0:LANES], dv)


def first_kernel(
    span, heads, scale, lf_in, ip_in, st_in, q_in, k_in, v_in, g_in, send, keep, cols, rows, q, k, v, g, lf, ip, st, sems, small
):
    width = q.shape[0]
    dk, dv = q.shape[1] // heads, v.shape[1] // heads
    gates = [pltpu.make_async_copy(x, y, small.at[i]) for i, (x, y) in enumerate(((lf_in, lf), (ip_in, ip), (st_in, st)))]
    for copy in gates:
        copy.start()
    copies = []
    for h in range(heads):
        for i, (src, dst, w) in enumerate(((k_in, k, dk), (v_in, v, dv), (q_in, q, dk), (g_in, g, dv))):
            at = pl.ds(h * w, w)
            copies.append(pltpu.make_async_copy(src.at[:, at], dst.at[:, at], sems.at[h, i]))
    now, after = copies[: 4 * len(span)], copies[4 * len(span) :]
    for copy in now:
        copy.start()
    for copy in gates:
        copy.wait()
    for copy in after:
        copy.start()
    filler = jnp.zeros((7 - heads, width), F32)
    sums = running_sums(jnp.concatenate([lf[...], st[...].astype(F32), filler], axis=0))
    decay_sum, segment = sums[0:heads], sums[heads : heads + 1]
    last, final_seg = decay_sum[:, width - 1 :], segment[:, width - 1 :]
    gate = jnp.exp(ip[...])
    tail = jnp.where(segment == final_seg, jnp.exp(last - decay_sum), 0.0)
    head = jnp.where(segment == 0.0, scale * jnp.exp(decay_sum), 0.0)
    gain = jnp.where(final_seg == 0.0, jnp.exp(last), 0.0)
    rows[DECAY : DECAY + heads, :] = decay_sum
    rows[GATE : GATE + heads, :] = gate
    rows[TAIL : TAIL + heads, :] = tail
    rows[HEAD : HEAD + heads, :] = head
    rows[SEG : SEG + 8, :] = jnp.broadcast_to(segment, (8, width))
    rows[TAIL_GATE : TAIL_GATE + heads, :] = tail * gate
    rows[GAIN : GAIN + heads, :] = jnp.broadcast_to(gain, (heads, width))
    cols[...] = rows[...].T
    for copy in now:
        copy.wait()
    states_of(span, heads, q, k, v, g, cols, rows, send, keep)
    for copy in after:
        copy.wait()


def next_kernel(span, heads, q, k, v, g, cols, rows, send, keep):
    states_of(span, heads, q, k, v, g, cols, rows, send, keep)


def chip_kernel(span, keep, near, rows, out, token):
    token[...] = jnp.zeros_like(token)
    n, width = keep.shape
    m = len(span)
    dk = n // m
    own = rows[GAIN + span[0] : GAIN + span[-1] + 1, 0:LANES]
    for i in range(m):
        at = slice(i * dk, (i + 1) * dk)
        out[at, :] = (keep[at, :] + wide_row(own, i, width) * near[at, :].astype(F32)).astype(BF16)
    out[n:, :] = gain_rows(own * gain_of(near, n, m), width)


def far_kernel(m, second, first, token, out):
    n, width = out.shape
    dk = n // m
    gain = gain_of(first, n, m)
    for i in range(m):
        at = slice(i * dk, (i + 1) * dk)
        out[at, :] = (first[at, :].astype(F32) + wide_row(gain, i, width) * second[at, :].astype(F32)).astype(BF16)


def block_kernel(heads, scale, q, k, v, g, cols, rows, ready, gq, gk, gv, token):
    token[...] = jnp.zeros_like(token)
    width = q.shape[0]
    half = width // 2
    dk, dv = q.shape[1] // heads, v.shape[1] // heads
    t = lax.broadcasted_iota(jnp.int32, (half, half), 0)
    u = lax.broadcasted_iota(jnp.int32, (half, half), 1)
    causal = t >= u
    spans = [slice(i * half, (i + 1) * half) for i in range(2)]
    seg_c = [cols[s, SEG : SEG + 1] for s in spans]
    seg_r = [rows[SEG : SEG + 1, s] for s in spans]
    pairs = ((0, 0), (1, 0), (1, 1))
    allowed = [(seg_c[a] == seg_r[b]) & causal if a == b else seg_c[a] == seg_r[b] for a, b in pairs]
    for h in range(heads):
        kk, vv = slice(h * dk, (h + 1) * dk), slice(h * dv, (h + 1) * dv)
        total_q, total_k, total_v = [None] * 2, [None] * 2, [None] * 2

        def add(total, i, x):
            total[i] = x if total[i] is None else total[i] + x

        for (a, b), ok in zip(pairs, allowed, strict=True):
            ra, rb = spans[a], spans[b]
            gap = cols[ra, DECAY + h : DECAY + h + 1] - rows[DECAY + h : DECAY + h + 1, rb]
            decay = scale * jnp.exp(jnp.where(ok, gap, -jnp.inf))
            product = decay * nt(g[ra, vv], v[rb, vv])
            first = (product * rows[GATE + h : GATE + h + 1, rb]).astype(BF16)
            third = (decay * nt(q[ra, kk], k[rb, kk])).astype(BF16)
            add(total_q, a, nn(first, k[rb, kk]))
            add(total_k, b, tn(product.astype(BF16), q[ra, kk]))
            add(total_v, b, tn(third, g[ra, vv]))
        for i in range(2):
            gate = cols[spans[i], GATE + h : GATE + h + 1]
            gq[spans[i], kk] = total_q[i]
            gk[spans[i], kk] = gate * total_k[i]
            gv[spans[i], vv] = gate * total_v[i]


def tail_kernel(span, heads, near, far, other, k, v, g, cols, gq, gk, gv, *refs):
    out_q, out_k, out_v, token, buf_q, buf_k, buf_v, sems = refs[-8:]
    token[...] = jnp.zeros_like(token)
    n, width = far.shape
    m = len(span)
    dk, dv = n // m, width
    even = lax.rem(lax.axis_index("ctx"), 2) == 0
    gain = gain_of(near, n, m)
    copies = []
    for i, h in enumerate(span):
        kk, vv, at = slice(h * dk, (h + 1) * dk), slice(h * dv, (h + 1) * dv), slice(i * dk, (i + 1) * dk)
        bv = slice(i * dv, (i + 1) * dv)
        x = far[at, :].astype(F32)
        y = near[at, :].astype(F32) + wide_row(gain, i, width) * other[at, :].astype(F32)
        incoming = jnp.where(even, x, y).astype(BF16)
        arriving = jnp.where(even, y, x).astype(BF16)
        tail = cols[:, TAIL_GATE + h : TAIL_GATE + h + 1]
        buf_q[:, at] = (gq[:, kk] + cols[:, HEAD + h : HEAD + h + 1] * nt(g[:, vv], incoming)).astype(BF16)
        buf_k[:, at] = (gk[:, kk] + tail * nt(v[:, vv], arriving)).astype(BF16)
        buf_v[:, bv] = (gv[:, vv] + tail * nn(k[:, kk], arriving)).astype(BF16)
        for j, (src, a, dst, b) in enumerate(((buf_q, at, out_q, kk), (buf_k, at, out_k, kk), (buf_v, bv, out_v, vv))):
            copies.append(pltpu.make_async_copy(src.at[:, a], dst.at[:, b], sems.at[i, j]))
            copies[-1].start()
    for copy in copies:
        copy.wait()


def call(kernel, outs, ins, specs_in, specs_out, scratch=(), mib=20, flops=0, moved=0, aliases=None):
    return pl.pallas_call(
        kernel,
        out_shape=[jax.ShapeDtypeStruct(*o) for o in outs],
        in_specs=specs_in,
        out_specs=specs_out,
        scratch_shapes=list(scratch),
        input_output_aliases=aliases or {},
        compiler_params=pltpu.CompilerParams(vmem_limit_bytes=mib << 20),
        cost_estimate=pl.CostEstimate(flops=flops // 1000000, bytes_accessed=moved // 1000000, transcendentals=0),
    )(*ins)


def in_hbm(x):
    return pltpu.with_memory_space_constraint(x, pltpu.HBM)


def swap(x, route):
    return lax.ppermute(x, "ctx", route)


def routes(size):
    chips = size // 2
    both = lambda pairs: [p for a, b in pairs for p in ((a, b), (b, a))]
    on_chip = both([(2 * c, 2 * c + 1) for c in range(chips)])
    adjacent = both([(2 * c + 1, 2 * c + 2) for c in range(chips - 1)])
    second = both([(2 * c + 1, 2 * c + 4) for c in range(chips - 2)])
    return on_chip, adjacent, second


def body(query_rows, key_rows, value_rows, out_grad, log_forget, input_pre, doc_starts):
    width, heads = log_forget.shape
    dk, dv = query_rows.shape[1] // heads, value_rows.shape[1] // heads
    scale = dk ** (-0.5)
    on_chip, adjacent, second = routes(lax.axis_size("ctx"))
    unit = 2 * width * dk * dv
    spans, at = [], 0
    for m in CHUNKS:
        spans.append(tuple(range(at, at + m)))
        at += m
    payload = [((m * dk + EXTRA, dv), BF16) for m in CHUNKS]
    total = [((m * dk, dv), F32) for m in CHUNKS]
    send, keep, cols, rows, q, k, v, g = call(
        functools.partial(first_kernel, spans[0], heads, scale),
        [
            payload[0],
            total[0],
            ((width, ROWS), F32),
            ((ROWS, width), F32),
            (query_rows.shape, BF16),
            (key_rows.shape, BF16),
            (value_rows.shape, BF16),
            (out_grad.shape, BF16),
        ],
        tuple(
            in_hbm(x)
            for x in (
                log_forget.T, input_pre.T, doc_starts.reshape(1, width), query_rows, key_rows, value_rows, out_grad
            )
        ),
        [HBM] * 7,
        [VM] * 8,
        [
            pltpu.VMEM((heads, width), F32),
            pltpu.VMEM((heads, width), F32),
            pltpu.VMEM((1, width), jnp.int32),
            pltpu.SemaphoreType.DMA((heads, 4)),
            pltpu.SemaphoreType.DMA((3,)),
        ],
        flops=2 * unit * CHUNKS[0],
        moved=12 << 20,
    )
    sends, keeps = [send], [keep]
    for i in range(1, len(CHUNKS)):
        send, keep = call(
            functools.partial(next_kernel, spans[i], heads),
            [payload[i], total[i]],
            (q, k, v, g, cols, rows),
            [VM] * 6,
            [VM] * 2,
            flops=2 * unit * CHUNKS[i],
            moved=4 << 20,
        )
        sends.append(send)
        keeps.append(keep)
    nears, firsts, seconds = [], [], []
    for i, span in enumerate(spans):
        near = swap(sends[i], on_chip)
        if i + 1 < len(spans):
            near, sends[i + 1] = lax.optimization_barrier((near, sends[i + 1]))
        chip, token = call(
            functools.partial(chip_kernel, span),
            [payload[i], ((8, LANES), F32)],
            (keeps[i], near, rows),
            [VM] * 3,
            [VM] * 2,
            mib=8,
        )
        seconds.append(swap(chip, second))
        firsts.append(swap(chip, adjacent))
        nears.append(near)
    gq, gk, gv, token = call(
        functools.partial(block_kernel, heads, scale),
        [((width, heads * dk), F32), ((width, heads * dk), F32), ((width, heads * dv), F32), ((8, LANES), F32)],
        (q, k, v, g, cols, rows, token),
        [VM] * 7,
        [VM] * 4,
        flops=8 * unit * heads,
        moved=14 << 20,
    )
    outs, token = (), token
    for i, span in enumerate(spans):
        m = len(span)
        (far,) = call(functools.partial(far_kernel, m), [((m * dk, dv), BF16)], (seconds[i], firsts[i], token), [VM] * 3, [VM], mib=8)
        other = swap(far, on_chip)
        *outs, token = call(
            functools.partial(tail_kernel, span, heads),
            [(query_rows.shape, BF16), (key_rows.shape, BF16), (value_rows.shape, BF16), ((8, LANES), F32)],
            (nears[i], far, other, k, v, g, cols, gq, gk, gv) + tuple(in_hbm(x) for x in outs),
            [VM] * 10 + [HBM] * len(outs),
            [HBM] * 3 + [VM],
            [
                pltpu.VMEM((width, m * dk), BF16),
                pltpu.VMEM((width, m * dk), BF16),
                pltpu.VMEM((width, m * dv), BF16),
                pltpu.SemaphoreType.DMA((m, 3)),
            ],
            flops=3 * unit * m,
            moved=(17 << 20) // len(spans),
            aliases={10 + j: j for j in range(len(outs))},
        )
    return tuple(outs)


def solution(mesh):
    row = P(("groups", "ctx"), None)
    in_specs = (row,) * 6 + (P(("groups", "ctx")),)
    return jax.shard_map(body, mesh=mesh, in_specs=in_specs, out_specs=(row,) * 3, check_vma=False)
```

time: 48 us -> 42.3 us (0.88)
  the two profiles are of different devices: /device:TPU:17 before, /device:TPU:0 now
where the time goes in v2:
time: 42.3 us; the launch traced here: 42.1 us
  starting transfers between devices  22.5 us (53%)
  Pallas kernels  15.4 us (36%)
  waiting for transfers between devices  3.49 us (8%)
  between operations  0.75 us (2%)
    ppermute x8, starting transfers between devices, swap(): return lax.ppermute(x, 'ctx', route)  22.5 us
    pallas_call x9, Pallas kernels, call(): pl.pallas_call(kernel, out_shape=[jax.ShapeDtypeStruct(*o) for o in outs]...  15.4 us
    ppermute x8, waiting for transfers between devices, swap(): return lax.ppermute(x, 'ctx', route)  3.49 us
  transfers between devices with their start and end apart: 8, of which 3 were waited for; matrix products, arithmetic and copies ran while one was open for 0% of the time, Pallas kernels for 21%

profile of v2, /device:TPU:0, one launch (start us, length us, event | category | flops | bytes accessed | tf_op | source)
XLA Modules:
  0.0 42.1 jit_solution(11421053601992667484)
XLA Ops:
  0.6 3.6 %shard_map.94 = (bf16[520,512]{1,0:T(8,128)(2,1)S(1)}, f32[512,512]{1,0:T(8,128)S(1)}, f32[512,32]{1,0:T(8,128)S(1)}, f32[32,512]{1,0:T(8,128)S(1)}, bf16[512,10...) custom-call(f32[4,512]{1,0:T(4,128)} %bitcast.3, ...), custom_call_target="tpu_custom_call" | custom-call | flops 536 | bytes 12 | tf_op jit(solution)/shard_map/pallas_call | solution.py:225
  4.3 0.5 %collective-permute-start = (bf16[520,512]{1,0:T(8,128)(2,1)S(1)}, bf16[520,512]{1,0:T(8,128)(2,1)S(1)}, u32[]{:S(2)}, u32[]{:S(2)}) collective-permute-start(bf16[520,512]{1,0:T(8,128)(2,1)S(1)} %get-tuple-element.29), channel_id=1, source_target_pairs={{0,1},{1,0},{2,3},{3,2},{4,5},{5,4},{6,7},{7,6},{8,9},{9,8},{10,11... | collective-permute-start | bytes 1597448 | tf_op jit(solution)/shard_map/ppermute | solution.py:242
  4.8 1.1 %shard_map.95 = (bf16[520,512]{1,0:T(8,128)(2,1)S(1)}, f32[512,512]{1,0:T(8,128)S(1)}) custom-call(bf16[512,1024]{1,0:T(8,128)(2,1)S(1)} %get-tuple-element.30.q, bf16[512,1024]{1,0:T(8,128)(2,1)S(1)} %get-tuple-element.31.k, bf16[512,2048]{1,0:T(8,128)(2,1)S(1)} %get-tuple-element.32.v, bf16[512,2048]{1,0:T(8,128)(2,1)S(1)} %get-tuple-element.33.g, ...), custom_call_target="tpu_custom_call" | custom-call | flops 536 | bytes 4 | tf_op jit(solution)/shard_map/pallas_call | solution.py:225
  6.0 0.4 collective-permute-done.near
  6.3 0.4 collective-permute-start.1
  6.7 0.7 %shard_map.97 = (bf16[520,512]{1,0:T(8,128)(2,1)S(1)}, f32[8,128]{1,0:T(8,128)}) custom-call(f32[512,512]{1,0:T(8,128)S(1)} %get-tuple-element.41.keep, bf16[520,512]{1,0:T(8,128)(2,1)S(1)} %collective-permute-done.near, f32[32,512]{1,0:T(8,128)S(1)} %get-tuple-element.35.rows), custom_call_target="tpu_custom_call" | custom-call | tf_op jit(solution)/shard_map/pallas_call | solution.py:225
  7.4 0.7 %collective-permute-start.5 = (bf16[520,512]{1,0:T(8,128)(2,1)S(1)}, bf16[520,512]{1,0:T(8,128)(2,1)S(1)}, u32[]{:S(2)}, u32[]{:S(2)}) collective-permute-start(bf16[520,512]{1,0:T(8,128)(2,1)S(1)} %get-tuple-element.42), channel_id=1, source_target_pairs={{1,2},{2,1},{3,4},{4,3},{5,6},{6,5},{7,8},{8,7},{9,10},{10,9},{11,... | collective-permute-start | bytes 1597448 | tf_op jit(solution)/shard_map/ppermute | solution.py:242
  8.1 0.7 %collective-permute-start.4 = (bf16[520,512]{1,0:T(8,128)(2,1)S(1)}, bf16[520,512]{1,0:T(8,128)(2,1)S(1)}, u32[]{:S(2)}, u32[]{:S(2)}) collective-permute-start(bf16[520,512]{1,0:T(8,128)(2,1)S(1)} %get-tuple-element.42), channel_id=1, source_target_pairs={{1,4},{4,1},{3,6},{6,3},{5,8},{8,5},{7,10},{10,7},{9,12},{12,9},{1... | collective-permute-start | bytes 1597448 | tf_op jit(solution)/shard_map/ppermute | solution.py:242
  8.8 0.0 collective-permute-done.1.near
  8.8 0.1 shard_map.96
  8.9 0.7 %collective-permute-start.3 = (bf16[520,512]{1,0:T(8,128)(2,1)S(1)}, bf16[520,512]{1,0:T(8,128)(2,1)S(1)}, u32[]{:S(2)}, u32[]{:S(2)}) collective-permute-start(bf16[520,512]{1,0:T(8,128)(2,1)S(1)} %get-tuple-element.39), channel_id=1, source_target_pairs={{1,2},{2,1},{3,4},{4,3},{5,6},{6,5},{7,8},{8,7},{9,10},{10,9},{11,... | collective-permute-start | bytes 1597448 | tf_op jit(solution)/shard_map/ppermute | solution.py:242
  9.7 0.7 %collective-permute-start.2 = (bf16[520,512]{1,0:T(8,128)(2,1)S(1)}, bf16[520,512]{1,0:T(8,128)(2,1)S(1)}, u32[]{:S(2)}, u32[]{:S(2)}) collective-permute-start(bf16[520,512]{1,0:T(8,128)(2,1)S(1)} %get-tuple-element.39), channel_id=1, source_target_pairs={{1,4},{4,1},{3,6},{6,3},{5,8},{8,5},{7,10},{10,7},{9,12},{12,9},{1... | collective-permute-start | bytes 1597448 | tf_op jit(solution)/shard_map/ppermute | solution.py:242
  10.4 4.6 %shard_map.98 = (f32[512,1024]{1,0:T(8,128)S(1)}, f32[512,1024]{1,0:T(8,128)S(1)}, f32[512,2048]{1,0:T(8,128)S(1)}, f32[8,128]{1,0:T(8,128)S(1)}) custom-call(bf16[512,1024]{1,0:T(8,128)(2,1)S(1)} %get-tuple-element.30.q, bf16[512,1024]{1,0:T(8,128)(2,1)S(1)} %get-tuple-element.31.k, bf16[512,2048]{1,0:T(8,128)(2,1)S(1)} %get-tuple-element.32.v, ...), custom_call_target="tpu_custom_call" | custom-call | flops 4294 | bytes 14 | tf_op jit(solution)/shard_map/pallas_call | solution.py:225
  15.0 0.0 collective-permute-done.5.first
  15.0 0.0 collective-permute-done.4.second
  15.0 0.2 shard_map.99.far
  15.1 11.3 %collective-permute-start.6 = (bf16[512,512]{1,0:T(8,128)(2,1)S(1)}, bf16[512,512]{1,0:T(8,128)(2,1)S(1)}, u32[]{:S(2)}, u32[]{:S(2)}) collective-permute-start(bf16[512,512]{1,0:T(8,128)(2,1)S(1)} %shard_map.99.far), channel_id=1, source_target_pairs={{0,1},{1,0},{2,3},{3,2},{4,5},{5,4},{6,7},{7,6},{8,9},{9,8},{10,11... | collective-permute-start | bytes 1572872 | tf_op jit(solution)/shard_map/ppermute | solution.py:242
  26.4 1.5 %collective-permute-done.6.other = bf16[512,512]{1,0:T(8,128)(2,1)S(1)} collective-permute-done((bf16[512,512]{1,0:T(8,128)(2,1)S(1)}, bf16[512,512]{1,0:T(8,128)(2,1)S(1)}, u32[]{:S(2)}, u32[]{:S(2)}) %collective-permute-start.6) | collective-permute-done | bytes 524320 | tf_op jit(solution)/shard_map/ppermute | solution.py:242
  28.0 2.1 %shard_map.100 = (bf16[512,1024]{1,0:T(8,128)(2,1)}, bf16[512,1024]{1,0:T(8,128)(2,1)}, bf16[512,2048]{1,0:T(8,128)(2,1)}, f32[8,128]{1,0:T(8,128)S(1)}) custom-call(bf16[520,512]{1,0:T(8,128)(2,1)S(1)} %collective-permute-done.near, bf16[512,512]{1,0:T(8,128)(2,1)S(1)} %shard_map.99.far, bf16[512,512]{1,0:T(8,128)(2,1)S(1)} %collective-permute-done.6.other, ...), custom_call_target="tpu_custom_call" | custom-call | flops 805 | bytes 8 | tf_op jit(solution)/shard_map/pallas_call | solution.py:225
  30.1 0.0 collective-permute-done.3.first
  30.1 0.0 collective-permute-done.2.second
  30.1 0.2 shard_map.101.far
  30.3 7.6 %collective-permute-start.7 = (bf16[512,512]{1,0:T(8,128)(2,1)S(1)}, bf16[512,512]{1,0:T(8,128)(2,1)S(1)}, u32[]{:S(2)}, u32[]{:S(2)}) collective-permute-start(bf16[512,512]{1,0:T(8,128)(2,1)S(1)} %shard_map.101.far), channel_id=1, source_target_pairs={{0,1},{1,0},{2,3},{3,2},{4,5},{5,4},{6,7},{7,6},{8,9},{9,8},{10,11... | collective-permute-start | bytes 1572872 | tf_op jit(solution)/shard_map/ppermute | solution.py:242
  37.9 1.5 %collective-permute-done.7.other = bf16[512,512]{1,0:T(8,128)(2,1)S(1)} collective-permute-done((bf16[512,512]{1,0:T(8,128)(2,1)S(1)}, bf16[512,512]{1,0:T(8,128)(2,1)S(1)}, u32[]{:S(2)}, u32[]{:S(2)}) %collective-permute-start.7) | collective-permute-done | bytes 524320 | tf_op jit(solution)/shard_map/ppermute | solution.py:242
  39.4 2.7 %shard_map.102 = (bf16[512,1024]{1,0:T(8,128)(2,1)}, bf16[512,1024]{1,0:T(8,128)(2,1)}, bf16[512,2048]{1,0:T(8,128)(2,1)}, f32[8,128]{1,0:T(8,128)}) custom-call(bf16[520,512]{1,0:T(8,128)(2,1)S(1)} %collective-permute-done.1.near, bf16[512,512]{1,0:T(8,128)(2,1)S(1)} %shard_map.101.far, ...), custom_call_target="tpu_custom_call", output_to_operand_aliasing={{0}: (10, {}), {1}: (11, {}), {2}: (12, {})} | custom-call | flops 805 | bytes 8 | tf_op jit(solution)/shard_map/pallas_call | solution.py:225
Async XLA Ops:
  4.3 2.1 %collective-permute-start = (bf16[520,512]{1,0:T(8,128)(2,1)S(1)}, bf16[520,512]{1,0:T(8,128)(2,1)S(1)}, u32[]{:S(2)}, u32[]{:S(2)}) collective-permute-start(bf16[520,512]{1,0:T(8,128)(2,1)S(1)} %get-tuple-element.29), channel_id=1, source_target_pairs={{0,1},{1,0},{2,3},{3,2},{4,5},{5,4},{6,7},{7,6},{8,9},{9,8},{10,11... | collective-permute-start | bytes 1597448 | tf_op jit(solution)/shard_map/ppermute | solution.py:242
  6.3 2.5 %collective-permute-start.1 = (bf16[520,512]{1,0:T(8,128)(2,1)S(1)}, bf16[520,512]{1,0:T(8,128)(2,1)S(1)}, u32[]{:S(2)}, u32[]{:S(2)}) collective-permute-start(bf16[520,512]{1,0:T(8,128)(2,1)S(1)} %get-tuple-element.37), channel_id=1, source_target_pairs={{0,1},{1,0},{2,3},{3,2},{4,5},{5,4},{6,7},{7,6},{8,9},{9,8},{10,11... | collective-permute-start | bytes 1597448 | tf_op jit(solution)/shard_map/ppermute | solution.py:242
  7.4 7.6 %collective-permute-start.5 = (bf16[520,512]{1,0:T(8,128)(2,1)S(1)}, bf16[520,512]{1,0:T(8,128)(2,1)S(1)}, u32[]{:S(2)}, u32[]{:S(2)}) collective-permute-start(bf16[520,512]{1,0:T(8,128)(2,1)S(1)} %get-tuple-element.42), channel_id=1, source_target_pairs={{1,2},{2,1},{3,4},{4,3},{5,6},{6,5},{7,8},{8,7},{9,10},{10,9},{11,... | collective-permute-start | bytes 1597448 | tf_op jit(solution)/shard_map/ppermute | solution.py:242
  8.1 6.9 %collective-permute-start.4 = (bf16[520,512]{1,0:T(8,128)(2,1)S(1)}, bf16[520,512]{1,0:T(8,128)(2,1)S(1)}, u32[]{:S(2)}, u32[]{:S(2)}) collective-permute-start(bf16[520,512]{1,0:T(8,128)(2,1)S(1)} %get-tuple-element.42), channel_id=1, source_target_pairs={{1,4},{4,1},{3,6},{6,3},{5,8},{8,5},{7,10},{10,7},{9,12},{12,9},{1... | collective-permute-start | bytes 1597448 | tf_op jit(solution)/shard_map/ppermute | solution.py:242
  8.9 21.1 %collective-permute-start.3 = (bf16[520,512]{1,0:T(8,128)(2,1)S(1)}, bf16[520,512]{1,0:T(8,128)(2,1)S(1)}, u32[]{:S(2)}, u32[]{:S(2)}) collective-permute-start(bf16[520,512]{1,0:T(8,128)(2,1)S(1)} %get-tuple-element.39), channel_id=1, source_target_pairs={{1,2},{2,1},{3,4},{4,3},{5,6},{6,5},{7,8},{8,7},{9,10},{10,9},{11,... | collective-permute-start | bytes 1597448 | tf_op jit(solution)/shard_map/ppermute | solution.py:242
  9.7 20.4 %collective-permute-start.2 = (bf16[520,512]{1,0:T(8,128)(2,1)S(1)}, bf16[520,512]{1,0:T(8,128)(2,1)S(1)}, u32[]{:S(2)}, u32[]{:S(2)}) collective-permute-start(bf16[520,512]{1,0:T(8,128)(2,1)S(1)} %get-tuple-element.39), channel_id=1, source_target_pairs={{1,4},{4,1},{3,6},{6,3},{5,8},{8,5},{7,10},{10,7},{9,12},{12,9},{1... | collective-permute-start | bytes 1597448 | tf_op jit(solution)/shard_map/ppermute | solution.py:242
  15.1 12.8 %collective-permute-start.6 = (bf16[512,512]{1,0:T(8,128)(2,1)S(1)}, bf16[512,512]{1,0:T(8,128)(2,1)S(1)}, u32[]{:S(2)}, u32[]{:S(2)}) collective-permute-start(bf16[512,512]{1,0:T(8,128)(2,1)S(1)} %shard_map.99.far), channel_id=1, source_target_pairs={{0,1},{1,0},{2,3},{3,2},{4,5},{5,4},{6,7},{7,6},{8,9},{9,8},{10,11... | collective-permute-start | bytes 1572872 | tf_op jit(solution)/shard_map/ppermute | solution.py:242
  30.3 9.1 %collective-permute-start.7 = (bf16[512,512]{1,0:T(8,128)(2,1)S(1)}, bf16[512,512]{1,0:T(8,128)(2,1)S(1)}, u32[]{:S(2)}, u32[]{:S(2)}) collective-permute-start(bf16[512,512]{1,0:T(8,128)(2,1)S(1)} %shard_map.101.far), channel_id=1, source_target_pairs={{0,1},{1,0},{2,3},{3,2},{4,5},{5,4},{6,7},{7,6},{8,9},{9,8},{10,11... | collective-permute-start | bytes 1572872 | tf_op jit(solution)/shard_map/ppermute | solution.py:242

commit v3 on v2

--- a/solution.py
+++ b/solution.py
@@ -136,7 +136,8 @@
     states_of(span, heads, q, k, v, g, cols, rows, send, keep)
 
 
-def chip_kernel(span, keep, near, rows, out, token):
+def chip_kernel(span, keep, near, rows, *refs):
+    out, token = refs[-2:] if len(refs) == 2 else refs[1:3]
     token[...] = jnp.zeros_like(token)
     n, width = keep.shape
     m = len(span)
@@ -148,7 +149,7 @@
     out[n:, :] = gain_rows(own * gain_of(near, n, m), width)
 
 
-def far_kernel(m, second, first, token, out):
+def far_kernel(m, first, second, token, out):
     n, width = out.shape
     dk = n // m
     gain = gain_of(first, n, m)
@@ -157,7 +158,7 @@
         out[at, :] = (first[at, :].astype(F32) + wide_row(gain, i, width) * second[at, :].astype(F32)).astype(BF16)
 
 
-def block_kernel(heads, scale, q, k, v, g, cols, rows, ready, gq, gk, gv, token):
+def block_kernel(span, heads, scale, q, k, v, g, cols, rows, ready, gq, gk, gv, token):
     token[...] = jnp.zeros_like(token)
     width = q.shape[0]
     half = width // 2
@@ -170,7 +171,7 @@
     seg_r = [rows[SEG : SEG + 1, s] for s in spans]
     pairs = ((0, 0), (1, 0), (1, 1))
     allowed = [(seg_c[a] == seg_r[b]) & causal if a == b else seg_c[a] == seg_r[b] for a, b in pairs]
-    for h in range(heads):
+    for n, h in enumerate(span):
         kk, vv = slice(h * dk, (h + 1) * dk), slice(h * dv, (h + 1) * dv)
         total_q, total_k, total_v = [None] * 2, [None] * 2, [None] * 2
 
@@ -189,39 +190,78 @@
             add(total_v, b, tn(third, g[ra, vv]))
         for i in range(2):
             gate = cols[spans[i], GATE + h : GATE + h + 1]
-            gq[spans[i], kk] = total_q[i]
-            gk[spans[i], kk] = gate * total_k[i]
-            gv[spans[i], vv] = gate * total_v[i]
-
-
-def tail_kernel(span, heads, near, far, other, k, v, g, cols, gq, gk, gv, *refs):
-    out_q, out_k, out_v, token, buf_q, buf_k, buf_v, sems = refs[-8:]
-    token[...] = jnp.zeros_like(token)
-    n, width = far.shape
+            gq[spans[i], n * dk : (n + 1) * dk] = total_q[i]
+            gk[spans[i], n * dk : (n + 1) * dk] = gate * total_k[i]
+            gv[spans[i], n * dv : (n + 1) * dv] = gate * total_v[i]
+
+
+def far_tail_kernel(span, far, k, v, g, cols, gq, gk, gv, *refs):
+    out_q, out_k, out_v, buf_q, buf_k, buf_v, sems = refs[-7:]
+    even = lax.rem(lax.axis_index("ctx"), 2) == 0
+    state = lambda at, width: far[at, :]
+    tail_terms(span, even, state, k, v, g, cols, gq, gk, gv, out_q, out_k, out_v, buf_q, buf_k, buf_v, sems)
+
+
+def near_tail_kernel(span, marks, near, other, far_ready, k, v, g, cols, gq, gk, gv, *refs):
+    out_q, out_k, out_v = refs[-7 - marks : -4 - marks]
+    buf_q, buf_k, buf_v, sems = refs[-4:]
+    for token in refs[-4 - marks : -4]:
+        token[...] = jnp.zeros_like(token)
+    odd = lax.rem(lax.axis_index("ctx"), 2) == 1
+    n, width = other.shape
+    gain = gain_of(near, n, len(span))
+    dk = n // len(span)
+
+    def state(at, width):
+        i = at.start // dk
+        return (near[at, :].astype(F32) + wide_row(gain, i, width) * other[at, :].astype(F32)).astype(BF16)
+
+    tail_terms(span, odd, state, k, v, g, cols, gq, gk, gv, out_q, out_k, out_v, buf_q, buf_k, buf_v, sems)
+
+
+def tail_terms(span, incoming, state, k, v, g, cols, gq, gk, gv, out_q, out_k, out_v, buf_q, buf_k, buf_v, sems):
     m = len(span)
-    dk, dv = n // m, width
-    even = lax.rem(lax.axis_index("ctx"), 2) == 0
-    gain = gain_of(near, n, m)
-    copies = []
-    for i, h in enumerate(span):
-        kk, vv, at = slice(h * dk, (h + 1) * dk), slice(h * dv, (h + 1) * dv), slice(i * dk, (i + 1) * dk)
-        bv = slice(i * dv, (i + 1) * dv)
-        x = far[at, :].astype(F32)
-        y = near[at, :].astype(F32) + wide_row(gain, i, width) * other[at, :].astype(F32)
-        incoming = jnp.where(even, x, y).astype(BF16)
-        arriving = jnp.where(even, y, x).astype(BF16)
-        tail = cols[:, TAIL_GATE + h : TAIL_GATE + h + 1]
-        buf_q[:, at] = (gq[:, kk] + cols[:, HEAD + h : HEAD + h + 1] * nt(g[:, vv], incoming)).astype(BF16)
-        buf_k[:, at] = (gk[:, kk] + tail * nt(v[:, vv], arriving)).astype(BF16)
-        buf_v[:, bv] = (gv[:, vv] + tail * nn(k[:, kk], arriving)).astype(BF16)
-        for j, (src, a, dst, b) in enumerate(((buf_q, at, out_q, kk), (buf_k, at, out_k, kk), (buf_v, bv, out_v, vv))):
-            copies.append(pltpu.make_async_copy(src.at[:, a], dst.at[:, b], sems.at[i, j]))
+    dk, dv = gk.shape[1] // m, gv.shape[1] // m
+
+    def copy_out(i, h, j):
+        src, dst, w = ((buf_q, out_q, dk), (buf_k, out_k, dk), (buf_v, out_v, dv))[j]
+        return pltpu.make_async_copy(
+            src.at[:, i * w : (i + 1) * w], dst.at[:, h * w : (h + 1) * w], sems.at[i, j]
+        )
+
+    def spans_of(i, h):
+        return (slice(i * dk, (i + 1) * dk), slice(h * dk, (h + 1) * dk)), (slice(i * dv, (i + 1) * dv), slice(h * dv, (h + 1) * dv))
+
+    @pl.when(incoming)
+    def _():
+        copies = []
+        for i, h in enumerate(span):
+            (at, kk), (_, vv) = spans_of(i, h)
+            head = cols[:, HEAD + h : HEAD + h + 1]
+            buf_q[:, at] = (gq[:, at] + head * nt(g[:, vv], state(at, dv))).astype(BF16)
+            copies.append(copy_out(i, h, 0))
             copies[-1].start()
-    for copy in copies:
-        copy.wait()
-
-
-def call(kernel, outs, ins, specs_in, specs_out, scratch=(), mib=20, flops=0, moved=0, aliases=None):
+        for copy in copies:
+            copy.wait()
+
+    @pl.when(jnp.logical_not(incoming))
+    def _():
+        copies = []
+        for i, h in enumerate(span):
+            (at, kk), (bv, vv) = spans_of(i, h)
+            tail = cols[:, TAIL_GATE + h : TAIL_GATE + h + 1]
+            arriving = state(at, dv)
+            buf_v[:, bv] = (gv[:, bv] + tail * nn(k[:, kk], arriving)).astype(BF16)
+            copies.append(copy_out(i, h, 2))
+            copies[-1].start()
+            buf_k[:, at] = (gk[:, at] + tail * nt(v[:, vv], arriving)).astype(BF16)
+            copies.append(copy_out(i, h, 1))
+            copies[-1].start()
+        for copy in copies:
+            copy.wait()
+
+
+def call(kernel, outs, ins, specs_in, specs_out, scratch=(), mib=20, aliases=None):
     return pl.pallas_call(
         kernel,
         out_shape=[jax.ShapeDtypeStruct(*o) for o in outs],
@@ -230,7 +270,7 @@
         scratch_shapes=list(scratch),
         input_output_aliases=aliases or {},
         compiler_params=pltpu.CompilerParams(vmem_limit_bytes=mib << 20),
-        cost_estimate=pl.CostEstimate(flops=flops // 1000000, bytes_accessed=moved // 1000000, transcendentals=0),
+        cost_estimate=pl.CostEstimate(flops=1000, bytes_accessed=1000, transcendentals=0),
     )(*ins)
 
 
@@ -256,31 +296,19 @@
     dk, dv = query_rows.shape[1] // heads, value_rows.shape[1] // heads
     scale = dk ** (-0.5)
     on_chip, adjacent, second = routes(lax.axis_size("ctx"))
-    unit = 2 * width * dk * dv
     spans, at = [], 0
     for m in CHUNKS:
         spans.append(tuple(range(at, at + m)))
         at += m
+    big = tuple(in_hbm(x) for x in (query_rows, key_rows, value_rows, out_grad))
+    small = tuple(in_hbm(x) for x in (log_forget.T, input_pre.T, doc_starts.reshape(1, width)))
+    mark = ((8, LANES), F32)
     payload = [((m * dk + EXTRA, dv), BF16) for m in CHUNKS]
     total = [((m * dk, dv), F32) for m in CHUNKS]
     send, keep, cols, rows, q, k, v, g = call(
         functools.partial(first_kernel, spans[0], heads, scale),
-        [
-            payload[0],
-            total[0],
-            ((width, ROWS), F32),
-            ((ROWS, width), F32),
-            (query_rows.shape, BF16),
-            (key_rows.shape, BF16),
-            (value_rows.shape, BF16),
-            (out_grad.shape, BF16),
-        ],
-        tuple(
-            in_hbm(x)
-            for x in (
-                log_forget.T, input_pre.T, doc_starts.reshape(1, width), query_rows, key_rows, value_rows, out_grad
-            )
-        ),
+        [payload[0], total[0], ((width, ROWS), F32), ((ROWS, width), F32)] + [(x.shape, BF16) for x in big],
+        small + big,
         [HBM] * 7,
         [VM] * 8,
         [
@@ -290,8 +318,6 @@
             pltpu.SemaphoreType.DMA((heads, 4)),
             pltpu.SemaphoreType.DMA((3,)),
         ],
-        flops=2 * unit * CHUNKS[0],
-        moved=12 << 20,
     )
     sends, keeps = [send], [keep]
     for i in range(1, len(CHUNKS)):
@@ -301,57 +327,75 @@
             (q, k, v, g, cols, rows),
             [VM] * 6,
             [VM] * 2,
-            flops=2 * unit * CHUNKS[i],
-            moved=4 << 20,
         )
         sends.append(send)
         keeps.append(keep)
     nears, firsts, seconds = [], [], []
     for i, span in enumerate(spans):
         near = swap(sends[i], on_chip)
-        if i + 1 < len(spans):
-            near, sends[i + 1] = lax.optimization_barrier((near, sends[i + 1]))
-        chip, token = call(
+        chip, token, *later = call(
             functools.partial(chip_kernel, span),
-            [payload[i], ((8, LANES), F32)],
-            (keeps[i], near, rows),
-            [VM] * 3,
-            [VM] * 2,
+            [payload[i], mark] + payload[i + 1 : i + 2],
+            (keeps[i], near, rows, *sends[i + 1 : i + 2]),
+            [VM] * (3 + len(sends[i + 1 : i + 2])),
+            [VM] * (2 + len(sends[i + 1 : i + 2])),
             mib=8,
-        )
+            aliases={3: 2} if i + 1 < len(spans) else None,
+        )
+        sends[i + 1 : i + 2] = later
+        firsts.append(swap(chip, adjacent))
         seconds.append(swap(chip, second))
-        firsts.append(swap(chip, adjacent))
         nears.append(near)
-    gq, gk, gv, token = call(
-        functools.partial(block_kernel, heads, scale),
-        [((width, heads * dk), F32), ((width, heads * dk), F32), ((width, heads * dv), F32), ((8, LANES), F32)],
-        (q, k, v, g, cols, rows, token),
-        [VM] * 7,
-        [VM] * 4,
-        flops=8 * unit * heads,
-        moved=14 << 20,
-    )
-    outs, token = (), token
+    blocks = []
     for i, span in enumerate(spans):
         m = len(span)
-        (far,) = call(functools.partial(far_kernel, m), [((m * dk, dv), BF16)], (seconds[i], firsts[i], token), [VM] * 3, [VM], mib=8)
+        *block, token = call(
+            functools.partial(block_kernel, span, heads, scale),
+            [((width, m * dk), F32), ((width, m * dk), F32), ((width, m * dv), F32), mark],
+            (q, k, v, g, cols, rows, token),
+            [VM] * 7,
+            [VM] * 4,
+        )
+        blocks.append(block)
+    outs = ()
+    shapes = [(query_rows.shape, BF16), (key_rows.shape, BF16), (value_rows.shape, BF16)]
+    for i, span in enumerate(spans):
+        m = len(span)
+        (far,) = call(
+            functools.partial(far_kernel, m),
+            [((m * dk, dv), BF16)],
+            (firsts[i], seconds[i], token),
+            [VM] * 3,
+            [VM],
+            mib=8,
+        )
         other = swap(far, on_chip)
-        *outs, token = call(
-            functools.partial(tail_kernel, span, heads),
-            [(query_rows.shape, BF16), (key_rows.shape, BF16), (value_rows.shape, BF16), ((8, LANES), F32)],
-            (nears[i], far, other, k, v, g, cols, gq, gk, gv) + tuple(in_hbm(x) for x in outs),
+        scratch = [
+            pltpu.VMEM((width, m * dk), BF16),
+            pltpu.VMEM((width, m * dk), BF16),
+            pltpu.VMEM((width, m * dv), BF16),
+            pltpu.SemaphoreType.DMA((m, 3)),
+        ]
+        outs = call(
+            functools.partial(far_tail_kernel, span),
+            shapes,
+            (far, k, v, g, cols, *blocks[i]) + tuple(in_hbm(x) for x in outs),
+            [VM] * 8 + [HBM] * len(outs),
+            [HBM] * 3,
+            scratch,
+            aliases={8 + j: j for j in range(len(outs))},
+        )
+        marks = int(i + 1 < len(spans))
+        outs = call(
+            functools.partial(near_tail_kernel, span, marks),
+            shapes + [mark] * marks,
+            (nears[i], other, far, k, v, g, cols, *blocks[i]) + tuple(in_hbm(x) for x in outs),
             [VM] * 10 + [HBM] * len(outs),
-            [HBM] * 3 + [VM],
-            [
-                pltpu.VMEM((width, m * dk), BF16),
-                pltpu.VMEM((width, m * dk), BF16),
-                pltpu.VMEM((width, m * dv), BF16),
-                pltpu.SemaphoreType.DMA((m, 3)),
-            ],
-            flops=3 * unit * m,
-            moved=(17 << 20) // len(spans),
+            [HBM] * 3 + [VM] * marks,
+            scratch,
             aliases={10 + j: j for j in range(len(outs))},
         )
+        token, outs = outs[-1], outs[:3]
     return tuple(outs)
 
 

time: 42.3 us -> 41.4 us (0.979)
  waiting for transfers between devices: 3.49 us -> 0.98 us
  Pallas kernels: 15.4 us -> 16.8 us
    ppermute x8, waiting for transfers between devices: 3.49 us -> 0.98 us  [swap(): return lax.ppermute(x, 'ctx', route)]
    pallas_call x9 -> x12, Pallas kernels: 15.4 us -> 16.8 us  [call(): pl.pallas_call(kernel, out_shape=[jax.ShapeDtypeStruct(*o) for o in outs]...]
  transfers between devices with their start and end apart: 8 -> 8, of which waited for: 3 -> 4; matrix products, arithmetic and copies ran while one was open for 0% -> 0% of each run, Pallas kernels for 21% -> 26%
where the time goes in v3:
time: 41.4 us; the launch traced here: 41.2 us
  starting transfers between devices  22.6 us (55%)
  Pallas kernels  16.8 us (41%)
  waiting for transfers between devices  0.98 us (2%)
  between operations  0.77 us (2%)
    ppermute x8, starting transfers between devices, swap(): return lax.ppermute(x, 'ctx', route)  22.6 us
    pallas_call x12, Pallas kernels, call(): pl.pallas_call(kernel, out_shape=[jax.ShapeDtypeStruct(*o) for o in outs]...  16.8 us
    ppermute x8, waiting for transfers between devices, swap(): return lax.ppermute(x, 'ctx', route)  0.98 us
  transfers between devices with their start and end apart: 8, of which 4 were waited for; matrix products, arithmetic and copies ran while one was open for 0% of the time, Pallas kernels for 26%

profile of v3, /device:TPU:0, one launch (start us, length us, event | category | flops | bytes accessed | tf_op | source)
XLA Modules:
  0.0 41.2 jit_solution(2001093255335966179)
XLA Ops:
  0.6 3.6 %shard_map.94 = (bf16[520,512]{1,0:T(8,128)(2,1)S(1)}, f32[512,512]{1,0:T(8,128)S(1)}, f32[512,32]{1,0:T(8,128)S(1)}, f32[32,512]{1,0:T(8,128)S(1)}, bf16[512,10...) custom-call(f32[4,512]{1,0:T(4,128)} %bitcast.3, ...), custom_call_target="tpu_custom_call" | custom-call | flops 1000 | bytes 1000 | tf_op jit(solution)/shard_map/pallas_call | solution.py:265
  4.3 0.5 %collective-permute-start = (bf16[520,512]{1,0:T(8,128)(2,1)S(1)}, bf16[520,512]{1,0:T(8,128)(2,1)S(1)}, u32[]{:S(2)}, u32[]{:S(2)}) collective-permute-start(bf16[520,512]{1,0:T(8,128)(2,1)S(1)} %get-tuple-element.36), channel_id=1, source_target_pairs={{0,1},{1,0},{2,3},{3,2},{4,5},{5,4},{6,7},{7,6},{8,9},{9,8},{10,11... | collective-permute-start | bytes 1597448 | tf_op jit(solution)/shard_map/ppermute | solution.py:282
  4.8 1.1 %shard_map.95 = (bf16[520,512]{1,0:T(8,128)(2,1)S(1)}, f32[512,512]{1,0:T(8,128)S(1)}) custom-call(bf16[512,1024]{1,0:T(8,128)(2,1)S(1)} %get-tuple-element.38.q, bf16[512,1024]{1,0:T(8,128)(2,1)S(1)} %get-tuple-element.39.k, bf16[512,2048]{1,0:T(8,128)(2,1)S(1)} %get-tuple-element.40.v, bf16[512,2048]{1,0:T(8,128)(2,1)S(1)} %get-tuple-element.41.g, ...), custom_call_target="tpu_custom_call" | custom-call | flops 1000 | bytes 1000 | tf_op jit(solution)/shard_map/pallas_call | solution.py:265
  6.0 0.4 collective-permute-done.near
  6.3 0.7 %shard_map.96 = (bf16[520,512]{1,0:T(8,128)(2,1)S(1)}, f32[8,128]{1,0:T(8,128)}, bf16[520,512]{1,0:T(8,128)(2,1)S(1)}) custom-call(f32[512,512]{1,0:T(8,128)S(1)} %get-tuple-element.35.keep, bf16[520,512]{1,0:T(8,128)(2,1)S(1)} %collective-permute-done.near, f32[32,512]{1,0:T(8,128)S(1)} %get-tuple-element.37.rows, ...), custom_call_target="tpu_custom_call", output_to_operand_aliasing={{2}: (3, {})} | custom-call | flops 1000 | bytes 1000 | tf_op jit(solution)/shard_map/pallas_call | solution.py:265
  7.0 0.4 collective-permute-start.1
  7.4 0.7 %collective-permute-start.4 = (bf16[520,512]{1,0:T(8,128)(2,1)S(1)}, bf16[520,512]{1,0:T(8,128)(2,1)S(1)}, u32[]{:S(2)}, u32[]{:S(2)}) collective-permute-start(bf16[520,512]{1,0:T(8,128)(2,1)S(1)} %get-tuple-element.47), channel_id=1, source_target_pairs={{1,2},{2,1},{3,4},{4,3},{5,6},{6,5},{7,8},{8,7},{9,10},{10,9},{11,... | collective-permute-start | bytes 1597448 | tf_op jit(solution)/shard_map/ppermute | solution.py:282
  8.1 0.7 %collective-permute-start.5 = (bf16[520,512]{1,0:T(8,128)(2,1)S(1)}, bf16[520,512]{1,0:T(8,128)(2,1)S(1)}, u32[]{:S(2)}, u32[]{:S(2)}) collective-permute-start(bf16[520,512]{1,0:T(8,128)(2,1)S(1)} %get-tuple-element.47), channel_id=1, source_target_pairs={{1,4},{4,1},{3,6},{6,3},{5,8},{8,5},{7,10},{10,7},{9,12},{12,9},{1... | collective-permute-start | bytes 1597448 | tf_op jit(solution)/shard_map/ppermute | solution.py:282
  8.8 0.2 collective-permute-done.1.near
  8.9 0.2 shard_map.97
  9.1 0.7 %collective-permute-start.2 = (bf16[520,512]{1,0:T(8,128)(2,1)S(1)}, bf16[520,512]{1,0:T(8,128)(2,1)S(1)}, u32[]{:S(2)}, u32[]{:S(2)}) collective-permute-start(bf16[520,512]{1,0:T(8,128)(2,1)S(1)} %get-tuple-element.46), channel_id=1, source_target_pairs={{1,2},{2,1},{3,4},{4,3},{5,6},{6,5},{7,8},{8,7},{9,10},{10,9},{11,... | collective-permute-start | bytes 1597448 | tf_op jit(solution)/shard_map/ppermute | solution.py:282
  9.8 0.7 %collective-permute-start.3 = (bf16[520,512]{1,0:T(8,128)(2,1)S(1)}, bf16[520,512]{1,0:T(8,128)(2,1)S(1)}, u32[]{:S(2)}, u32[]{:S(2)}) collective-permute-start(bf16[520,512]{1,0:T(8,128)(2,1)S(1)} %get-tuple-element.46), channel_id=1, source_target_pairs={{1,4},{4,1},{3,6},{6,3},{5,8},{8,5},{7,10},{10,7},{9,12},{12,9},{1... | collective-permute-start | bytes 1597448 | tf_op jit(solution)/shard_map/ppermute | solution.py:282
  10.5 2.3 %shard_map.98 = (f32[512,512]{1,0:T(8,128)S(1)}, f32[512,512]{1,0:T(8,128)S(1)}, f32[512,1024]{1,0:T(8,128)S(1)}, f32[8,128]{1,0:T(8,128)S(1)}) custom-call(bf16[512,1024]{1,0:T(8,128)(2,1)S(1)} %get-tuple-element.38.q, bf16[512,1024]{1,0:T(8,128)(2,1)S(1)} %get-tuple-element.39.k, bf16[512,2048]{1,0:T(8,128)(2,1)S(1)} %get-tuple-element.40.v, ...), custom_call_target="tpu_custom_call" | custom-call | flops 1000 | bytes 1000 | tf_op jit(solution)/shard_map/pallas_call | solution.py:265
  12.9 2.3 %shard_map.99 = (f32[512,512]{1,0:T(8,128)S(1)}, f32[512,512]{1,0:T(8,128)S(1)}, f32[512,1024]{1,0:T(8,128)S(1)}, f32[8,128]{1,0:T(8,128)S(1)}) custom-call(bf16[512,1024]{1,0:T(8,128)(2,1)S(1)} %get-tuple-element.38.q, bf16[512,1024]{1,0:T(8,128)(2,1)S(1)} %get-tuple-element.39.k, bf16[512,2048]{1,0:T(8,128)(2,1)S(1)} %get-tuple-element.40.v, ...), custom_call_target="tpu_custom_call" | custom-call | flops 1000 | bytes 1000 | tf_op jit(solution)/shard_map/pallas_call | solution.py:265
  15.2 0.0 collective-permute-done.4.first
  15.2 0.0 collective-permute-done.5.second
  15.2 0.2 shard_map.100.far.far_ready
  15.4 11.0 %collective-permute-start.6 = (bf16[512,512]{1,0:T(8,128)(2,1)S(1)}, bf16[512,512]{1,0:T(8,128)(2,1)S(1)}, u32[]{:S(2)}, u32[]{:S(2)}) collective-permute-start(bf16[512,512]{1,0:T(8,128)(2,1)S(1)} %shard_map.100.far.far_ready), channel_id=1, source_target_pairs={{0,1},{1,0},{2,3},{3,2},{4,5},{5,4},{6,7},{7,6},{8,9},{9,8},{10,11... | collective-permute-start | bytes 1572872 | tf_op jit(solution)/shard_map/ppermute | solution.py:282
  26.4 1.3 %shard_map.101 = (bf16[512,1024]{1,0:T(8,128)(2,1)}, bf16[512,1024]{1,0:T(8,128)(2,1)}, bf16[512,2048]{1,0:T(8,128)(2,1)}) custom-call(bf16[512,512]{1,0:T(8,128)(2,1)S(1)} %shard_map.100.far.far_ready, bf16[512,1024]{1,0:T(8,128)(2,1)S(1)} %get-tuple-element.39.k, bf16[512,2048]{1,0:T(8,128)(2,1)S(1)} %get-tuple-element.40.v, ...), custom_call_target="tpu_custom_call" | custom-call | flops 1000 | bytes 1000 | tf_op jit(solution)/shard_map/pallas_call | solution.py:265
  27.7 0.2 collective-permute-done.6.other
  27.9 1.8 %shard_map.102 = (bf16[512,1024]{1,0:T(8,128)(2,1)}, bf16[512,1024]{1,0:T(8,128)(2,1)}, bf16[512,2048]{1,0:T(8,128)(2,1)}, f32[8,128]{1,0:T(8,128)S(1)}) custom-call(bf16[520,512]{1,0:T(8,128)(2,1)S(1)} %collective-permute-done.near, ...), custom_call_target="tpu_custom_call", output_to_operand_aliasing={{0}: (10, {}), {1}: (11, {}), {2}: (12, {})} | custom-call | flops 1000 | bytes 1000 | tf_op jit(solution)/shard_map/pallas_call | solution.py:265
  29.7 0.0 collective-permute-done.2.first
  29.7 0.0 collective-permute-done.3.second
  29.7 0.2 shard_map.103.far.far_ready
  29.9 8.0 %collective-permute-start.7 = (bf16[512,512]{1,0:T(8,128)(2,1)S(1)}, bf16[512,512]{1,0:T(8,128)(2,1)S(1)}, u32[]{:S(2)}, u32[]{:S(2)}) collective-permute-start(bf16[512,512]{1,0:T(8,128)(2,1)S(1)} %shard_map.103.far.far_ready), channel_id=1, source_target_pairs={{0,1},{1,0},{2,3},{3,2},{4,5},{5,4},{6,7},{7,6},{8,9},{9,8},{10,11... | collective-permute-start | bytes 1572872 | tf_op jit(solution)/shard_map/ppermute | solution.py:282
  37.9 1.3 %shard_map.104 = (bf16[512,1024]{1,0:T(8,128)(2,1)}, bf16[512,1024]{1,0:T(8,128)(2,1)}, bf16[512,2048]{1,0:T(8,128)(2,1)}) custom-call(bf16[512,512]{1,0:T(8,128)(2,1)S(1)} %shard_map.103.far.far_ready, bf16[512,1024]{1,0:T(8,128)(2,1)S(1)} %get-tuple-element.39.k, ...), custom_call_target="tpu_custom_call", output_to_operand_aliasing={{0}: (8, {}), {1}: (9, {}), {2}: (10, {})} | custom-call | flops 1000 | bytes 1000 | tf_op jit(solution)/shard_map/pallas_call | solution.py:265
  39.2 0.2 collective-permute-done.7.other
  39.4 1.8 %shard_map.105 = (bf16[512,1024]{1,0:T(8,128)(2,1)}, bf16[512,1024]{1,0:T(8,128)(2,1)}, bf16[512,2048]{1,0:T(8,128)(2,1)}) custom-call(bf16[520,512]{1,0:T(8,128)(2,1)S(1)} %collective-permute-done.1.near, bf16[512,512]{1,0:T(8,128)(2,1)S(1)} %collective-permute-done.7.other, ...), custom_call_target="tpu_custom_call", output_to_operand_aliasing={{0}: (10, {}), {1}: (11, {}), {2}: (12, {})} | custom-call | flops 1000 | bytes 1000 | tf_op jit(solution)/shard_map/pallas_call | solution.py:265
Async XLA Ops:
  4.3 2.1 %collective-permute-start = (bf16[520,512]{1,0:T(8,128)(2,1)S(1)}, bf16[520,512]{1,0:T(8,128)(2,1)S(1)}, u32[]{:S(2)}, u32[]{:S(2)}) collective-permute-start(bf16[520,512]{1,0:T(8,128)(2,1)S(1)} %get-tuple-element.36), channel_id=1, source_target_pairs={{0,1},{1,0},{2,3},{3,2},{4,5},{5,4},{6,7},{7,6},{8,9},{9,8},{10,11... | collective-permute-start | bytes 1597448 | tf_op jit(solution)/shard_map/ppermute | solution.py:282
  7.0 1.9 %collective-permute-start.1 = (bf16[520,512]{1,0:T(8,128)(2,1)S(1)}, bf16[520,512]{1,0:T(8,128)(2,1)S(1)}, u32[]{:S(2)}, u32[]{:S(2)}) collective-permute-start(bf16[520,512]{1,0:T(8,128)(2,1)S(1)} %get-tuple-element.44), channel_id=1, source_target_pairs={{0,1},{1,0},{2,3},{3,2},{4,5},{5,4},{6,7},{7,6},{8,9},{9,8},{10,11... | collective-permute-start | bytes 1597448 | tf_op jit(solution)/shard_map/ppermute | solution.py:282
  7.4 7.8 %collective-permute-start.4 = (bf16[520,512]{1,0:T(8,128)(2,1)S(1)}, bf16[520,512]{1,0:T(8,128)(2,1)S(1)}, u32[]{:S(2)}, u32[]{:S(2)}) collective-permute-start(bf16[520,512]{1,0:T(8,128)(2,1)S(1)} %get-tuple-element.47), channel_id=1, source_target_pairs={{1,2},{2,1},{3,4},{4,3},{5,6},{6,5},{7,8},{8,7},{9,10},{10,9},{11,... | collective-permute-start | bytes 1597448 | tf_op jit(solution)/shard_map/ppermute | solution.py:282
  8.1 7.1 %collective-permute-start.5 = (bf16[520,512]{1,0:T(8,128)(2,1)S(1)}, bf16[520,512]{1,0:T(8,128)(2,1)S(1)}, u32[]{:S(2)}, u32[]{:S(2)}) collective-permute-start(bf16[520,512]{1,0:T(8,128)(2,1)S(1)} %get-tuple-element.47), channel_id=1, source_target_pairs={{1,4},{4,1},{3,6},{6,3},{5,8},{8,5},{7,10},{10,7},{9,12},{12,9},{1... | collective-permute-start | bytes 1597448 | tf_op jit(solution)/shard_map/ppermute | solution.py:282
  9.1 20.6 %collective-permute-start.2 = (bf16[520,512]{1,0:T(8,128)(2,1)S(1)}, bf16[520,512]{1,0:T(8,128)(2,1)S(1)}, u32[]{:S(2)}, u32[]{:S(2)}) collective-permute-start(bf16[520,512]{1,0:T(8,128)(2,1)S(1)} %get-tuple-element.46), channel_id=1, source_target_pairs={{1,2},{2,1},{3,4},{4,3},{5,6},{6,5},{7,8},{8,7},{9,10},{10,9},{11,... | collective-permute-start | bytes 1597448 | tf_op jit(solution)/shard_map/ppermute | solution.py:282
  9.8 19.9 %collective-permute-start.3 = (bf16[520,512]{1,0:T(8,128)(2,1)S(1)}, bf16[520,512]{1,0:T(8,128)(2,1)S(1)}, u32[]{:S(2)}, u32[]{:S(2)}) collective-permute-start(bf16[520,512]{1,0:T(8,128)(2,1)S(1)} %get-tuple-element.46), channel_id=1, source_target_pairs={{1,4},{4,1},{3,6},{6,3},{5,8},{8,5},{7,10},{10,7},{9,12},{12,9},{1... | collective-permute-start | bytes 1597448 | tf_op jit(solution)/shard_map/ppermute | solution.py:282
  15.4 12.5 %collective-permute-start.6 = (bf16[512,512]{1,0:T(8,128)(2,1)S(1)}, bf16[512,512]{1,0:T(8,128)(2,1)S(1)}, u32[]{:S(2)}, u32[]{:S(2)}) collective-permute-start(bf16[512,512]{1,0:T(8,128)(2,1)S(1)} %shard_map.100.far.far_ready), channel_id=1, source_target_pairs={{0,1},{1,0},{2,3},{3,2},{4,5},{5,4},{6,7},{7,6},{8,9},{9,8},{10,11... | collective-permute-start | bytes 1572872 | tf_op jit(solution)/shard_map/ppermute | solution.py:282
  29.9 9.5 %collective-permute-start.7 = (bf16[512,512]{1,0:T(8,128)(2,1)S(1)}, bf16[512,512]{1,0:T(8,128)(2,1)S(1)}, u32[]{:S(2)}, u32[]{:S(2)}) collective-permute-start(bf16[512,512]{1,0:T(8,128)(2,1)S(1)} %shard_map.103.far.far_ready), channel_id=1, source_target_pairs={{0,1},{1,0},{2,3},{3,2},{4,5},{5,4},{6,7},{7,6},{8,9},{9,8},{10,11... | collective-permute-start | bytes 1572872 | tf_op jit(solution)/shard_map/ppermute | solution.py:282

commit v4 on v3

--- a/solution.py
+++ b/solution.py
@@ -137,7 +137,8 @@
 
 
 def chip_kernel(span, keep, near, rows, *refs):
-    out, token = refs[-2:] if len(refs) == 2 else refs[1:3]
+    through = (len(refs) - 3) // 2
+    out, again, token = refs[through : through + 3]
     token[...] = jnp.zeros_like(token)
     n, width = keep.shape
     m = len(span)
@@ -147,18 +148,25 @@
         at = slice(i * dk, (i + 1) * dk)
         out[at, :] = (keep[at, :] + wide_row(own, i, width) * near[at, :].astype(F32)).astype(BF16)
     out[n:, :] = gain_rows(own * gain_of(near, n, m), width)
-
-
-def far_kernel(m, first, second, token, out):
+    again[...] = out[...]
+
+
+def through_kernel(after, x, token, out):
+    del after, x, token, out
+
+
+def far_kernel(m, second, first, relayed, token, out):
     n, width = out.shape
     dk = n // m
-    gain = gain_of(first, n, m)
+    gain = gain_of(first, n, m) + gain_of(relayed, n, m)
     for i in range(m):
         at = slice(i * dk, (i + 1) * dk)
-        out[at, :] = (first[at, :].astype(F32) + wide_row(gain, i, width) * second[at, :].astype(F32)).astype(BF16)
-
-
-def block_kernel(span, heads, scale, q, k, v, g, cols, rows, ready, gq, gk, gv, token):
+        adjacent = first[at, :].astype(F32) + relayed[at, :].astype(F32)
+        out[at, :] = (adjacent + wide_row(gain, i, width) * second[at, :].astype(F32)).astype(BF16)
+
+
+def block_kernel(span, heads, scale, q, k, v, g, cols, rows, ready, *refs):
+    gq, gk, gv, token = refs[:4] if len(refs) == 4 else refs[1:5]
     token[...] = jnp.zeros_like(token)
     width = q.shape[0]
     half = width // 2
@@ -286,16 +294,17 @@
     chips = size // 2
     both = lambda pairs: [p for a, b in pairs for p in ((a, b), (b, a))]
     on_chip = both([(2 * c, 2 * c + 1) for c in range(chips)])
-    adjacent = both([(2 * c + 1, 2 * c + 2) for c in range(chips - 1)])
+    mates = both([(2 * c + 1, 2 * c + 2) for c in range(0, chips, 2)])
     second = both([(2 * c + 1, 2 * c + 4) for c in range(chips - 2)])
-    return on_chip, adjacent, second
+    relay = [p for c in range(0, chips, 2) for p in ((2 * c + 2, 2 * c), (2 * c + 1, 2 * c + 3))]
+    return on_chip, mates, second, relay
 
 
 def body(query_rows, key_rows, value_rows, out_grad, log_forget, input_pre, doc_starts):
     width, heads = log_forget.shape
     dk, dv = query_rows.shape[1] // heads, value_rows.shape[1] // heads
     scale = dk ** (-0.5)
-    on_chip, adjacent, second = routes(lax.axis_size("ctx"))
+    on_chip, mates, second, relay = routes(lax.axis_size("ctx"))
     spans, at = [], 0
     for m in CHUNKS:
         spans.append(tuple(range(at, at + m)))
@@ -330,33 +339,51 @@
         )
         sends.append(send)
         keeps.append(keep)
-    nears, firsts, seconds = [], [], []
+    nears, firsts, seconds, blocks, relayed = [], [], [], [], []
+    passed = ()
     for i, span in enumerate(spans):
         near = swap(sends[i], on_chip)
-        chip, token, *later = call(
+        passed = passed + tuple(sends[i + 1 : i + 2])
+        count = len(passed)
+        chip, copy, token, *passed = call(
             functools.partial(chip_kernel, span),
-            [payload[i], mark] + payload[i + 1 : i + 2],
-            (keeps[i], near, rows, *sends[i + 1 : i + 2]),
-            [VM] * (3 + len(sends[i + 1 : i + 2])),
-            [VM] * (2 + len(sends[i + 1 : i + 2])),
+            [payload[i]] * 2 + [mark] + [(x.shape, BF16) for x in passed],
+            (keeps[i], near, rows, *passed),
+            [VM] * (3 + count),
+            [VM] * (3 + count),
             mib=8,
-            aliases={3: 2} if i + 1 < len(spans) else None,
-        )
-        sends[i + 1 : i + 2] = later
-        firsts.append(swap(chip, adjacent))
-        seconds.append(swap(chip, second))
+            aliases={3 + j: 3 + j for j in range(count)},
+        )
+        if i > 0:
+            seconds.append(swap(passed[0], second))
+        if i + 1 < len(spans):
+            sends[i + 1] = passed[-1]
+        passed = (copy,)
+        firsts.append(swap(chip, mates))
         nears.append(near)
-    blocks = []
+    seconds.append(swap(copy, second))
+    passed = ()
     for i, span in enumerate(spans):
         m = len(span)
-        *block, token = call(
+        count = len(passed)
+        *block, token, = call(
             functools.partial(block_kernel, span, heads, scale),
-            [((width, m * dk), F32), ((width, m * dk), F32), ((width, m * dv), F32), mark],
-            (q, k, v, g, cols, rows, token),
-            [VM] * 7,
-            [VM] * 4,
-        )
+            [((width, m * dk), F32), ((width, m * dk), F32), ((width, m * dv), F32), mark]
+            + [(x.shape, BF16) for x in passed],
+            (q, k, v, g, cols, rows, token, *passed),
+            [VM] * (7 + count),
+            [VM] * (4 + count),
+            aliases={7 + j: 4 + j for j in range(count)},
+        )
+        if count:
+            seconds.append(swap(token, second))
+            *block, token = block
+            passed = ()
         blocks.append(block)
+        (seconds[i],) = call(
+            through_kernel, payload[i : i + 1], (firsts[i], seconds[i], token), [VM] * 3, [VM], mib=8, aliases={1: 0}
+        )
+        relayed.append(swap(seconds[i], relay))
     outs = ()
     shapes = [(query_rows.shape, BF16), (key_rows.shape, BF16), (value_rows.shape, BF16)]
     for i, span in enumerate(spans):
@@ -364,8 +391,8 @@
         (far,) = call(
             functools.partial(far_kernel, m),
             [((m * dk, dv), BF16)],
-            (firsts[i], seconds[i], token),
-            [VM] * 3,
+            (seconds[i], firsts[i], relayed[i], token),
+            [VM] * 4,
             [VM],
             mib=8,
         )

time: 41.4 us -> 41.1 us (level)
  starting transfers between devices: 22.6 us -> 8.14 us
  waiting for transfers between devices: 0.98 us -> 15 us
    ppermute x8 -> x10, starting transfers between devices: 22.6 us -> 8.14 us  [swap(): return lax.ppermute(x, 'ctx', route)]
    ppermute x8 -> x10, waiting for transfers between devices: 0.98 us -> 15 us  [swap(): return lax.ppermute(x, 'ctx', route)]
    pallas_call x12 -> x14, Pallas kernels: 16.8 us -> 17 us  [call(): pl.pallas_call(kernel, out_shape=[jax.ShapeDtypeStruct(*o) for o in outs]...]
  transfers between devices with their start and end apart: 8 -> 10, of which waited for: 4 -> 6; matrix products, arithmetic and copies ran while one was open for 0% -> 0% of each run, Pallas kernels for 26% -> 26%
where the time goes in v4:
time: 41.1 us; the launch traced here: 40.9 us
  Pallas kernels  17 us (41%)
  waiting for transfers between devices  15 us (36%)
  starting transfers between devices  8.14 us (20%)
  between operations  0.8 us (2%)
    pallas_call x14, Pallas kernels, call(): pl.pallas_call(kernel, out_shape=[jax.ShapeDtypeStruct(*o) for o in outs]...  17 us
    ppermute x10, waiting for transfers between devices, swap(): return lax.ppermute(x, 'ctx', route)  15 us
    ppermute x10, starting transfers between devices, swap(): return lax.ppermute(x, 'ctx', route)  8.14 us
  transfers between devices with their start and end apart: 10, of which 6 were waited for; matrix products, arithmetic and copies ran while one was open for 0% of the time, Pallas kernels for 26%

profile of v4, /device:TPU:0, one launch (start us, length us, event | category | flops | bytes accessed | tf_op | source)
XLA Modules:
  0.0 40.9 jit_solution(12158714654351517424)
XLA Ops:
  0.6 3.6 %shard_map.94 = (bf16[520,512]{1,0:T(8,128)(2,1)S(1)}, f32[512,512]{1,0:T(8,128)S(1)}, f32[512,32]{1,0:T(8,128)S(1)}, f32[32,512]{1,0:T(8,128)S(1)}, bf16[512,10...) custom-call(f32[4,512]{1,0:T(4,128)} %bitcast.3, ...), custom_call_target="tpu_custom_call" | custom-call | flops 1000 | bytes 1000 | tf_op jit(solution)/shard_map/pallas_call | solution.py:273
  4.3 0.5 %collective-permute-start = (bf16[520,512]{1,0:T(8,128)(2,1)S(1)}, bf16[520,512]{1,0:T(8,128)(2,1)S(1)}, u32[]{:S(2)}, u32[]{:S(2)}) collective-permute-start(bf16[520,512]{1,0:T(8,128)(2,1)S(1)} %get-tuple-element.39), channel_id=1, source_target_pairs={{0,1},{1,0},{2,3},{3,2},{4,5},{5,4},{6,7},{7,6},{8,9},{9,8},{10,11... | collective-permute-start | bytes 1597448 | tf_op jit(solution)/shard_map/ppermute | solution.py:290
  4.8 1.1 %shard_map.95 = (bf16[520,512]{1,0:T(8,128)(2,1)S(1)}, f32[512,512]{1,0:T(8,128)S(1)}) custom-call(bf16[512,1024]{1,0:T(8,128)(2,1)S(1)} %get-tuple-element.41.q, bf16[512,1024]{1,0:T(8,128)(2,1)S(1)} %get-tuple-element.42.k, bf16[512,2048]{1,0:T(8,128)(2,1)S(1)} %get-tuple-element.43.v, bf16[512,2048]{1,0:T(8,128)(2,1)S(1)} %get-tuple-element.44.g, ...), custom_call_target="tpu_custom_call" | custom-call | flops 1000 | bytes 1000 | tf_op jit(solution)/shard_map/pallas_call | solution.py:273
  6.0 0.4 collective-permute-done.near
  6.3 0.6 %shard_map.96 = (bf16[520,512]{1,0:T(8,128)(2,1)S(1)}, bf16[520,512]{1,0:T(8,128)(2,1)S(1)}, f32[8,128]{1,0:T(8,128)}, bf16[520,512]{1,0:T(8,128)(2,1)S(1)}) custom-call(f32[512,512]{1,0:T(8,128)S(1)} %get-tuple-element.38.keep, bf16[520,512]{1,0:T(8,128)(2,1)S(1)} %collective-permute-done.near, ...), custom_call_target="tpu_custom_call", output_to_operand_aliasing={{3}: (3, {})} | custom-call | flops 1000 | bytes 1000 | tf_op jit(solution)/shard_map/pallas_call | solution.py:273
  6.9 0.4 collective-permute-start.1
  7.3 0.7 %collective-permute-start.5 = (bf16[520,512]{1,0:T(8,128)(2,1)S(1)}, bf16[520,512]{1,0:T(8,128)(2,1)S(1)}, u32[]{:S(2)}, u32[]{:S(2)}) collective-permute-start(bf16[520,512]{1,0:T(8,128)(2,1)S(1)} %get-tuple-element.55), channel_id=1, source_target_pairs={{1,2},{2,1},{5,6},{6,5},{9,10},{10,9},{13,14},{14,13},{17,18},{18,... | collective-permute-start | bytes 1597448 | tf_op jit(solution)/shard_map/ppermute | solution.py:290
  8.0 0.9 %collective-permute-done.1.near = bf16[520,512]{1,0:T(8,128)(2,1)S(1)} collective-permute-done((bf16[520,512]{1,0:T(8,128)(2,1)S(1)}, bf16[520,512]{1,0:T(8,128)(2,1)S(1)}, u32[]{:S(2)}, u32[]{:S(2)}) %collective-permute-start.1) | collective-permute-done | bytes 532512 | tf_op jit(solution)/shard_map/ppermute | solution.py:290
  8.9 0.3 shard_map.97
  9.1 0.7 %collective-permute-start.6 = (bf16[520,512]{1,0:T(8,128)(2,1)S(1)}, bf16[520,512]{1,0:T(8,128)(2,1)S(1)}, u32[]{:S(2)}, u32[]{:S(2)}) collective-permute-start(bf16[520,512]{1,0:T(8,128)(2,1)S(1)} %get-tuple-element.56), channel_id=1, source_target_pairs={{1,4},{4,1},{3,6},{6,3},{5,8},{8,5},{7,10},{10,7},{9,12},{12,9},{1... | collective-permute-start | bytes 1597448 | tf_op jit(solution)/shard_map/ppermute | solution.py:290
  9.8 0.7 %collective-permute-start.2 = (bf16[520,512]{1,0:T(8,128)(2,1)S(1)}, bf16[520,512]{1,0:T(8,128)(2,1)S(1)}, u32[]{:S(2)}, u32[]{:S(2)}) collective-permute-start(bf16[520,512]{1,0:T(8,128)(2,1)S(1)} %get-tuple-element.50), channel_id=1, source_target_pairs={{1,2},{2,1},{5,6},{6,5},{9,10},{10,9},{13,14},{14,13},{17,18},{18,... | collective-permute-start | bytes 1597448 | tf_op jit(solution)/shard_map/ppermute | solution.py:290
  10.5 0.7 %collective-permute-start.3 = (bf16[520,512]{1,0:T(8,128)(2,1)S(1)}, bf16[520,512]{1,0:T(8,128)(2,1)S(1)}, u32[]{:S(2)}, u32[]{:S(2)}) collective-permute-start(bf16[520,512]{1,0:T(8,128)(2,1)S(1)} %get-tuple-element.51), channel_id=1, source_target_pairs={{1,4},{4,1},{3,6},{6,3},{5,8},{8,5},{7,10},{10,7},{9,12},{12,9},{1... | collective-permute-start | bytes 1597448 | tf_op jit(solution)/shard_map/ppermute | solution.py:290
  11.2 2.3 %shard_map.98 = (f32[512,512]{1,0:T(8,128)S(1)}, f32[512,512]{1,0:T(8,128)S(1)}, f32[512,1024]{1,0:T(8,128)S(1)}, f32[8,128]{1,0:T(8,128)S(1)}) custom-call(bf16[512,1024]{1,0:T(8,128)(2,1)S(1)} %get-tuple-element.41.q, bf16[512,1024]{1,0:T(8,128)(2,1)S(1)} %get-tuple-element.42.k, bf16[512,2048]{1,0:T(8,128)(2,1)S(1)} %get-tuple-element.43.v, ...), custom_call_target="tpu_custom_call" | custom-call | flops 1000 | bytes 1000 | tf_op jit(solution)/shard_map/pallas_call | solution.py:273
  13.6 0.0 collective-permute-done.5.after.first
  13.6 0.0 collective-permute-done.6.x
  13.6 1.3 %collective-permute-start.7 = (bf16[520,512]{1,0:T(8,128)(2,1)S(1)}, bf16[520,512]{1,0:T(8,128)(2,1)S(1)}, u32[]{:S(2)}, u32[]{:S(2)}) collective-permute-start(bf16[520,512]{1,0:T(8,128)(2,1)S(1)} %shard_map.101.second), channel_id=1, source_target_pairs={{2,0},{1,3},{6,4},{5,7},{10,8},{9,11},{14,12},{13,15},{18,16},{17,... | collective-permute-start | bytes 1597448 | tf_op jit(solution)/shard_map/ppermute | solution.py:290
  14.9 2.3 %shard_map.99 = (f32[512,512]{1,0:T(8,128)S(1)}, f32[512,512]{1,0:T(8,128)S(1)}, f32[512,1024]{1,0:T(8,128)S(1)}, f32[8,128]{1,0:T(8,128)S(1)}) custom-call(bf16[512,1024]{1,0:T(8,128)(2,1)S(1)} %get-tuple-element.41.q, bf16[512,1024]{1,0:T(8,128)(2,1)S(1)} %get-tuple-element.42.k, bf16[512,2048]{1,0:T(8,128)(2,1)S(1)} %get-tuple-element.43.v, ...), custom_call_target="tpu_custom_call" | custom-call | flops 1000 | bytes 1000 | tf_op jit(solution)/shard_map/pallas_call | solution.py:273
  17.3 0.0 collective-permute-done.2.after.first
  17.3 0.0 collective-permute-done.3.x
  17.3 1.3 %collective-permute-start.4 = (bf16[520,512]{1,0:T(8,128)(2,1)S(1)}, bf16[520,512]{1,0:T(8,128)(2,1)S(1)}, u32[]{:S(2)}, u32[]{:S(2)}) collective-permute-start(bf16[520,512]{1,0:T(8,128)(2,1)S(1)} %shard_map.100.second), channel_id=1, source_target_pairs={{2,0},{1,3},{6,4},{5,7},{10,8},{9,11},{14,12},{13,15},{18,16},{17,... | collective-permute-start | bytes 1597448 | tf_op jit(solution)/shard_map/ppermute | solution.py:290
  18.6 12.1 %collective-permute-done.7.relayed = bf16[520,512]{1,0:T(8,128)(2,1)S(1)} collective-permute-done((bf16[520,512]{1,0:T(8,128)(2,1)S(1)}, bf16[520,512]{1,0:T(8,128)(2,1)S(1)}, u32[]{:S(2)}, u32[]{:S(2)}) %collective-permute-start.7) | collective-permute-done | bytes 532512 | tf_op jit(solution)/shard_map/ppermute | solution.py:290
  30.7 0.2 shard_map.102.far.far_ready
  30.9 0.9 %collective-permute-start.8 = (bf16[512,512]{1,0:T(8,128)(2,1)S(1)}, bf16[512,512]{1,0:T(8,128)(2,1)S(1)}, u32[]{:S(2)}, u32[]{:S(2)}) collective-permute-start(bf16[512,512]{1,0:T(8,128)(2,1)S(1)} %shard_map.102.far.far_ready), channel_id=1, source_target_pairs={{0,1},{1,0},{2,3},{3,2},{4,5},{5,4},{6,7},{7,6},{8,9},{9,8},{10,11... | collective-permute-start | bytes 1572872 | tf_op jit(solution)/shard_map/ppermute | solution.py:290
  31.8 1.3 %shard_map.103 = (bf16[512,1024]{1,0:T(8,128)(2,1)}, bf16[512,1024]{1,0:T(8,128)(2,1)}, bf16[512,2048]{1,0:T(8,128)(2,1)}) custom-call(bf16[512,512]{1,0:T(8,128)(2,1)S(1)} %shard_map.102.far.far_ready, bf16[512,1024]{1,0:T(8,128)(2,1)S(1)} %get-tuple-element.42.k, bf16[512,2048]{1,0:T(8,128)(2,1)S(1)} %get-tuple-element.43.v, ...), custom_call_target="tpu_custom_call" | custom-call | flops 1000 | bytes 1000 | tf_op jit(solution)/shard_map/pallas_call | solution.py:273
  33.2 0.2 collective-permute-done.8.other
  33.4 1.8 %shard_map.104 = (bf16[512,1024]{1,0:T(8,128)(2,1)}, bf16[512,1024]{1,0:T(8,128)(2,1)}, bf16[512,2048]{1,0:T(8,128)(2,1)}, f32[8,128]{1,0:T(8,128)S(1)}) custom-call(bf16[520,512]{1,0:T(8,128)(2,1)S(1)} %collective-permute-done.near, ...), custom_call_target="tpu_custom_call", output_to_operand_aliasing={{0}: (10, {}), {1}: (11, {}), {2}: (12, {})} | custom-call | flops 1000 | bytes 1000 | tf_op jit(solution)/shard_map/pallas_call | solution.py:273
  35.2 1.2 %collective-permute-done.4.relayed = bf16[520,512]{1,0:T(8,128)(2,1)S(1)} collective-permute-done((bf16[520,512]{1,0:T(8,128)(2,1)S(1)}, bf16[520,512]{1,0:T(8,128)(2,1)S(1)}, u32[]{:S(2)}, u32[]{:S(2)}) %collective-permute-start.4) | collective-permute-done | bytes 532512 | tf_op jit(solution)/shard_map/ppermute | solution.py:290
  36.4 0.2 shard_map.105.far.far_ready
  36.6 0.9 %collective-permute-start.9 = (bf16[512,512]{1,0:T(8,128)(2,1)S(1)}, bf16[512,512]{1,0:T(8,128)(2,1)S(1)}, u32[]{:S(2)}, u32[]{:S(2)}) collective-permute-start(bf16[512,512]{1,0:T(8,128)(2,1)S(1)} %shard_map.105.far.far_ready), channel_id=1, source_target_pairs={{0,1},{1,0},{2,3},{3,2},{4,5},{5,4},{6,7},{7,6},{8,9},{9,8},{10,11... | collective-permute-start | bytes 1572872 | tf_op jit(solution)/shard_map/ppermute | solution.py:290
  37.6 1.3 %shard_map.106 = (bf16[512,1024]{1,0:T(8,128)(2,1)}, bf16[512,1024]{1,0:T(8,128)(2,1)}, bf16[512,2048]{1,0:T(8,128)(2,1)}) custom-call(bf16[512,512]{1,0:T(8,128)(2,1)S(1)} %shard_map.105.far.far_ready, bf16[512,1024]{1,0:T(8,128)(2,1)S(1)} %get-tuple-element.42.k, ...), custom_call_target="tpu_custom_call", output_to_operand_aliasing={{0}: (8, {}), {1}: (9, {}), {2}: (10, {})} | custom-call | flops 1000 | bytes 1000 | tf_op jit(solution)/shard_map/pallas_call | solution.py:273
  38.9 0.2 collective-permute-done.9.other
  39.1 1.8 %shard_map.107 = (bf16[512,1024]{1,0:T(8,128)(2,1)}, bf16[512,1024]{1,0:T(8,128)(2,1)}, bf16[512,2048]{1,0:T(8,128)(2,1)}) custom-call(bf16[520,512]{1,0:T(8,128)(2,1)S(1)} %collective-permute-done.1.near, bf16[512,512]{1,0:T(8,128)(2,1)S(1)} %collective-permute-done.9.other, ...), custom_call_target="tpu_custom_call", output_to_operand_aliasing={{0}: (10, {}), {1}: (11, {}), {2}: (12, {})} | custom-call | flops 1000 | bytes 1000 | tf_op jit(solution)/shard_map/pallas_call | solution.py:273
  (2 shorter events, 0.0 us)
Async XLA Ops:
  4.3 2.1 %collective-permute-start = (bf16[520,512]{1,0:T(8,128)(2,1)S(1)}, bf16[520,512]{1,0:T(8,128)(2,1)S(1)}, u32[]{:S(2)}, u32[]{:S(2)}) collective-permute-start(bf16[520,512]{1,0:T(8,128)(2,1)S(1)} %get-tuple-element.39), channel_id=1, source_target_pairs={{0,1},{1,0},{2,3},{3,2},{4,5},{5,4},{6,7},{7,6},{8,9},{9,8},{10,11... | collective-permute-start | bytes 1597448 | tf_op jit(solution)/shard_map/ppermute | solution.py:290
  6.9 1.9 %collective-permute-start.1 = (bf16[520,512]{1,0:T(8,128)(2,1)S(1)}, bf16[520,512]{1,0:T(8,128)(2,1)S(1)}, u32[]{:S(2)}, u32[]{:S(2)}) collective-permute-start(bf16[520,512]{1,0:T(8,128)(2,1)S(1)} %get-tuple-element.47), channel_id=1, source_target_pairs={{0,1},{1,0},{2,3},{3,2},{4,5},{5,4},{6,7},{7,6},{8,9},{9,8},{10,11... | collective-permute-start | bytes 1597448 | tf_op jit(solution)/shard_map/ppermute | solution.py:290
  7.3 6.3 %collective-permute-start.5 = (bf16[520,512]{1,0:T(8,128)(2,1)S(1)}, bf16[520,512]{1,0:T(8,128)(2,1)S(1)}, u32[]{:S(2)}, u32[]{:S(2)}) collective-permute-start(bf16[520,512]{1,0:T(8,128)(2,1)S(1)} %get-tuple-element.55), channel_id=1, source_target_pairs={{1,2},{2,1},{5,6},{6,5},{9,10},{10,9},{13,14},{14,13},{17,18},{18,... | collective-permute-start | bytes 1597448 | tf_op jit(solution)/shard_map/ppermute | solution.py:290
  9.1 4.5 %collective-permute-start.6 = (bf16[520,512]{1,0:T(8,128)(2,1)S(1)}, bf16[520,512]{1,0:T(8,128)(2,1)S(1)}, u32[]{:S(2)}, u32[]{:S(2)}) collective-permute-start(bf16[520,512]{1,0:T(8,128)(2,1)S(1)} %get-tuple-element.56), channel_id=1, source_target_pairs={{1,4},{4,1},{3,6},{6,3},{5,8},{8,5},{7,10},{10,7},{9,12},{12,9},{1... | collective-permute-start | bytes 1597448 | tf_op jit(solution)/shard_map/ppermute | solution.py:290
  9.8 7.4 %collective-permute-start.2 = (bf16[520,512]{1,0:T(8,128)(2,1)S(1)}, bf16[520,512]{1,0:T(8,128)(2,1)S(1)}, u32[]{:S(2)}, u32[]{:S(2)}) collective-permute-start(bf16[520,512]{1,0:T(8,128)(2,1)S(1)} %get-tuple-element.50), channel_id=1, source_target_pairs={{1,2},{2,1},{5,6},{6,5},{9,10},{10,9},{13,14},{14,13},{17,18},{18,... | collective-permute-start | bytes 1597448 | tf_op jit(solution)/shard_map/ppermute | solution.py:290
  10.5 6.7 %collective-permute-start.3 = (bf16[520,512]{1,0:T(8,128)(2,1)S(1)}, bf16[520,512]{1,0:T(8,128)(2,1)S(1)}, u32[]{:S(2)}, u32[]{:S(2)}) collective-permute-start(bf16[520,512]{1,0:T(8,128)(2,1)S(1)} %get-tuple-element.51), channel_id=1, source_target_pairs={{1,4},{4,1},{3,6},{6,3},{5,8},{8,5},{7,10},{10,7},{9,12},{12,9},{1... | collective-permute-start | bytes 1597448 | tf_op jit(solution)/shard_map/ppermute | solution.py:290
  13.6 17.1 %collective-permute-start.7 = (bf16[520,512]{1,0:T(8,128)(2,1)S(1)}, bf16[520,512]{1,0:T(8,128)(2,1)S(1)}, u32[]{:S(2)}, u32[]{:S(2)}) collective-permute-start(bf16[520,512]{1,0:T(8,128)(2,1)S(1)} %shard_map.101.second), channel_id=1, source_target_pairs={{2,0},{1,3},{6,4},{5,7},{10,8},{9,11},{14,12},{13,15},{18,16},{17,... | collective-permute-start | bytes 1597448 | tf_op jit(solution)/shard_map/ppermute | solution.py:290
  17.3 19.1 %collective-permute-start.4 = (bf16[520,512]{1,0:T(8,128)(2,1)S(1)}, bf16[520,512]{1,0:T(8,128)(2,1)S(1)}, u32[]{:S(2)}, u32[]{:S(2)}) collective-permute-start(bf16[520,512]{1,0:T(8,128)(2,1)S(1)} %shard_map.100.second), channel_id=1, source_target_pairs={{2,0},{1,3},{6,4},{5,7},{10,8},{9,11},{14,12},{13,15},{18,16},{17,... | collective-permute-start | bytes 1597448 | tf_op jit(solution)/shard_map/ppermute | solution.py:290
  30.9 2.5 %collective-permute-start.8 = (bf16[512,512]{1,0:T(8,128)(2,1)S(1)}, bf16[512,512]{1,0:T(8,128)(2,1)S(1)}, u32[]{:S(2)}, u32[]{:S(2)}) collective-permute-start(bf16[512,512]{1,0:T(8,128)(2,1)S(1)} %shard_map.102.far.far_ready), channel_id=1, source_target_pairs={{0,1},{1,0},{2,3},{3,2},{4,5},{5,4},{6,7},{7,6},{8,9},{9,8},{10,11... | collective-permute-start | bytes 1572872 | tf_op jit(solution)/shard_map/ppermute | solution.py:290
  36.6 2.5 %collective-permute-start.9 = (bf16[512,512]{1,0:T(8,128)(2,1)S(1)}, bf16[512,512]{1,0:T(8,128)(2,1)S(1)}, u32[]{:S(2)}, u32[]{:S(2)}) collective-permute-start(bf16[512,512]{1,0:T(8,128)(2,1)S(1)} %shard_map.105.far.far_ready), channel_id=1, source_target_pairs={{0,1},{1,0},{2,3},{3,2},{4,5},{5,4},{6,7},{7,6},{8,9},{9,8},{10,11... | collective-permute-start | bytes 1572872 | tf_op jit(solution)/shard_map/ppermute | solution.py:290

commit v5 on v4

--- a/solution.py
+++ b/solution.py
@@ -137,8 +137,8 @@
 
 
 def chip_kernel(span, keep, near, rows, *refs):
-    through = (len(refs) - 3) // 2
-    out, again, token = refs[through : through + 3]
+    through = (len(refs) - 2) // 2
+    out, token = refs[through : through + 2]
     token[...] = jnp.zeros_like(token)
     n, width = keep.shape
     m = len(span)
@@ -148,21 +148,20 @@
         at = slice(i * dk, (i + 1) * dk)
         out[at, :] = (keep[at, :] + wide_row(own, i, width) * near[at, :].astype(F32)).astype(BF16)
     out[n:, :] = gain_rows(own * gain_of(near, n, m), width)
-    again[...] = out[...]
 
 
 def through_kernel(after, x, token, out):
     del after, x, token, out
 
 
-def far_kernel(m, second, first, relayed, token, out):
+def far_kernel(m, second, other, first, relayed, token, out):
     n, width = out.shape
     dk = n // m
     gain = gain_of(first, n, m) + gain_of(relayed, n, m)
     for i in range(m):
         at = slice(i * dk, (i + 1) * dk)
         adjacent = first[at, :].astype(F32) + relayed[at, :].astype(F32)
-        out[at, :] = (adjacent + wide_row(gain, i, width) * second[at, :].astype(F32)).astype(BF16)
+        out[at, :] = (adjacent + wide_row(gain, i, width) * (second[at, :].astype(F32) + other[at, :].astype(F32))).astype(BF16)
 
 
 def block_kernel(span, heads, scale, q, k, v, g, cols, rows, ready, *refs):
@@ -295,16 +294,19 @@
     both = lambda pairs: [p for a, b in pairs for p in ((a, b), (b, a))]
     on_chip = both([(2 * c, 2 * c + 1) for c in range(chips)])
     mates = both([(2 * c + 1, 2 * c + 2) for c in range(0, chips, 2)])
-    second = both([(2 * c + 1, 2 * c + 4) for c in range(chips - 2)])
+    ahead = [(2 * c + 1, 2 * c + 4) for c in range(chips - 2)]
+    back = [(2 * c, 2 * c - 3) for c in range(2, chips)]
+    feed = ahead[1::2] + back[0::2]
+    rest = ahead[0::2] + back[1::2]
     relay = [p for c in range(0, chips, 2) for p in ((2 * c + 2, 2 * c), (2 * c + 1, 2 * c + 3))]
-    return on_chip, mates, second, relay
+    return on_chip, mates, feed, rest, relay
 
 
 def body(query_rows, key_rows, value_rows, out_grad, log_forget, input_pre, doc_starts):
     width, heads = log_forget.shape
     dk, dv = query_rows.shape[1] // heads, value_rows.shape[1] // heads
     scale = dk ** (-0.5)
-    on_chip, mates, second, relay = routes(lax.axis_size("ctx"))
+    on_chip, mates, feed, rest, relay = routes(lax.axis_size("ctx"))
     spans, at = [], 0
     for m in CHUNKS:
         spans.append(tuple(range(at, at + m)))
@@ -339,29 +341,29 @@
         )
         sends.append(send)
         keeps.append(keep)
-    nears, firsts, seconds, blocks, relayed = [], [], [], [], []
+    nears, firsts, seconds, others, blocks, relayed = [], [], [], [], [], []
     passed = ()
     for i, span in enumerate(spans):
         near = swap(sends[i], on_chip)
         passed = passed + tuple(sends[i + 1 : i + 2])
         count = len(passed)
-        chip, copy, token, *passed = call(
+        chip, token, *passed = call(
             functools.partial(chip_kernel, span),
-            [payload[i]] * 2 + [mark] + [(x.shape, BF16) for x in passed],
+            [payload[i], mark] + [(x.shape, BF16) for x in passed],
             (keeps[i], near, rows, *passed),
             [VM] * (3 + count),
-            [VM] * (3 + count),
+            [VM] * (2 + count),
             mib=8,
-            aliases={3 + j: 3 + j for j in range(count)},
-        )
-        if i > 0:
-            seconds.append(swap(passed[0], second))
+            aliases={3 + j: 2 + j for j in range(count)},
+        )
+        seconds.append(swap(chip, feed))
+        others.append(swap(chip, rest))
         if i + 1 < len(spans):
             sends[i + 1] = passed[-1]
-        passed = (copy,)
+        passed = ()
         firsts.append(swap(chip, mates))
         nears.append(near)
-    seconds.append(swap(copy, second))
+    marks = [token]
     passed = ()
     for i, span in enumerate(spans):
         m = len(span)
@@ -375,13 +377,11 @@
             [VM] * (4 + count),
             aliases={7 + j: 4 + j for j in range(count)},
         )
-        if count:
-            seconds.append(swap(token, second))
-            *block, token = block
-            passed = ()
         blocks.append(block)
+        marks.append(token)
+    for i, ready in enumerate((marks[0], marks[1])):
         (seconds[i],) = call(
-            through_kernel, payload[i : i + 1], (firsts[i], seconds[i], token), [VM] * 3, [VM], mib=8, aliases={1: 0}
+            through_kernel, payload[i : i + 1], (firsts[i], seconds[i], ready), [VM] * 3, [VM], mib=8, aliases={1: 0}
         )
         relayed.append(swap(seconds[i], relay))
     outs = ()
@@ -391,8 +391,8 @@
         (far,) = call(
             functools.partial(far_kernel, m),
             [((m * dk, dv), BF16)],
-            (seconds[i], firsts[i], relayed[i], token),
-            [VM] * 4,
+            (seconds[i], others[i], firsts[i], relayed[i], token),
+            [VM] * 5,
             [VM],
             mib=8,
         )

time: 41.1 us -> 40.6 us (0.988)
  waiting for transfers between devices: 15 us -> 12.9 us
  starting transfers between devices: 8.14 us -> 9.52 us
    ppermute x10 -> x12, waiting for transfers between devices: 15 us -> 12.9 us  [swap(): return lax.ppermute(x, 'ctx', route)]
    ppermute x10 -> x12, starting transfers between devices: 8.14 us -> 9.52 us  [swap(): return lax.ppermute(x, 'ctx', route)]
  transfers between devices with their start and end apart: 10 -> 12, of which waited for: 6 -> 6; matrix products, arithmetic and copies ran while one was open for 0% -> 0% of each run, Pallas kernels for 26% -> 27%
where the time goes in v5:
time: 40.6 us; the launch traced here: 40.3 us
  Pallas kernels  17.1 us (42%)
  waiting for transfers between devices  12.9 us (32%)
  starting transfers between devices  9.52 us (23%)
  between operations  0.83 us (2%)
    pallas_call x14, Pallas kernels, call(): pl.pallas_call(kernel, out_shape=[jax.ShapeDtypeStruct(*o) for o in outs]...  17.1 us
    ppermute x12, waiting for transfers between devices, swap(): return lax.ppermute(x, 'ctx', route)  12.9 us
    ppermute x12, starting transfers between devices, swap(): return lax.ppermute(x, 'ctx', route)  9.52 us
  transfers between devices with their start and end apart: 12, of which 6 were waited for; matrix products, arithmetic and copies ran while one was open for 0% of the time, Pallas kernels for 27%

profile of v5, /device:TPU:0, one launch (start us, length us, event | category | flops | bytes accessed | tf_op | source)
XLA Modules:
  0.0 40.3 jit_solution(6127948606515589677)
XLA Ops:
  0.6 3.6 %shard_map.94 = (bf16[520,512]{1,0:T(8,128)(2,1)S(1)}, f32[512,512]{1,0:T(8,128)S(1)}, f32[512,32]{1,0:T(8,128)S(1)}, f32[32,512]{1,0:T(8,128)S(1)}, bf16[512,10...) custom-call(f32[4,512]{1,0:T(4,128)} %bitcast.3, ...), custom_call_target="tpu_custom_call" | custom-call | flops 1000 | bytes 1000 | tf_op jit(solution)/shard_map/pallas_call | solution.py:272
  4.3 0.5 %collective-permute-start = (bf16[520,512]{1,0:T(8,128)(2,1)S(1)}, bf16[520,512]{1,0:T(8,128)(2,1)S(1)}, u32[]{:S(2)}, u32[]{:S(2)}) collective-permute-start(bf16[520,512]{1,0:T(8,128)(2,1)S(1)} %get-tuple-element.36), channel_id=1, source_target_pairs={{0,1},{1,0},{2,3},{3,2},{4,5},{5,4},{6,7},{7,6},{8,9},{9,8},{10,11... | collective-permute-start | bytes 1597448 | tf_op jit(solution)/shard_map/ppermute | solution.py:289
  4.8 1.1 %shard_map.95 = (bf16[520,512]{1,0:T(8,128)(2,1)S(1)}, f32[512,512]{1,0:T(8,128)S(1)}) custom-call(bf16[512,1024]{1,0:T(8,128)(2,1)S(1)} %get-tuple-element.38.q, bf16[512,1024]{1,0:T(8,128)(2,1)S(1)} %get-tuple-element.39.k, bf16[512,2048]{1,0:T(8,128)(2,1)S(1)} %get-tuple-element.40.v, bf16[512,2048]{1,0:T(8,128)(2,1)S(1)} %get-tuple-element.41.g, ...), custom_call_target="tpu_custom_call" | custom-call | flops 1000 | bytes 1000 | tf_op jit(solution)/shard_map/pallas_call | solution.py:272
  6.0 0.4 collective-permute-done.near
  6.3 0.7 %shard_map.96 = (bf16[520,512]{1,0:T(8,128)(2,1)S(1)}, f32[8,128]{1,0:T(8,128)}, bf16[520,512]{1,0:T(8,128)(2,1)S(1)}) custom-call(f32[512,512]{1,0:T(8,128)S(1)} %get-tuple-element.35.keep, bf16[520,512]{1,0:T(8,128)(2,1)S(1)} %collective-permute-done.near, f32[32,512]{1,0:T(8,128)S(1)} %get-tuple-element.37.rows, ...), custom_call_target="tpu_custom_call", output_to_operand_aliasing={{2}: (3, {})} | custom-call | flops 1000 | bytes 1000 | tf_op jit(solution)/shard_map/pallas_call | solution.py:272
  7.0 0.4 collective-permute-start.1
  7.4 0.7 %collective-permute-start.6 = (bf16[520,512]{1,0:T(8,128)(2,1)S(1)}, bf16[520,512]{1,0:T(8,128)(2,1)S(1)}, u32[]{:S(2)}, u32[]{:S(2)}) collective-permute-start(bf16[520,512]{1,0:T(8,128)(2,1)S(1)} %get-tuple-element.49), channel_id=1, source_target_pairs={{1,2},{2,1},{5,6},{6,5},{9,10},{10,9},{13,14},{14,13},{17,18},{18,... | collective-permute-start | bytes 1597448 | tf_op jit(solution)/shard_map/ppermute | solution.py:289
  8.1 0.7 %collective-permute-start.7 = (bf16[520,512]{1,0:T(8,128)(2,1)S(1)}, bf16[520,512]{1,0:T(8,128)(2,1)S(1)}, u32[]{:S(2)}, u32[]{:S(2)}) collective-permute-start(bf16[520,512]{1,0:T(8,128)(2,1)S(1)} %get-tuple-element.49), channel_id=1, source_target_pairs={{3,6},{7,10},{11,14},{4,1},{8,5},{12,9},{19,22},{23,26},{27,30},{2... | collective-permute-start | bytes 1597448 | tf_op jit(solution)/shard_map/ppermute | solution.py:289
  8.8 0.2 collective-permute-done.1.near
  8.9 0.1 shard_map.97
  9.1 0.7 %collective-permute-start.2 = (bf16[520,512]{1,0:T(8,128)(2,1)S(1)}, bf16[520,512]{1,0:T(8,128)(2,1)S(1)}, u32[]{:S(2)}, u32[]{:S(2)}) collective-permute-start(bf16[520,512]{1,0:T(8,128)(2,1)S(1)} %get-tuple-element.46), channel_id=1, source_target_pairs={{1,2},{2,1},{5,6},{6,5},{9,10},{10,9},{13,14},{14,13},{17,18},{18,... | collective-permute-start | bytes 1597448 | tf_op jit(solution)/shard_map/ppermute | solution.py:289
  9.8 0.7 %collective-permute-start.3 = (bf16[520,512]{1,0:T(8,128)(2,1)S(1)}, bf16[520,512]{1,0:T(8,128)(2,1)S(1)}, u32[]{:S(2)}, u32[]{:S(2)}) collective-permute-start(bf16[520,512]{1,0:T(8,128)(2,1)S(1)} %get-tuple-element.46), channel_id=1, source_target_pairs={{3,6},{7,10},{11,14},{4,1},{8,5},{12,9},{19,22},{23,26},{27,30},{2... | collective-permute-start | bytes 1597448 | tf_op jit(solution)/shard_map/ppermute | solution.py:289
  10.5 0.7 %collective-permute-start.8 = (bf16[520,512]{1,0:T(8,128)(2,1)S(1)}, bf16[520,512]{1,0:T(8,128)(2,1)S(1)}, u32[]{:S(2)}, u32[]{:S(2)}) collective-permute-start(bf16[520,512]{1,0:T(8,128)(2,1)S(1)} %get-tuple-element.49), channel_id=1, source_target_pairs={{1,4},{5,8},{9,12},{6,3},{10,7},{14,11},{17,20},{21,24},{25,28},{2... | collective-permute-start | bytes 1597448 | tf_op jit(solution)/shard_map/ppermute | solution.py:289
  11.2 0.0 collective-permute-done.6.after.first
  11.2 0.0 collective-permute-done.7.x
  11.2 1.3 %collective-permute-start.9 = (bf16[520,512]{1,0:T(8,128)(2,1)S(1)}, bf16[520,512]{1,0:T(8,128)(2,1)S(1)}, u32[]{:S(2)}, u32[]{:S(2)}) collective-permute-start(bf16[520,512]{1,0:T(8,128)(2,1)S(1)} %shard_map.100.second), channel_id=1, source_target_pairs={{2,0},{1,3},{6,4},{5,7},{10,8},{9,11},{14,12},{13,15},{18,16},{17,... | collective-permute-start | bytes 1597448 | tf_op jit(solution)/shard_map/ppermute | solution.py:289
  12.5 2.3 %shard_map.98 = (f32[512,512]{1,0:T(8,128)S(1)}, f32[512,512]{1,0:T(8,128)S(1)}, f32[512,1024]{1,0:T(8,128)S(1)}, f32[8,128]{1,0:T(8,128)S(1)}) custom-call(bf16[512,1024]{1,0:T(8,128)(2,1)S(1)} %get-tuple-element.38.q, bf16[512,1024]{1,0:T(8,128)(2,1)S(1)} %get-tuple-element.39.k, bf16[512,2048]{1,0:T(8,128)(2,1)S(1)} %get-tuple-element.40.v, ...), custom_call_target="tpu_custom_call" | custom-call | flops 1000 | bytes 1000 | tf_op jit(solution)/shard_map/pallas_call | solution.py:272
  14.9 0.7 %collective-permute-start.4 = (bf16[520,512]{1,0:T(8,128)(2,1)S(1)}, bf16[520,512]{1,0:T(8,128)(2,1)S(1)}, u32[]{:S(2)}, u32[]{:S(2)}) collective-permute-start(bf16[520,512]{1,0:T(8,128)(2,1)S(1)} %get-tuple-element.46), channel_id=1, source_target_pairs={{1,4},{5,8},{9,12},{6,3},{10,7},{14,11},{17,20},{21,24},{25,28},{2... | collective-permute-start | bytes 1597448 | tf_op jit(solution)/shard_map/ppermute | solution.py:289
  15.6 0.0 collective-permute-done.2.after.first
  15.6 0.0 collective-permute-done.3.x
  15.6 1.3 %collective-permute-start.5 = (bf16[520,512]{1,0:T(8,128)(2,1)S(1)}, bf16[520,512]{1,0:T(8,128)(2,1)S(1)}, u32[]{:S(2)}, u32[]{:S(2)}) collective-permute-start(bf16[520,512]{1,0:T(8,128)(2,1)S(1)} %shard_map.99.second), channel_id=1, source_target_pairs={{2,0},{1,3},{6,4},{5,7},{10,8},{9,11},{14,12},{13,15},{18,16},{17,... | collective-permute-start | bytes 1597448 | tf_op jit(solution)/shard_map/ppermute | solution.py:289
  16.9 2.3 %shard_map.101 = (f32[512,512]{1,0:T(8,128)S(1)}, f32[512,512]{1,0:T(8,128)S(1)}, f32[512,1024]{1,0:T(8,128)S(1)}, f32[8,128]{1,0:T(8,128)S(1)}) custom-call(bf16[512,1024]{1,0:T(8,128)(2,1)S(1)} %get-tuple-element.38.q, bf16[512,1024]{1,0:T(8,128)(2,1)S(1)} %get-tuple-element.39.k, bf16[512,2048]{1,0:T(8,128)(2,1)S(1)} %get-tuple-element.40.v, ...), custom_call_target="tpu_custom_call" | custom-call | flops 1000 | bytes 1000 | tf_op jit(solution)/shard_map/pallas_call | solution.py:272
  19.2 0.0 collective-permute-done.8.other
  19.3 11.3 %collective-permute-done.9.relayed = bf16[520,512]{1,0:T(8,128)(2,1)S(1)} collective-permute-done((bf16[520,512]{1,0:T(8,128)(2,1)S(1)}, bf16[520,512]{1,0:T(8,128)(2,1)S(1)}, u32[]{:S(2)}, u32[]{:S(2)}) %collective-permute-start.9) | collective-permute-done | bytes 532512 | tf_op jit(solution)/shard_map/ppermute | solution.py:289
  30.6 0.3 shard_map.102.far.far_ready
  30.9 1.8 %collective-permute-start.10 = (bf16[512,512]{1,0:T(8,128)(2,1)S(1)}, bf16[512,512]{1,0:T(8,128)(2,1)S(1)}, u32[]{:S(2)}, u32[]{:S(2)}) collective-permute-start(bf16[512,512]{1,0:T(8,128)(2,1)S(1)} %shard_map.102.far.far_ready), channel_id=1, source_target_pairs={{0,1},{1,0},{2,3},{3,2},{4,5},{5,4},{6,7},{7,6},{8,9},{9,8},{10,11... | collective-permute-start | bytes 1572872 | tf_op jit(solution)/shard_map/ppermute | solution.py:289
  32.7 1.3 %shard_map.103 = (bf16[512,1024]{1,0:T(8,128)(2,1)}, bf16[512,1024]{1,0:T(8,128)(2,1)}, bf16[512,2048]{1,0:T(8,128)(2,1)}) custom-call(bf16[512,512]{1,0:T(8,128)(2,1)S(1)} %shard_map.102.far.far_ready, bf16[512,1024]{1,0:T(8,128)(2,1)S(1)} %get-tuple-element.39.k, bf16[512,2048]{1,0:T(8,128)(2,1)S(1)} %get-tuple-element.40.v, ...), custom_call_target="tpu_custom_call" | custom-call | flops 1000 | bytes 1000 | tf_op jit(solution)/shard_map/pallas_call | solution.py:272
  34.0 0.2 collective-permute-done.10.other
  34.2 1.8 %shard_map.104 = (bf16[512,1024]{1,0:T(8,128)(2,1)}, bf16[512,1024]{1,0:T(8,128)(2,1)}, bf16[512,2048]{1,0:T(8,128)(2,1)}, f32[8,128]{1,0:T(8,128)S(1)}) custom-call(bf16[520,512]{1,0:T(8,128)(2,1)S(1)} %collective-permute-done.near, ...), custom_call_target="tpu_custom_call", output_to_operand_aliasing={{0}: (10, {}), {1}: (11, {}), {2}: (12, {})} | custom-call | flops 1000 | bytes 1000 | tf_op jit(solution)/shard_map/pallas_call | solution.py:272
  36.0 0.0 collective-permute-done.4.other
  36.0 0.3 collective-permute-done.5.relayed
  36.3 0.3 shard_map.105.far.far_ready
  36.6 0.1 collective-permute-start.11
  36.7 1.3 %shard_map.106 = (bf16[512,1024]{1,0:T(8,128)(2,1)}, bf16[512,1024]{1,0:T(8,128)(2,1)}, bf16[512,2048]{1,0:T(8,128)(2,1)}) custom-call(bf16[512,512]{1,0:T(8,128)(2,1)S(1)} %shard_map.105.far.far_ready, bf16[512,1024]{1,0:T(8,128)(2,1)S(1)} %get-tuple-element.39.k, ...), custom_call_target="tpu_custom_call", output_to_operand_aliasing={{0}: (8, {}), {1}: (9, {}), {2}: (10, {})} | custom-call | flops 1000 | bytes 1000 | tf_op jit(solution)/shard_map/pallas_call | solution.py:272
  38.0 0.6 %collective-permute-done.11.other = bf16[512,512]{1,0:T(8,128)(2,1)S(1)} collective-permute-done((bf16[512,512]{1,0:T(8,128)(2,1)S(1)}, bf16[512,512]{1,0:T(8,128)(2,1)S(1)}, u32[]{:S(2)}, u32[]{:S(2)}) %collective-permute-start.11) | collective-permute-done | bytes 524320 | tf_op jit(solution)/shard_map/ppermute | solution.py:289
  38.6 1.8 %shard_map.107 = (bf16[512,1024]{1,0:T(8,128)(2,1)}, bf16[512,1024]{1,0:T(8,128)(2,1)}, bf16[512,2048]{1,0:T(8,128)(2,1)}) custom-call(bf16[520,512]{1,0:T(8,128)(2,1)S(1)} %collective-permute-done.1.near, bf16[512,512]{1,0:T(8,128)(2,1)S(1)} %collective-permute-done.11.other, ...), custom_call_target="tpu_custom_call", output_to_operand_aliasing={{0}: (10, {}), {1}: (11, {}), {2}: (12, {})} | custom-call | flops 1000 | bytes 1000 | tf_op jit(solution)/shard_map/pallas_call | solution.py:272
  (2 shorter events, 0.0 us)
Async XLA Ops:
  4.3 2.1 %collective-permute-start = (bf16[520,512]{1,0:T(8,128)(2,1)S(1)}, bf16[520,512]{1,0:T(8,128)(2,1)S(1)}, u32[]{:S(2)}, u32[]{:S(2)}) collective-permute-start(bf16[520,512]{1,0:T(8,128)(2,1)S(1)} %get-tuple-element.36), channel_id=1, source_target_pairs={{0,1},{1,0},{2,3},{3,2},{4,5},{5,4},{6,7},{7,6},{8,9},{9,8},{10,11... | collective-permute-start | bytes 1597448 | tf_op jit(solution)/shard_map/ppermute | solution.py:289
  7.0 1.9 %collective-permute-start.1 = (bf16[520,512]{1,0:T(8,128)(2,1)S(1)}, bf16[520,512]{1,0:T(8,128)(2,1)S(1)}, u32[]{:S(2)}, u32[]{:S(2)}) collective-permute-start(bf16[520,512]{1,0:T(8,128)(2,1)S(1)} %get-tuple-element.44), channel_id=1, source_target_pairs={{0,1},{1,0},{2,3},{3,2},{4,5},{5,4},{6,7},{7,6},{8,9},{9,8},{10,11... | collective-permute-start | bytes 1597448 | tf_op jit(solution)/shard_map/ppermute | solution.py:289
  7.4 3.8 %collective-permute-start.6 = (bf16[520,512]{1,0:T(8,128)(2,1)S(1)}, bf16[520,512]{1,0:T(8,128)(2,1)S(1)}, u32[]{:S(2)}, u32[]{:S(2)}) collective-permute-start(bf16[520,512]{1,0:T(8,128)(2,1)S(1)} %get-tuple-element.49), channel_id=1, source_target_pairs={{1,2},{2,1},{5,6},{6,5},{9,10},{10,9},{13,14},{14,13},{17,18},{18,... | collective-permute-start | bytes 1597448 | tf_op jit(solution)/shard_map/ppermute | solution.py:289
  8.1 3.1 %collective-permute-start.7 = (bf16[520,512]{1,0:T(8,128)(2,1)S(1)}, bf16[520,512]{1,0:T(8,128)(2,1)S(1)}, u32[]{:S(2)}, u32[]{:S(2)}) collective-permute-start(bf16[520,512]{1,0:T(8,128)(2,1)S(1)} %get-tuple-element.49), channel_id=1, source_target_pairs={{3,6},{7,10},{11,14},{4,1},{8,5},{12,9},{19,22},{23,26},{27,30},{2... | collective-permute-start | bytes 1597448 | tf_op jit(solution)/shard_map/ppermute | solution.py:289
  9.1 6.5 %collective-permute-start.2 = (bf16[520,512]{1,0:T(8,128)(2,1)S(1)}, bf16[520,512]{1,0:T(8,128)(2,1)S(1)}, u32[]{:S(2)}, u32[]{:S(2)}) collective-permute-start(bf16[520,512]{1,0:T(8,128)(2,1)S(1)} %get-tuple-element.46), channel_id=1, source_target_pairs={{1,2},{2,1},{5,6},{6,5},{9,10},{10,9},{13,14},{14,13},{17,18},{18,... | collective-permute-start | bytes 1597448 | tf_op jit(solution)/shard_map/ppermute | solution.py:289
  9.8 5.8 %collective-permute-start.3 = (bf16[520,512]{1,0:T(8,128)(2,1)S(1)}, bf16[520,512]{1,0:T(8,128)(2,1)S(1)}, u32[]{:S(2)}, u32[]{:S(2)}) collective-permute-start(bf16[520,512]{1,0:T(8,128)(2,1)S(1)} %get-tuple-element.46), channel_id=1, source_target_pairs={{3,6},{7,10},{11,14},{4,1},{8,5},{12,9},{19,22},{23,26},{27,30},{2... | collective-permute-start | bytes 1597448 | tf_op jit(solution)/shard_map/ppermute | solution.py:289
  10.5 8.8 %collective-permute-start.8 = (bf16[520,512]{1,0:T(8,128)(2,1)S(1)}, bf16[520,512]{1,0:T(8,128)(2,1)S(1)}, u32[]{:S(2)}, u32[]{:S(2)}) collective-permute-start(bf16[520,512]{1,0:T(8,128)(2,1)S(1)} %get-tuple-element.49), channel_id=1, source_target_pairs={{1,4},{5,8},{9,12},{6,3},{10,7},{14,11},{17,20},{21,24},{25,28},{2... | collective-permute-start | bytes 1597448 | tf_op jit(solution)/shard_map/ppermute | solution.py:289
  11.2 19.4 %collective-permute-start.9 = (bf16[520,512]{1,0:T(8,128)(2,1)S(1)}, bf16[520,512]{1,0:T(8,128)(2,1)S(1)}, u32[]{:S(2)}, u32[]{:S(2)}) collective-permute-start(bf16[520,512]{1,0:T(8,128)(2,1)S(1)} %shard_map.100.second), channel_id=1, source_target_pairs={{2,0},{1,3},{6,4},{5,7},{10,8},{9,11},{14,12},{13,15},{18,16},{17,... | collective-permute-start | bytes 1597448 | tf_op jit(solution)/shard_map/ppermute | solution.py:289
  14.9 21.2 %collective-permute-start.4 = (bf16[520,512]{1,0:T(8,128)(2,1)S(1)}, bf16[520,512]{1,0:T(8,128)(2,1)S(1)}, u32[]{:S(2)}, u32[]{:S(2)}) collective-permute-start(bf16[520,512]{1,0:T(8,128)(2,1)S(1)} %get-tuple-element.46), channel_id=1, source_target_pairs={{1,4},{5,8},{9,12},{6,3},{10,7},{14,11},{17,20},{21,24},{25,28},{2... | collective-permute-start | bytes 1597448 | tf_op jit(solution)/shard_map/ppermute | solution.py:289
  15.6 20.7 %collective-permute-start.5 = (bf16[520,512]{1,0:T(8,128)(2,1)S(1)}, bf16[520,512]{1,0:T(8,128)(2,1)S(1)}, u32[]{:S(2)}, u32[]{:S(2)}) collective-permute-start(bf16[520,512]{1,0:T(8,128)(2,1)S(1)} %shard_map.99.second), channel_id=1, source_target_pairs={{2,0},{1,3},{6,4},{5,7},{10,8},{9,11},{14,12},{13,15},{18,16},{17,... | collective-permute-start | bytes 1597448 | tf_op jit(solution)/shard_map/ppermute | solution.py:289
  30.9 3.4 %collective-permute-start.10 = (bf16[512,512]{1,0:T(8,128)(2,1)S(1)}, bf16[512,512]{1,0:T(8,128)(2,1)S(1)}, u32[]{:S(2)}, u32[]{:S(2)}) collective-permute-start(bf16[512,512]{1,0:T(8,128)(2,1)S(1)} %shard_map.102.far.far_ready), channel_id=1, source_target_pairs={{0,1},{1,0},{2,3},{3,2},{4,5},{5,4},{6,7},{7,6},{8,9},{9,8},{10,11... | collective-permute-start | bytes 1572872 | tf_op jit(solution)/shard_map/ppermute | solution.py:289
  36.6 2.0 %collective-permute-start.11 = (bf16[512,512]{1,0:T(8,128)(2,1)S(1)}, bf16[512,512]{1,0:T(8,128)(2,1)S(1)}, u32[]{:S(2)}, u32[]{:S(2)}) collective-permute-start(bf16[512,512]{1,0:T(8,128)(2,1)S(1)} %shard_map.105.far.far_ready), channel_id=1, source_target_pairs={{0,1},{1,0},{2,3},{3,2},{4,5},{5,4},{6,7},{7,6},{8,9},{9,8},{10,11... | collective-permute-start | bytes 1572872 | tf_op jit(solution)/shard_map/ppermute | solution.py:289

commit v6 on v5

--- a/solution.py
+++ b/solution.py
@@ -154,7 +154,7 @@
     del after, x, token, out
 
 
-def far_kernel(m, second, other, first, relayed, token, out):
+def far_kernel(m, relayed, second, first, other, token, out):
     n, width = out.shape
     dk = n // m
     gain = gain_of(first, n, m) + gain_of(relayed, n, m)
@@ -391,7 +391,7 @@
         (far,) = call(
             functools.partial(far_kernel, m),
             [((m * dk, dv), BF16)],
-            (seconds[i], others[i], firsts[i], relayed[i], token),
+            (relayed[i], seconds[i], firsts[i], others[i], token),
             [VM] * 5,
             [VM],
             mib=8,

time: 40.6 us -> 40.6 us (level)
  no operation moved by 1% of the time
where the time goes in v6:
time: 40.6 us; the launch traced here: 40.3 us
  Pallas kernels  17.1 us (42%)
  waiting for transfers between devices  12.9 us (32%)
  starting transfers between devices  9.52 us (23%)
  between operations  0.83 us (2%)
    pallas_call x14, Pallas kernels, call(): pl.pallas_call(kernel, out_shape=[jax.ShapeDtypeStruct(*o) for o in outs]...  17.1 us
    ppermute x12, waiting for transfers between devices, swap(): return lax.ppermute(x, 'ctx', route)  12.9 us
    ppermute x12, starting transfers between devices, swap(): return lax.ppermute(x, 'ctx', route)  9.52 us
  transfers between devices with their start and end apart: 12, of which 6 were waited for; matrix products, arithmetic and copies ran while one was open for 0% of the time, Pallas kernels for 27%

profile of v6, /device:TPU:0, one launch (start us, length us, event | category | flops | bytes accessed | tf_op | source)
XLA Modules:
  0.0 40.3 jit_solution(2890583816930216820)
XLA Ops:
  0.6 3.6 %shard_map.94 = (bf16[520,512]{1,0:T(8,128)(2,1)S(1)}, f32[512,512]{1,0:T(8,128)S(1)}, f32[512,32]{1,0:T(8,128)S(1)}, f32[32,512]{1,0:T(8,128)S(1)}, bf16[512,10...) custom-call(f32[4,512]{1,0:T(4,128)} %bitcast.3, ...), custom_call_target="tpu_custom_call" | custom-call | flops 1000 | bytes 1000 | tf_op jit(solution)/shard_map/pallas_call | solution.py:272
  4.3 0.5 %collective-permute-start = (bf16[520,512]{1,0:T(8,128)(2,1)S(1)}, bf16[520,512]{1,0:T(8,128)(2,1)S(1)}, u32[]{:S(2)}, u32[]{:S(2)}) collective-permute-start(bf16[520,512]{1,0:T(8,128)(2,1)S(1)} %get-tuple-element.36), channel_id=1, source_target_pairs={{0,1},{1,0},{2,3},{3,2},{4,5},{5,4},{6,7},{7,6},{8,9},{9,8},{10,11... | collective-permute-start | bytes 1597448 | tf_op jit(solution)/shard_map/ppermute | solution.py:289
  4.8 1.1 %shard_map.95 = (bf16[520,512]{1,0:T(8,128)(2,1)S(1)}, f32[512,512]{1,0:T(8,128)S(1)}) custom-call(bf16[512,1024]{1,0:T(8,128)(2,1)S(1)} %get-tuple-element.38.q, bf16[512,1024]{1,0:T(8,128)(2,1)S(1)} %get-tuple-element.39.k, bf16[512,2048]{1,0:T(8,128)(2,1)S(1)} %get-tuple-element.40.v, bf16[512,2048]{1,0:T(8,128)(2,1)S(1)} %get-tuple-element.41.g, ...), custom_call_target="tpu_custom_call" | custom-call | flops 1000 | bytes 1000 | tf_op jit(solution)/shard_map/pallas_call | solution.py:272
  6.0 0.4 collective-permute-done.near
  6.3 0.7 %shard_map.96 = (bf16[520,512]{1,0:T(8,128)(2,1)S(1)}, f32[8,128]{1,0:T(8,128)}, bf16[520,512]{1,0:T(8,128)(2,1)S(1)}) custom-call(f32[512,512]{1,0:T(8,128)S(1)} %get-tuple-element.35.keep, bf16[520,512]{1,0:T(8,128)(2,1)S(1)} %collective-permute-done.near, f32[32,512]{1,0:T(8,128)S(1)} %get-tuple-element.37.rows, ...), custom_call_target="tpu_custom_call", output_to_operand_aliasing={{2}: (3, {})} | custom-call | flops 1000 | bytes 1000 | tf_op jit(solution)/shard_map/pallas_call | solution.py:272
  7.0 0.4 collective-permute-start.1
  7.4 0.7 %collective-permute-start.6 = (bf16[520,512]{1,0:T(8,128)(2,1)S(1)}, bf16[520,512]{1,0:T(8,128)(2,1)S(1)}, u32[]{:S(2)}, u32[]{:S(2)}) collective-permute-start(bf16[520,512]{1,0:T(8,128)(2,1)S(1)} %get-tuple-element.49), channel_id=1, source_target_pairs={{1,2},{2,1},{5,6},{6,5},{9,10},{10,9},{13,14},{14,13},{17,18},{18,... | collective-permute-start | bytes 1597448 | tf_op jit(solution)/shard_map/ppermute | solution.py:289
  8.1 0.7 %collective-permute-start.7 = (bf16[520,512]{1,0:T(8,128)(2,1)S(1)}, bf16[520,512]{1,0:T(8,128)(2,1)S(1)}, u32[]{:S(2)}, u32[]{:S(2)}) collective-permute-start(bf16[520,512]{1,0:T(8,128)(2,1)S(1)} %get-tuple-element.49), channel_id=1, source_target_pairs={{3,6},{7,10},{11,14},{4,1},{8,5},{12,9},{19,22},{23,26},{27,30},{2... | collective-permute-start | bytes 1597448 | tf_op jit(solution)/shard_map/ppermute | solution.py:289
  8.8 0.2 collective-permute-done.1.near
  8.9 0.1 shard_map.97
  9.1 0.7 %collective-permute-start.2 = (bf16[520,512]{1,0:T(8,128)(2,1)S(1)}, bf16[520,512]{1,0:T(8,128)(2,1)S(1)}, u32[]{:S(2)}, u32[]{:S(2)}) collective-permute-start(bf16[520,512]{1,0:T(8,128)(2,1)S(1)} %get-tuple-element.46), channel_id=1, source_target_pairs={{1,2},{2,1},{5,6},{6,5},{9,10},{10,9},{13,14},{14,13},{17,18},{18,... | collective-permute-start | bytes 1597448 | tf_op jit(solution)/shard_map/ppermute | solution.py:289
  9.8 0.7 %collective-permute-start.3 = (bf16[520,512]{1,0:T(8,128)(2,1)S(1)}, bf16[520,512]{1,0:T(8,128)(2,1)S(1)}, u32[]{:S(2)}, u32[]{:S(2)}) collective-permute-start(bf16[520,512]{1,0:T(8,128)(2,1)S(1)} %get-tuple-element.46), channel_id=1, source_target_pairs={{3,6},{7,10},{11,14},{4,1},{8,5},{12,9},{19,22},{23,26},{27,30},{2... | collective-permute-start | bytes 1597448 | tf_op jit(solution)/shard_map/ppermute | solution.py:289
  10.5 0.7 %collective-permute-start.9 = (bf16[520,512]{1,0:T(8,128)(2,1)S(1)}, bf16[520,512]{1,0:T(8,128)(2,1)S(1)}, u32[]{:S(2)}, u32[]{:S(2)}) collective-permute-start(bf16[520,512]{1,0:T(8,128)(2,1)S(1)} %get-tuple-element.49), channel_id=1, source_target_pairs={{1,4},{5,8},{9,12},{6,3},{10,7},{14,11},{17,20},{21,24},{25,28},{2... | collective-permute-start | bytes 1597448 | tf_op jit(solution)/shard_map/ppermute | solution.py:289
  11.2 0.0 collective-permute-done.6.after.first
  11.2 0.0 collective-permute-done.7.x
  11.2 1.3 %collective-permute-start.8 = (bf16[520,512]{1,0:T(8,128)(2,1)S(1)}, bf16[520,512]{1,0:T(8,128)(2,1)S(1)}, u32[]{:S(2)}, u32[]{:S(2)}) collective-permute-start(bf16[520,512]{1,0:T(8,128)(2,1)S(1)} %shard_map.100.second), channel_id=1, source_target_pairs={{2,0},{1,3},{6,4},{5,7},{10,8},{9,11},{14,12},{13,15},{18,16},{17,... | collective-permute-start | bytes 1597448 | tf_op jit(solution)/shard_map/ppermute | solution.py:289
  12.5 2.3 %shard_map.98 = (f32[512,512]{1,0:T(8,128)S(1)}, f32[512,512]{1,0:T(8,128)S(1)}, f32[512,1024]{1,0:T(8,128)S(1)}, f32[8,128]{1,0:T(8,128)S(1)}) custom-call(bf16[512,1024]{1,0:T(8,128)(2,1)S(1)} %get-tuple-element.38.q, bf16[512,1024]{1,0:T(8,128)(2,1)S(1)} %get-tuple-element.39.k, bf16[512,2048]{1,0:T(8,128)(2,1)S(1)} %get-tuple-element.40.v, ...), custom_call_target="tpu_custom_call" | custom-call | flops 1000 | bytes 1000 | tf_op jit(solution)/shard_map/pallas_call | solution.py:272
  14.9 0.7 %collective-permute-start.5 = (bf16[520,512]{1,0:T(8,128)(2,1)S(1)}, bf16[520,512]{1,0:T(8,128)(2,1)S(1)}, u32[]{:S(2)}, u32[]{:S(2)}) collective-permute-start(bf16[520,512]{1,0:T(8,128)(2,1)S(1)} %get-tuple-element.46), channel_id=1, source_target_pairs={{1,4},{5,8},{9,12},{6,3},{10,7},{14,11},{17,20},{21,24},{25,28},{2... | collective-permute-start | bytes 1597448 | tf_op jit(solution)/shard_map/ppermute | solution.py:289
  15.6 0.0 collective-permute-done.2.after.first
  15.6 0.0 collective-permute-done.3.x
  15.6 1.3 %collective-permute-start.4 = (bf16[520,512]{1,0:T(8,128)(2,1)S(1)}, bf16[520,512]{1,0:T(8,128)(2,1)S(1)}, u32[]{:S(2)}, u32[]{:S(2)}) collective-permute-start(bf16[520,512]{1,0:T(8,128)(2,1)S(1)} %shard_map.99.second), channel_id=1, source_target_pairs={{2,0},{1,3},{6,4},{5,7},{10,8},{9,11},{14,12},{13,15},{18,16},{17,... | collective-permute-start | bytes 1597448 | tf_op jit(solution)/shard_map/ppermute | solution.py:289
  16.9 2.3 %shard_map.101 = (f32[512,512]{1,0:T(8,128)S(1)}, f32[512,512]{1,0:T(8,128)S(1)}, f32[512,1024]{1,0:T(8,128)S(1)}, f32[8,128]{1,0:T(8,128)S(1)}) custom-call(bf16[512,1024]{1,0:T(8,128)(2,1)S(1)} %get-tuple-element.38.q, bf16[512,1024]{1,0:T(8,128)(2,1)S(1)} %get-tuple-element.39.k, bf16[512,2048]{1,0:T(8,128)(2,1)S(1)} %get-tuple-element.40.v, ...), custom_call_target="tpu_custom_call" | custom-call | flops 1000 | bytes 1000 | tf_op jit(solution)/shard_map/pallas_call | solution.py:272
  19.2 0.0 collective-permute-done.9.other
  19.3 11.3 %collective-permute-done.8.relayed = bf16[520,512]{1,0:T(8,128)(2,1)S(1)} collective-permute-done((bf16[520,512]{1,0:T(8,128)(2,1)S(1)}, bf16[520,512]{1,0:T(8,128)(2,1)S(1)}, u32[]{:S(2)}, u32[]{:S(2)}) %collective-permute-start.8) | collective-permute-done | bytes 532512 | tf_op jit(solution)/shard_map/ppermute | solution.py:289
  30.6 0.3 shard_map.102.far.far_ready
  30.9 1.8 %collective-permute-start.10 = (bf16[512,512]{1,0:T(8,128)(2,1)S(1)}, bf16[512,512]{1,0:T(8,128)(2,1)S(1)}, u32[]{:S(2)}, u32[]{:S(2)}) collective-permute-start(bf16[512,512]{1,0:T(8,128)(2,1)S(1)} %shard_map.102.far.far_ready), channel_id=1, source_target_pairs={{0,1},{1,0},{2,3},{3,2},{4,5},{5,4},{6,7},{7,6},{8,9},{9,8},{10,11... | collective-permute-start | bytes 1572872 | tf_op jit(solution)/shard_map/ppermute | solution.py:289
  32.7 1.3 %shard_map.103 = (bf16[512,1024]{1,0:T(8,128)(2,1)}, bf16[512,1024]{1,0:T(8,128)(2,1)}, bf16[512,2048]{1,0:T(8,128)(2,1)}) custom-call(bf16[512,512]{1,0:T(8,128)(2,1)S(1)} %shard_map.102.far.far_ready, bf16[512,1024]{1,0:T(8,128)(2,1)S(1)} %get-tuple-element.39.k, bf16[512,2048]{1,0:T(8,128)(2,1)S(1)} %get-tuple-element.40.v, ...), custom_call_target="tpu_custom_call" | custom-call | flops 1000 | bytes 1000 | tf_op jit(solution)/shard_map/pallas_call | solution.py:272
  34.0 0.2 collective-permute-done.10.other
  34.2 1.8 %shard_map.104 = (bf16[512,1024]{1,0:T(8,128)(2,1)}, bf16[512,1024]{1,0:T(8,128)(2,1)}, bf16[512,2048]{1,0:T(8,128)(2,1)}, f32[8,128]{1,0:T(8,128)S(1)}) custom-call(bf16[520,512]{1,0:T(8,128)(2,1)S(1)} %collective-permute-done.near, ...), custom_call_target="tpu_custom_call", output_to_operand_aliasing={{0}: (10, {}), {1}: (11, {}), {2}: (12, {})} | custom-call | flops 1000 | bytes 1000 | tf_op jit(solution)/shard_map/pallas_call | solution.py:272
  36.0 0.0 collective-permute-done.5.other
  36.0 0.3 collective-permute-done.4.relayed
  36.3 0.3 shard_map.105.far.far_ready
  36.6 0.1 collective-permute-start.11
  36.7 1.3 %shard_map.106 = (bf16[512,1024]{1,0:T(8,128)(2,1)}, bf16[512,1024]{1,0:T(8,128)(2,1)}, bf16[512,2048]{1,0:T(8,128)(2,1)}) custom-call(bf16[512,512]{1,0:T(8,128)(2,1)S(1)} %shard_map.105.far.far_ready, bf16[512,1024]{1,0:T(8,128)(2,1)S(1)} %get-tuple-element.39.k, ...), custom_call_target="tpu_custom_call", output_to_operand_aliasing={{0}: (8, {}), {1}: (9, {}), {2}: (10, {})} | custom-call | flops 1000 | bytes 1000 | tf_op jit(solution)/shard_map/pallas_call | solution.py:272
  38.0 0.6 %collective-permute-done.11.other = bf16[512,512]{1,0:T(8,128)(2,1)S(1)} collective-permute-done((bf16[512,512]{1,0:T(8,128)(2,1)S(1)}, bf16[512,512]{1,0:T(8,128)(2,1)S(1)}, u32[]{:S(2)}, u32[]{:S(2)}) %collective-permute-start.11) | collective-permute-done | bytes 524320 | tf_op jit(solution)/shard_map/ppermute | solution.py:289
  38.6 1.8 %shard_map.107 = (bf16[512,1024]{1,0:T(8,128)(2,1)}, bf16[512,1024]{1,0:T(8,128)(2,1)}, bf16[512,2048]{1,0:T(8,128)(2,1)}) custom-call(bf16[520,512]{1,0:T(8,128)(2,1)S(1)} %collective-permute-done.1.near, bf16[512,512]{1,0:T(8,128)(2,1)S(1)} %collective-permute-done.11.other, ...), custom_call_target="tpu_custom_call", output_to_operand_aliasing={{0}: (10, {}), {1}: (11, {}), {2}: (12, {})} | custom-call | flops 1000 | bytes 1000 | tf_op jit(solution)/shard_map/pallas_call | solution.py:272
  (2 shorter events, 0.0 us)
Async XLA Ops:
  4.3 2.1 %collective-permute-start = (bf16[520,512]{1,0:T(8,128)(2,1)S(1)}, bf16[520,512]{1,0:T(8,128)(2,1)S(1)}, u32[]{:S(2)}, u32[]{:S(2)}) collective-permute-start(bf16[520,512]{1,0:T(8,128)(2,1)S(1)} %get-tuple-element.36), channel_id=1, source_target_pairs={{0,1},{1,0},{2,3},{3,2},{4,5},{5,4},{6,7},{7,6},{8,9},{9,8},{10,11... | collective-permute-start | bytes 1597448 | tf_op jit(solution)/shard_map/ppermute | solution.py:289
  7.0 1.9 %collective-permute-start.1 = (bf16[520,512]{1,0:T(8,128)(2,1)S(1)}, bf16[520,512]{1,0:T(8,128)(2,1)S(1)}, u32[]{:S(2)}, u32[]{:S(2)}) collective-permute-start(bf16[520,512]{1,0:T(8,128)(2,1)S(1)} %get-tuple-element.44), channel_id=1, source_target_pairs={{0,1},{1,0},{2,3},{3,2},{4,5},{5,4},{6,7},{7,6},{8,9},{9,8},{10,11... | collective-permute-start | bytes 1597448 | tf_op jit(solution)/shard_map/ppermute | solution.py:289
  7.4 3.8 %collective-permute-start.6 = (bf16[520,512]{1,0:T(8,128)(2,1)S(1)}, bf16[520,512]{1,0:T(8,128)(2,1)S(1)}, u32[]{:S(2)}, u32[]{:S(2)}) collective-permute-start(bf16[520,512]{1,0:T(8,128)(2,1)S(1)} %get-tuple-element.49), channel_id=1, source_target_pairs={{1,2},{2,1},{5,6},{6,5},{9,10},{10,9},{13,14},{14,13},{17,18},{18,... | collective-permute-start | bytes 1597448 | tf_op jit(solution)/shard_map/ppermute | solution.py:289
  8.1 3.1 %collective-permute-start.7 = (bf16[520,512]{1,0:T(8,128)(2,1)S(1)}, bf16[520,512]{1,0:T(8,128)(2,1)S(1)}, u32[]{:S(2)}, u32[]{:S(2)}) collective-permute-start(bf16[520,512]{1,0:T(8,128)(2,1)S(1)} %get-tuple-element.49), channel_id=1, source_target_pairs={{3,6},{7,10},{11,14},{4,1},{8,5},{12,9},{19,22},{23,26},{27,30},{2... | collective-permute-start | bytes 1597448 | tf_op jit(solution)/shard_map/ppermute | solution.py:289
  9.1 6.5 %collective-permute-start.2 = (bf16[520,512]{1,0:T(8,128)(2,1)S(1)}, bf16[520,512]{1,0:T(8,128)(2,1)S(1)}, u32[]{:S(2)}, u32[]{:S(2)}) collective-permute-start(bf16[520,512]{1,0:T(8,128)(2,1)S(1)} %get-tuple-element.46), channel_id=1, source_target_pairs={{1,2},{2,1},{5,6},{6,5},{9,10},{10,9},{13,14},{14,13},{17,18},{18,... | collective-permute-start | bytes 1597448 | tf_op jit(solution)/shard_map/ppermute | solution.py:289
  9.8 5.8 %collective-permute-start.3 = (bf16[520,512]{1,0:T(8,128)(2,1)S(1)}, bf16[520,512]{1,0:T(8,128)(2,1)S(1)}, u32[]{:S(2)}, u32[]{:S(2)}) collective-permute-start(bf16[520,512]{1,0:T(8,128)(2,1)S(1)} %get-tuple-element.46), channel_id=1, source_target_pairs={{3,6},{7,10},{11,14},{4,1},{8,5},{12,9},{19,22},{23,26},{27,30},{2... | collective-permute-start | bytes 1597448 | tf_op jit(solution)/shard_map/ppermute | solution.py:289
  10.5 8.8 %collective-permute-start.9 = (bf16[520,512]{1,0:T(8,128)(2,1)S(1)}, bf16[520,512]{1,0:T(8,128)(2,1)S(1)}, u32[]{:S(2)}, u32[]{:S(2)}) collective-permute-start(bf16[520,512]{1,0:T(8,128)(2,1)S(1)} %get-tuple-element.49), channel_id=1, source_target_pairs={{1,4},{5,8},{9,12},{6,3},{10,7},{14,11},{17,20},{21,24},{25,28},{2... | collective-permute-start | bytes 1597448 | tf_op jit(solution)/shard_map/ppermute | solution.py:289
  11.2 19.4 %collective-permute-start.8 = (bf16[520,512]{1,0:T(8,128)(2,1)S(1)}, bf16[520,512]{1,0:T(8,128)(2,1)S(1)}, u32[]{:S(2)}, u32[]{:S(2)}) collective-permute-start(bf16[520,512]{1,0:T(8,128)(2,1)S(1)} %shard_map.100.second), channel_id=1, source_target_pairs={{2,0},{1,3},{6,4},{5,7},{10,8},{9,11},{14,12},{13,15},{18,16},{17,... | collective-permute-start | bytes 1597448 | tf_op jit(solution)/shard_map/ppermute | solution.py:289
  14.9 21.2 %collective-permute-start.5 = (bf16[520,512]{1,0:T(8,128)(2,1)S(1)}, bf16[520,512]{1,0:T(8,128)(2,1)S(1)}, u32[]{:S(2)}, u32[]{:S(2)}) collective-permute-start(bf16[520,512]{1,0:T(8,128)(2,1)S(1)} %get-tuple-element.46), channel_id=1, source_target_pairs={{1,4},{5,8},{9,12},{6,3},{10,7},{14,11},{17,20},{21,24},{25,28},{2... | collective-permute-start | bytes 1597448 | tf_op jit(solution)/shard_map/ppermute | solution.py:289
  15.6 20.7 %collective-permute-start.4 = (bf16[520,512]{1,0:T(8,128)(2,1)S(1)}, bf16[520,512]{1,0:T(8,128)(2,1)S(1)}, u32[]{:S(2)}, u32[]{:S(2)}) collective-permute-start(bf16[520,512]{1,0:T(8,128)(2,1)S(1)} %shard_map.99.second), channel_id=1, source_target_pairs={{2,0},{1,3},{6,4},{5,7},{10,8},{9,11},{14,12},{13,15},{18,16},{17,... | collective-permute-start | bytes 1597448 | tf_op jit(solution)/shard_map/ppermute | solution.py:289
  30.9 3.4 %collective-permute-start.10 = (bf16[512,512]{1,0:T(8,128)(2,1)S(1)}, bf16[512,512]{1,0:T(8,128)(2,1)S(1)}, u32[]{:S(2)}, u32[]{:S(2)}) collective-permute-start(bf16[512,512]{1,0:T(8,128)(2,1)S(1)} %shard_map.102.far.far_ready), channel_id=1, source_target_pairs={{0,1},{1,0},{2,3},{3,2},{4,5},{5,4},{6,7},{7,6},{8,9},{9,8},{10,11... | collective-permute-start | bytes 1572872 | tf_op jit(solution)/shard_map/ppermute | solution.py:289
  36.6 2.0 %collective-permute-start.11 = (bf16[512,512]{1,0:T(8,128)(2,1)S(1)}, bf16[512,512]{1,0:T(8,128)(2,1)S(1)}, u32[]{:S(2)}, u32[]{:S(2)}) collective-permute-start(bf16[512,512]{1,0:T(8,128)(2,1)S(1)} %shard_map.105.far.far_ready), channel_id=1, source_target_pairs={{0,1},{1,0},{2,3},{3,2},{4,5},{5,4},{6,7},{7,6},{8,9},{9,8},{10,11... | collective-permute-start | bytes 1572872 | tf_op jit(solution)/shard_map/ppermute | solution.py:289
